TPU v7x, 256 devices: a whole 4x4x8 slice. The times are simulated.
256 devices in a mesh: rows: 32 (over z, y), cls: 8 (over x, core).
Axes of the slice: x: 4, y: 4, z: 8, core: 2. Of those that a mesh axis runs over, the one named last changes fastest.
Arguments:
- embeddings: bfloat16 [65536, 1024], P('rows'), may hold values from -6 to 6
- residuals: float32 [65536, 1024], P('rows', 'cls'), may hold values from -6 to 6
- projections: bfloat16 [64, 1024, 512], P('rows'), may hold values from -0.1875 to 0.1875
- phases: bfloat16 [64, 512], P('rows'), may hold values from -3.140625 to 3.140625
- old_coef: float32 [2, 512, 1024], P(None, None, 'cls'), may hold values from -6 to 6
- block_order: int32 [2], replicated, may hold values from 0 to 63, as said below
Outputs:
- new_residuals: float32 [65536, 1024], P('rows', 'cls')
- new_coef: float32 [2, 512, 1024], P(None, None, 'cls')
Inputs may be any that keep to these rules, and one draw needn't show every extreme that they name: `block_order`: the 2 entries are distinct block numbers, one of them 64 - 1; block k is held by index k // 2 of rows.
All inputs are finite; a program needn't handle non-finite values.
Results may differ from a plain program's by a relative error of at most 0.0028.
Values may be sent and summed in bfloat16 or wider, within the bound.
No kernel may reach another device: no remote copies, remote signals or barrier semaphores. Data moves between devices by JAX's collectives and lax.ppermute only.
A program may use at most 64 MiB of HBM per device.

v0:
```python
import jax
import jax.numpy as jnp
from jax import lax
from jax.sharding import PartitionSpec as P

STEPS = 2


HIGH = lax.Precision.HIGHEST


def spread(block, axis, holder):
    block = jnp.where(lax.axis_index(axis) == holder, block, jnp.zeros_like(block))
    return lax.psum(block, axis)


def solve_chol(matrix, right):
    lower = jnp.linalg.cholesky(matrix)
    middle = lax.linalg.triangular_solve(lower, right, left_side=True, lower=True)
    return lax.linalg.triangular_solve(lower, middle, left_side=True, lower=True, transpose_a=True)


def split_three(values):
    upper = values.astype(jnp.bfloat16)
    remain = values - upper.astype(jnp.float32)
    middle = remain.astype(jnp.bfloat16)
    lowest = (remain - middle.astype(jnp.float32)).astype(jnp.bfloat16)
    return (upper, middle, lowest)


def feats_times(feats, values, dims):
    total = None
    for part_value in split_three(values):
        term = lax.dot_general(feats, part_value, dims, preferred_element_type=jnp.float32)
        total = term if total is None else total + term
    return total


def shards(embeddings, residuals, projections, phases, old_coef, block_order):
    local_blocks = projections.shape[0]
    width = projections.shape[2]
    total_rows = embeddings.shape[0] * lax.axis_size("rows")
    ridge = 0.25 * total_rows / width
    scale = 1.0 / width**0.5
    current = residuals
    results = []
    inner_rows = (((0,), (0,)), ((), ()))
    outer_rows = (((1,), (0,)), ((), ()))
    for step in range(STEPS):
        block = block_order[step]
        holder = block // local_blocks
        slot = block % local_blocks
        mine_weight = lax.dynamic_index_in_dim(projections, slot, 0, keepdims=False)
        mine_shift = lax.dynamic_index_in_dim(phases, slot, 0, keepdims=False)
        weight, shift = (spread(mine_weight, "rows", holder), spread(mine_shift, "rows", holder))
        angles = jnp.dot(embeddings, weight, preferred_element_type=jnp.float32) + shift.astype(
            jnp.float32
        )
        feats = (jnp.cos(angles) * scale).astype(jnp.bfloat16)
        cross = feats_times(feats, current, inner_rows)
        gram_part = lax.dot_general(feats, feats, inner_rows, preferred_element_type=jnp.float32)
        gram, cross = lax.psum((gram_part, cross), "rows")
        right = cross + jnp.dot(gram, old_coef[step], precision=HIGH)
        system = gram + ridge * jnp.eye(width, dtype=jnp.float32)
        fresh = solve_chol(system, right)
        current = current - feats_times(feats, fresh - old_coef[step], outer_rows)
        results.append(fresh)
    return (current, jnp.stack(results))


def solution(mesh):
    in_specs = (
        P("rows", None),
        P("rows", "cls"),
        P("rows", None, None),
        P("rows", None),
        P(None, None, "cls"),
        P(),
    )
    out_specs = (P("rows", "cls"), P(None, None, "cls"))
    return jax.shard_map(shards, mesh=mesh, in_specs=in_specs, out_specs=out_specs, check_vma=False)
```

profile of v0, /device:TPU:1, one launch (start us, length us, event | category | flops | bytes accessed | tf_op | source)
XLA Modules:
  0.0 835.4 jit_solution(12881480881001109372)
XLA Ops:
  7.2 1.3 fusion.122
  13.8 3.1 select_bitcast_fusion
  17.5 64.7 %all-reduce.3 = (bf16[512]{0:T(512)(128)(2,1)S(1)}, bf16[512]{0:T(512)(128)(2,1)S(1)}) all-reduce(bf16[512]{0:T(512)(128)(2,1)S(1)} %get-tuple-element.38, bf16[512]{0:T(512)(128)(2,1)S(1)} %get-tuple-element.37), channel_id=1, replica_groups=mesh['rows'=32,'cls'=8] {'rows'}, use_global_device_ids=true, to_apply=%region_1.2 | all-reduce | flops 1024 | bytes 4096 | tf_op jit(solution)/shard_map/psum | solution.py:14
  82.2 89.0 %all-reduce.13.cloned.1.call-done = (bf16[1024,512]{1,0:T(8,128)(2,1)}, bf16[1024,512]{1,0:T(8,128)(2,1)}) async-done(((bf16[1024,512]{1,0:T(8,128)(2,1)}, bf16[1024,512]{1,0:T(8,128)(2,1)}), (bf16[1024,512]{1,0:T(8,128)(2,1)}, bf16[1024,512]{1,0:T(8,128)(2,1)})) %all-reduce.13.cloned.1.call-update) | async-done | bytes 2097168 | tf_op jit(solution)/shard_map/psum | solution.py:14
  171.2 17.7 %multiply_convert_fusion.1 = bf16[512,2048]{1,0:T(8,128)(2,1)S(1)} fusion(bf16[1024,512]{1,0:T(8,128)(2,1)} %get-tuple-element.61, bf16[2048,1024]{1,0:T(8,128)(2,1)} %param.11, f32[512]{0:T(512)S(1)} %convert_element_type.76), kind=kOutput, calls=%fused_computation.5 | convolution fusion | flops 2150629376 | bytes 7342080 | tf_op jit(solution)/shard_map/dot_general | solution.py:56
  189.0 2.3 fusion.123
  192.7 1.5 convolution_add_fusion.6
  194.6 17.3 %multiply_convert_fusion = bf16[512,2048]{1,0:T(8,128)(2,1)S(1)} fusion(bf16[1024,512]{1,0:T(8,128)(2,1)S(1)} %copy-done.16, bf16[2048,1024]{1,0:T(8,128)(2,1)} %param.11, f32[512]{0:T(512)S(1)} %convert_element_type.88), kind=kOutput, calls=%fused_computation.4 | convolution fusion | flops 2150629376 | bytes 7342080 | tf_op jit(solution)/shard_map/dot_general | solution.py:56
  212.0 2.3 fusion.124
  214.2 128.4 %all-reduce.11.cloned.1.call-done = (f32[512,512]{0,1:T(8,128)}, f32[512,128]{1,0:T(8,128)}) async-done(((f32[512,512]{0,1:T(8,128)}, f32[512,128]{1,0:T(8,128)}), (f32[512,512]{0,1:T(8,128)}, f32[512,128]{1,0:T(8,128)})) %all-reduce.11.cloned.1.call-update) | async-done | bytes 1310736 | tf_op jit(solution)/shard_map/psum | solution.py:62
  342.7 2.4 select_add_fusion.1
  345.0 2.5 copy.9
  347.6 1.4 fusion.3
  350.0 11.7 %cholesky.286 = f32[128,128]{1,0:T(8,128)S(1)} custom-call(f32[128,128]{1,0:T(8,128)S(1)} %cholesky.426), custom_call_target="Cholesky" | custom-call | tf_op jit(solution)/shard_map/jit(cholesky)/cholesky | solution.py:18
  361.8 1.1 cholesky.312
  362.9 9.8 %custom-call.31 = f32[1,128,128]{1,2,0:T(8,128)S(1)} custom-call(f32[1,128,128]{2,1,0:T(8,128)S(1)} %get-tuple-element.88), custom_call_target="InvertDiagBlocksLowerTriangular" | custom-call | tf_op jit(solution)/shard_map/jit(cholesky)/cholesky | solution.py:18
  372.7 1.9 constant_dynamic-update-slice_fusion.5
  374.6 1.3 convolution_subtract_fusion.1
  375.9 11.9 %cholesky.305 = f32[128,128]{1,0:T(8,128)S(1)} custom-call(f32[128,128]{1,0:T(8,128)S(1)} %cholesky.430), custom_call_target="Cholesky" | custom-call | tf_op jit(solution)/shard_map/jit(cholesky)/cholesky | solution.py:18
  388.4 9.8 %custom-call.32 = f32[1,128,128]{1,2,0:T(8,128)S(1)} custom-call(f32[1,128,128]{2,1,0:T(8,128)S(1)} %get-tuple-element.85), custom_call_target="InvertDiagBlocksLowerTriangular" | custom-call | tf_op jit(solution)/shard_map/jit(cholesky)/cholesky | solution.py:18
  399.1 1.4 convolution_subtract_fusion.3
  400.6 11.7 %cholesky.326 = f32[128,128]{1,0:T(8,128)S(1)} custom-call(f32[128,128]{1,0:T(8,128)S(1)} %cholesky.435), custom_call_target="Cholesky" | custom-call | tf_op jit(solution)/shard_map/jit(cholesky)/cholesky | solution.py:18
  413.6 9.8 %custom-call.33 = f32[1,128,128]{1,2,0:T(8,128)S(1)} custom-call(f32[1,128,128]{2,1,0:T(8,128)S(1)} %get-tuple-element.82), custom_call_target="InvertDiagBlocksLowerTriangular" | custom-call | tf_op jit(solution)/shard_map/jit(cholesky)/cholesky | solution.py:18
  424.2 1.4 convolution_subtract_fusion.17
  425.6 12.1 %cholesky.343 = f32[128,128]{1,0:T(8,128)S(1)} custom-call(f32[128,128]{1,0:T(8,128)S(1)} %convolution_subtract_fusion.17), custom_call_target="Cholesky" | custom-call | tf_op jit(solution)/shard_map/jit(cholesky)/cholesky | solution.py:18
  442.3 2.3 select_select_fusion.1
  444.7 11.2 %while.8 = (s32[]{:T(128)}, f32[512,512]{1,0:T(8,128)}, s32[4,2]{0,1:T(2,128)S(1)}, f32[4,128,128]{2,1,0:T(8,128)S(1)}, s32[]{:T(128)}) while((s32[]{:T(128)}, f32[512,512]{1,0:T(8,128)}, s32[4,2]{0,1:T(2,128)S(1)}, f32[4,128,128]{2,1,0:T(8,128)S(1)}, s32[]{:T(128)}) %tuple.66), condition=%wide.while_cond.1, body=%wide.while_body.1.sunk | while | flops 2 | bytes 131181 | solution.py:20
  445.3 2.2 bitcast_dynamic-update-slice_fusion.4
  448.1 2.2 bitcast_dynamic-update-slice_fusion.4
  450.9 2.2 bitcast_dynamic-update-slice_fusion.4
  453.7 2.1 bitcast_dynamic-update-slice_fusion.4
  456.6 40.1 %custom-call.35 = f32[4,128,128]{1,2,0:T(8,128)S(1)} custom-call(f32[4,128,128]{2,1,0:T(8,128)} %copy-done.14), custom_call_target="InvertDiagBlocksLowerTriangular" | custom-call | tf_op jit(solution)/shard_map/triangular_solve/custom-call.8 | solution.py:20
  496.7 2.9 convolution_add_fusion.9
  500.0 1.2 convolution_subtract_fusion.11
  503.8 1.0 fusion.98
  505.3 1.0 fusion.96
  510.6 1.4 convolution_add_fusion.4
  512.8 148.3 %all-reduce.9.cloned.1.call-done = (f32[512,512]{0,1:T(8,128)}, f32[512,128]{1,0:T(8,128)}) async-done(((f32[512,512]{0,1:T(8,128)}, f32[512,128]{1,0:T(8,128)}), (f32[512,512]{0,1:T(8,128)}, f32[512,128]{1,0:T(8,128)})) %all-reduce.9.cloned.1.call-update) | async-done | bytes 1310736 | tf_op jit(solution)/shard_map/psum | solution.py:62
  661.1 2.3 select_add_fusion
  663.4 2.6 copy.11
  665.9 1.8 fusion.2
  667.7 1.0 copy-done.9
  668.8 11.9 %cholesky.358 = f32[128,128]{1,0:T(8,128)S(1)} custom-call(f32[128,128]{1,0:T(8,128)S(1)} %cholesky.439), custom_call_target="Cholesky" | custom-call | tf_op jit(solution)/shard_map/jit(cholesky)/cholesky | solution.py:18
  680.7 1.1 cholesky.384
  681.8 9.8 %custom-call.36 = f32[1,128,128]{1,2,0:T(8,128)S(1)} custom-call(f32[1,128,128]{2,1,0:T(8,128)S(1)} %get-tuple-element.78), custom_call_target="InvertDiagBlocksLowerTriangular" | custom-call | tf_op jit(solution)/shard_map/jit(cholesky)/cholesky | solution.py:18
  691.6 1.9 constant_dynamic-update-slice_fusion.3
  693.5 1.2 convolution_subtract_fusion
  694.8 11.7 %cholesky.377 = f32[128,128]{1,0:T(8,128)S(1)} custom-call(f32[128,128]{1,0:T(8,128)S(1)} %cholesky.443), custom_call_target="Cholesky" | custom-call | tf_op jit(solution)/shard_map/jit(cholesky)/cholesky | solution.py:18
  708.4 9.8 %custom-call.37 = f32[1,128,128]{1,2,0:T(8,128)S(1)} custom-call(f32[1,128,128]{2,1,0:T(8,128)S(1)} %get-tuple-element.75), custom_call_target="InvertDiagBlocksLowerTriangular" | custom-call | tf_op jit(solution)/shard_map/jit(cholesky)/cholesky | solution.py:18
  719.1 1.4 convolution_subtract_fusion.2
  720.6 11.9 %cholesky.398 = f32[128,128]{1,0:T(8,128)S(1)} custom-call(f32[128,128]{1,0:T(8,128)S(1)} %cholesky.448), custom_call_target="Cholesky" | custom-call | tf_op jit(solution)/shard_map/jit(cholesky)/cholesky | solution.py:18
  733.8 9.8 %custom-call.38 = f32[1,128,128]{1,2,0:T(8,128)S(1)} custom-call(f32[1,128,128]{2,1,0:T(8,128)S(1)} %get-tuple-element.72), custom_call_target="InvertDiagBlocksLowerTriangular" | custom-call | tf_op jit(solution)/shard_map/jit(cholesky)/cholesky | solution.py:18
  744.5 1.4 convolution_subtract_fusion.14
  745.9 11.7 %cholesky.415 = f32[128,128]{1,0:T(8,128)S(1)} custom-call(f32[128,128]{1,0:T(8,128)S(1)} %convolution_subtract_fusion.14), custom_call_target="Cholesky" | custom-call | tf_op jit(solution)/shard_map/jit(cholesky)/cholesky | solution.py:18
  761.4 2.3 select_select_fusion
  763.7 11.2 %while.9 = (s32[]{:T(128)}, f32[512,512]{1,0:T(8,128)}, s32[4,2]{0,1:T(2,128)S(1)}, f32[4,128,128]{2,1,0:T(8,128)S(1)}, s32[]{:T(128)}) while((s32[]{:T(128)}, f32[512,512]{1,0:T(8,128)}, s32[4,2]{0,1:T(2,128)S(1)}, f32[4,128,128]{2,1,0:T(8,128)S(1)}, s32[]{:T(128)}) %tuple.81), condition=%wide.while_cond.1.clone, body=%wide.while_body.1.clone.sunk | while | flops 2 | bytes 131181 | solution.py:20
  764.3 2.2 bitcast_dynamic-update-slice_fusion.5
  767.1 2.2 bitcast_dynamic-update-slice_fusion.5
  770.0 2.2 bitcast_dynamic-update-slice_fusion.5
  772.8 2.1 bitcast_dynamic-update-slice_fusion.5
  775.6 40.4 %custom-call.40 = f32[4,128,128]{1,2,0:T(8,128)S(1)} custom-call(f32[4,128,128]{2,1,0:T(8,128)} %copy-done.13), custom_call_target="InvertDiagBlocksLowerTriangular" | custom-call | tf_op jit(solution)/shard_map/triangular_solve/custom-call.8 | solution.py:20
  816.0 3.2 convolution_add_fusion.8
  819.6 1.1 convolution_subtract_fusion.7
  825.8 1.8 fusion
  (123 shorter events, 36.2 us)
Async XLA Ops:
  7.2 164.1 %all-reduce.13.cloned.1.call-start = ((), (), s32[]{:S(2)}) async-start(), calls=%async_computation.2 | async-start | bytes 4194304 | tf_op jit(solution)/shard_map/psum | solution.py:14
  16.8 0.7 copy-start.15
  16.8 325.8 %all-reduce.11.cloned.1.call-start = ((), (), s32[]{:S(2)}) async-start(), calls=%async_computation.1 | async-start | bytes 2621440 | tf_op jit(solution)/shard_map/psum | solution.py:62
  189.0 3.8 copy-start
  189.0 2.3 copy-start.2
  192.7 1.9 copy-start.16
  194.2 466.8 %all-reduce.9.cloned.1.call-start = ((), (), s32[]{:S(2)}) async-start(), calls=%async_computation | async-start | bytes 2621440 | tf_op jit(solution)/shard_map/psum | solution.py:62
  342.7 4.9 copy-start.4
  349.0 1.0 copy-start.10
  455.8 0.7 copy-start.14
  496.7 6.5 copy-start.11
  496.7 4.8 copy-start.8
  499.7 6.7 copy-start.1
  499.7 6.7 copy-start.5
  507.2 1.2 copy-start.3
  667.7 1.0 copy-start.9
  774.9 0.7 copy-start.13
  816.0 5.0 copy-start.7
  819.6 4.7 copy-start.6
  825.8 1.8 copy-start.12
Sparse Core Ops, SparseCore 0:
  17.0 154.2 all-reduce.12
  194.3 148.2 all-reduce.10
  512.2 148.8 all-reduce.8
where the time goes:
time: 849 us; the launch traced here: 835 us
  waiting for transfers between devices  366 us (43%)
  other arithmetic  260 us (31%)
  matrix products  84 us (10%)
  blocking collectives  64.7 us (8%)
  local copies, waits for them, and re-layouts  35.5 us (4%)
  between operations  25.1 us (3%)
    psum x2, waiting for transfers between devices, shards(): gram, cross = lax.psum((gram_part, cross), 'rows')  277 us
    another operation x29, other arithmetic, solve_chol(): lower = jnp.linalg.cholesky(matrix)  162 us
    psum x1, waiting for transfers between devices, spread(): return lax.psum(block, axis)  89 us
    another operation x5, other arithmetic, solve_chol(): lax.linalg.triangular_solve(lower, middle, left_side=True, lower=True, tr...  85.2 us
    psum x1, blocking collectives, spread(): return lax.psum(block, axis)  64.7 us
    dot_general x2, matrix products, shards(): jnp.dot(embeddings, weight, preferred_element_type=jnp.float32)  35 us
    another operation x27, local copies, waits for them, and re-layouts, solve_chol(): lax.linalg.triangular_solve(lower, middle, left_side=True, lower=True, tr...  22.3 us
  transfers between devices with their start and end apart: 3, of which 3 were waited for; matrix products, arithmetic and copies ran while one was open for 2% of the time, Pallas kernels for 0%

commit v1 on v0

v1 whole, which is shorter than its diff:
```python
import functools
import math

import jax
import jax.numpy as jnp
from jax import lax
from jax.experimental import pallas as pl
from jax.experimental.pallas import tpu as pltpu
from jax.sharding import Mesh
from jax.sharding import PartitionSpec as P

STEPS = 2
BF = jnp.bfloat16
F32 = jnp.float32
ROWS = ("z", "y")
CLS = ("x", "c")

SINE = (
    6.283185160088491,
    -41.34165503116555,
    81.60100405640866,
    -76.54978188256763,
    39.536702776697375,
)
TOLERANCE = 1e-6
MAX_LOOPS = 2000


def cosine(angle, scale):
    turns = angle * (1.0 / (2.0 * math.pi))
    offset = turns - lax.round(turns, lax.RoundingMethod.TO_NEAREST_EVEN)
    q = 0.25 - jnp.abs(offset)
    z = q * q
    total = SINE[-1] * scale
    for coefficient in SINE[-2::-1]:
        total = total * z + coefficient * scale
    return total * q


def split_two(values):
    upper = values.astype(BF)
    return upper, (values - upper.astype(F32)).astype(BF)


def feature_kernel(place, e_ref, w_ref, shift_ref, r_ref, f_ref, out_ref, acc_ref):
    step = pl.program_id(0)
    rows = e_ref.shape[0]
    width = w_ref.shape[2]
    scale = 1.0 / width**0.5
    chunk = 256
    e = e_ref[...]
    for s in range(STEPS):
        for col in range(0, width, chunk):
            angle = jnp.dot(e, w_ref[s, :, col : col + chunk], preferred_element_type=F32)
            angle = angle + shift_ref[s : s + 1, col : col + chunk]
            f_ref[:, s * width + col : s * width + col + chunk] = cosine(angle, scale).astype(BF)
    lane = pl.multiple_of(place[0] * 128, 128)
    upper, lower = split_two(r_ref[...].T)
    left = [upper, lower]
    for s in range(STEPS):
        left.append(f_ref[:, pl.ds(pl.multiple_of(s * width + lane, 128), 128)].T)
    left = jnp.concatenate(left, axis=0)
    part = jnp.dot(left, f_ref[...], preferred_element_type=F32)

    @pl.when(step == 0)
    def _():
        acc_ref[...] = part

    @pl.when(step > 0)
    def _():
        acc_ref[...] += part

    @pl.when(step == pl.num_programs(0) - 1)
    def _():
        half = pl.multiple_of(place[1] * 256, 128)
        for group, (row, first) in enumerate(((256, 0), (384, width), (384, 0))):
            for side in range(2):
                lanes = pl.ds(pl.multiple_of(first + half + side * 128, 128), 128)
                block = acc_ref[row : row + 128, lanes]
                out_ref[side * 16 : side * 16 + 16, group * 8 : group * 8 + 8, :] = block.reshape(16, 8, 128)
        cross = acc_ref[0:128, :] + acc_ref[128:256, :]
        out_ref[:, 24:56, :] = cross.T.reshape(32, 32, 128)


def features(embeddings, weights, shifts, residuals, place):
    total, depth = embeddings.shape
    width = weights.shape[2]
    tile = 512
    return pl.pallas_call(
        feature_kernel,
        grid_spec=pltpu.PrefetchScalarGridSpec(
            num_scalar_prefetch=1,
            grid=(total // tile,),
            in_specs=[
                pl.BlockSpec((tile, depth), lambda i, p: (i, 0)),
                pl.BlockSpec((STEPS, depth, width), lambda i, p: (0, 0, 0)),
                pl.BlockSpec((STEPS, width), lambda i, p: (0, 0)),
                pl.BlockSpec((tile, 128), lambda i, p: (i, 0)),
            ],
            out_specs=[
                pl.BlockSpec((tile, STEPS * width), lambda i, p: (i, 0)),
                pl.BlockSpec((32, 56, 128), lambda i, p: (0, 0, 0)),
            ],
            scratch_shapes=[pltpu.VMEM((512, STEPS * width), F32)],
        ),
        out_shape=[
            jax.ShapeDtypeStruct((total, STEPS * width), BF),
            jax.ShapeDtypeStruct((32, 56, 128), F32),
        ],
        compiler_params=pltpu.CompilerParams(vmem_limit_bytes=40 << 20),
        name="features",
    )(place, embeddings, weights, shifts, residuals)


def times(upper, lower, values):
    high, low = split_two(values)
    both = jnp.dot(upper, jnp.concatenate([high, low], axis=1), preferred_element_type=F32)
    return both[:, :128] + both[:, 128:] + jnp.dot(lower, high, preferred_element_type=F32)


def conjugate_gradients(upper_ref, lower_ref, right, ridge):
    size = jnp.sum(right * right, axis=0, keepdims=True)
    floor = size * (TOLERANCE * TOLERANCE)

    def one(x, r, p, rr):
        ap = times(upper_ref[...], lower_ref[...], p) + ridge * p
        curve = jnp.sum(p * ap, axis=0, keepdims=True)
        alpha = jnp.where(curve > 0.0, rr / curve, 0.0)
        x = x + alpha * p
        r = r - alpha * ap
        new = jnp.sum(r * r, axis=0, keepdims=True)
        beta = jnp.where(rr > 0.0, new / rr, 0.0)
        return x, r, r + beta * p, new

    def body(state):
        count, x, r, p, rr = state
        for _ in range(2):
            x, r, p, rr = one(x, r, p, rr)
        return count + 1, x, r, p, rr

    def open_still(state):
        return jnp.logical_and(state[0] < MAX_LOOPS, jnp.max(state[4] - floor) > 0.0)

    state = (jnp.int32(0), jnp.zeros_like(right), right, right, size)
    return lax.while_loop(open_still, body, state)[1]


def solve_kernel(ridge, place, *refs):
    pieces = refs[:8]
    all_ref, old_ref, f_ref, r_ref, coef_ref, out_ref, upper, lower = refs[8:]
    for shift in range(4):
        for other in range(2):
            ref = pieces[shift * 2 + other]
            px = lax.rem(place[0] + 4 - shift, 4)
            pc = lax.rem(place[1] + other, 2)
            row = pl.multiple_of(px * 128, 128)
            for group in range(3):
                for side in range(2):
                    lanes = pl.ds(pl.multiple_of(pc * 256 + side * 128, 128), 128)
                    block = ref[side * 16 : side * 16 + 16, group * 8 : group * 8 + 8, :].reshape(128, 128)
                    high, low = split_two(block)
                    upper[group, pl.ds(row, 128), lanes] = high
                    lower[group, pl.ds(row, 128), lanes] = low
    cross = all_ref[:, 24:56, :].reshape(1024, 128)
    first = conjugate_gradients(upper.at[0], lower.at[0], cross[:512] - ridge * old_ref[0], ridge)
    coef_ref[0] = old_ref[0] + first
    cross = cross[512:] - times(upper[2], lower[2], first)
    second = conjugate_gradients(upper.at[1], lower.at[1], cross - ridge * old_ref[1], ridge)
    coef_ref[1] = old_ref[1] + second
    high, low = split_two(jnp.concatenate([first, second], axis=0))
    delta = jnp.concatenate([high, low], axis=1)
    tile = 256
    for row in range(0, f_ref.shape[0], tile):
        both = jnp.dot(f_ref[row : row + tile, :], delta, preferred_element_type=F32)
        out_ref[row : row + tile, :] = r_ref[row : row + tile, :] - both[:, :128] - both[:, 128:]


def solve(pieces, everything, old, feats, residuals, place, ridge):
    whole = pl.BlockSpec(memory_space=pltpu.VMEM)
    return pl.pallas_call(
        functools.partial(solve_kernel, ridge),
        in_specs=[pl.BlockSpec(memory_space=pltpu.SMEM)] + [whole] * 12,
        out_specs=[whole, whole],
        out_shape=[
            jax.ShapeDtypeStruct(old.shape, F32),
            jax.ShapeDtypeStruct(residuals.shape, F32),
        ],
        scratch_shapes=[pltpu.VMEM((3, 512, 512), BF), pltpu.VMEM((3, 512, 512), BF)],
        compiler_params=pltpu.CompilerParams(vmem_limit_bytes=48 << 20),
        name="solve",
    )(place, *pieces, everything, old, feats, residuals)


def exchange(values, axes):
    return lax.all_to_all(values, axes, split_axis=0, concat_axis=0, tiled=True)


def gather(values, axes, count):
    return exchange(jnp.broadcast_to(values[None], (count,) + values.shape), axes)


def body(embeddings, residuals, projections, phases, old_coef, block_order):
    local_blocks, depth, width = projections.shape
    nx, nc = lax.axis_size("x"), lax.axis_size("c")
    nrows = lax.axis_size("z") * lax.axis_size("y")
    ix, ic = lax.axis_index("x"), lax.axis_index("c")
    ridge = 0.25 * (embeddings.shape[0] * nrows) / width
    holder = block_order // local_blocks
    slot = block_order % local_blocks
    part = depth // (nx * nc)
    at = (ix * nc + ic) * part
    share = nrows // STEPS

    sent = []
    both = jnp.concatenate([lax.dynamic_slice(phases, (slot[s], 0), (1, width)) for s in range(STEPS)], axis=0)
    both = jnp.pad(both, ((0, 8 - STEPS), (0, 0)))
    for s in range(STEPS):
        mine = lax.dynamic_slice(projections, (slot[s], at, 0), (1, part, width))
        sent.append(mine.reshape(share, part // share, width))
    sent = jnp.concatenate(sent, axis=0)
    sent = jnp.concatenate([sent, jnp.broadcast_to(both[None], (nrows, 8, width))], axis=1)
    got = exchange(sent, ROWS)
    source = holder[lax.axis_index(ROWS) // share]
    piece = lax.dynamic_slice(got, (source, 0, 0), (1, 8, width))[0]
    shifts = jnp.concatenate(
        [lax.dynamic_slice(got, (holder[s], 8 + s, 0), (1, 1, width))[0] for s in range(STEPS)], axis=0
    ).astype(F32)
    mine = gather(piece, ROWS, nrows).reshape(STEPS, part, width)
    chips = gather(mine, "x", nx)
    swap = [(i, (i + 1) % nc) for i in range(nc)]
    other = lax.ppermute(chips, "c", swap)
    even = jnp.where(ic == 0, chips, other)
    odd = jnp.where(ic == 0, other, chips)
    weights = jnp.stack([even, odd], axis=1)
    weights = weights.transpose(2, 0, 1, 3, 4).reshape(STEPS, depth, width)

    place = jnp.stack([ix, ic]).astype(jnp.int32)
    feats, parts = features(embeddings, weights, shifts, residuals, place)

    summed = jnp.sum(exchange(parts, ROWS), axis=0)
    everything = gather(summed, ROWS, nrows)
    grams = everything[:, :24, :]
    pieces = []
    for shift in range(nx):
        moved = grams
        if shift:
            moved = lax.ppermute(grams, "x", [(i, (i + shift) % nx) for i in range(nx)])
        pieces += [moved, lax.ppermute(moved, "c", swap)]
    coef, current = solve(pieces, everything, old_coef, feats, residuals, place, ridge)
    return current, coef


def solution(mesh):
    grid = Mesh(mesh.devices.reshape(8, 4, 4, 2), ROWS + CLS)
    in_specs = (
        P(ROWS, None),
        P(ROWS, CLS),
        P(ROWS, None, None),
        P(ROWS, None),
        P(None, None, CLS),
        P(),
    )
    out_specs = (P(ROWS, CLS), P(None, None, CLS))
    return jax.shard_map(body, mesh=grid, in_specs=in_specs, out_specs=out_specs, check_vma=False)
```

time: 849 us -> 212 us (0.25); the launches traced: 835 us -> 211 us
  waiting for transfers between devices: 366 us -> 20.4 us
  other arithmetic: 260 us -> 2.02 us
  matrix products: 84 us -> 0 us
  Pallas kernels: 0 us -> 49.1 us
  starting transfers between devices: 0.47 us -> 34 us
  local copies, waits for them, and re-layouts: 35.5 us -> 7.47 us
  blocking collectives: 64.7 us -> 87.7 us
  between operations: 25.1 us -> 9.88 us
    psum x3 -> x0, waiting for transfers between devices: 366 us -> none  [the longest x2 277 us: shards(): gram, cross = lax.psum((gram_part, cross), 'rows')]
    another operation x37 -> x1, other arithmetic: 249 us -> 0.14 us  [body(): weights = jnp.stack([even, odd], axis=1)]
    all_to_all x0 -> x4, blocking collectives: none -> 87.7 us  [exchange(): return lax.all_to_all(values, axes, split_axis=0, concat_axis=0, tiled=True)]
    psum x1 -> x0, blocking collectives: 64.7 us -> none  [spread(): return lax.psum(block, axis)]
    dot_general x18 -> x0, matrix products: 57.1 us -> none  [the longest x2 35 us: shards(): jnp.dot(embeddings, weight, preferred_element_type=jnp.float32)]
    pallas_call x0 -> x2, Pallas kernels: none -> 49.1 us  [the longest x1 36.3 us: solve(): pl.pallas_call(functools.partial(solve_kernel, ridge), in_specs=[pl.Block...]
    another operation x40 -> x0, matrix products: 26.9 us -> none  [the longest x12 15.5 us: solve_chol(): lower = jnp.linalg.cholesky(matrix)]
    another operation x35 -> x0, local copies, waits for them, and re-layouts: 24.5 us -> none  [the longest x27 22.3 us: solve_chol(): lax.linalg.triangular_solve(lower, middle, left_side=True, lower=True, tr...]
  transfers between devices with their start and end apart: 3 -> 9, of which waited for: 3 -> 4; matrix products, arithmetic and copies ran while one was open for 2% -> 0% of each run, Pallas kernels for 0% -> 0%
where the time goes in v1:
time: 212 us; the launch traced here: 211 us
  blocking collectives  87.7 us (41%)
  Pallas kernels  49.1 us (23%)
  starting transfers between devices  34 us (16%)
  waiting for transfers between devices  20.4 us (10%)
  between operations  9.88 us (5%)
  local copies, waits for them, and re-layouts  7.47 us (4%)
    all_to_all x4, blocking collectives, exchange(): return lax.all_to_all(values, axes, split_axis=0, concat_axis=0, tiled=True)  87.7 us
    pallas_call x1, Pallas kernels, solve(): pl.pallas_call(functools.partial(solve_kernel, ridge), in_specs=[pl.Block...  36.3 us
    ppermute x4, starting transfers between devices, body(): pieces += [moved, lax.ppermute(moved, 'c', swap)]  14.9 us
    all_to_all x1, waiting for transfers between devices, exchange(): return lax.all_to_all(values, axes, split_axis=0, concat_axis=0, tiled=True)  13.7 us
    pallas_call x1, Pallas kernels, features(): pl.pallas_call(feature_kernel, grid_spec=pltpu.PrefetchScalarGridSpec(num...  12.8 us
    all_to_all x1, starting transfers between devices, exchange(): return lax.all_to_all(values, axes, split_axis=0, concat_axis=0, tiled=True)  12 us
    ppermute x3, waiting for transfers between devices, body(): moved = lax.ppermute(grams, 'x', [(i, (i + shift) % nx) for i in range(nx)])  5.32 us
    ppermute x1, starting transfers between devices, body(): other = lax.ppermute(chips, 'c', swap)  4.89 us
  transfers between devices with their start and end apart: 9, of which 4 were waited for; matrix products, arithmetic and copies ran while one was open for 0% of the time, Pallas kernels for 0%

profile of v1, /device:TPU:1, one launch (start us, length us, event | category | flops | bytes accessed | tf_op | source)
XLA Modules:
  0.0 210.6 jit_solution(5300688004251298294)
XLA Ops:
  0.6 0.7 and_select_fusion
  1.4 0.6 fusion.4
  5.6 0.8 constant_dynamic-slice_fusion.1
  6.4 1.0 dynamic-slice_bitcast_fusion.1
  7.4 0.9 pad_maximum_fusion
  8.3 12.0 %all-to-all-start = ((bf16[32,16,512]{2,1,0:T(8,128)(2,1)}), bf16[32,16,512]{2,1,0:T(8,128)(2,1)S(1)}, u32[]{:S(2)}, u32[]{:S(2)}) async-start(bf16[32,16,512]{2,1,0:T(8,128)(2,1)} %pad_maximum_fusion), calls=%async_computation | async-start | bytes 1048576 | tf_op jit(solution)/shard_map/all_to_all | solution.py:195
  20.3 0.6 fusion.3
  22.8 13.7 %all-to-all-done = bf16[32,16,512]{2,1,0:T(8,128)(2,1)S(1)} async-done(((bf16[32,16,512]{2,1,0:T(8,128)(2,1)}), bf16[32,16,512]{2,1,0:T(8,128)(2,1)S(1)}, u32[]{:S(2)}, u32[]{:S(2)}) %all-to-all-start) | async-done | bytes 524320 | tf_op jit(solution)/shard_map/all_to_all | solution.py:195
  36.6 15.5 %all_to_all.25 = bf16[32,8,512]{2,1,0:T(8,128)(2,1)S(1)} all-to-all(bf16[32,8,512]{2,1,0:T(8,128)(2,1)S(1)} %broadcast_in_dim.28), channel_id=1, replica_groups=mesh['z'=8,'y'=4,'x'=4,'c'=2] {'z','y'}, dimensions={0} | all-to-all | bytes 524288 | tf_op jit(solution)/shard_map/all_to_all | solution.py:195
  52.1 0.1 broadcast_in_dim.30
  52.2 15.0 %all_to_all.26 = bf16[4,2,128,512]{3,2,1,0:T(8,128)(2,1)S(1)} all-to-all(bf16[4,2,128,512]{3,2,1,0:T(8,128)(2,1)S(1)} %broadcast_in_dim.30), channel_id=1, replica_groups=mesh['z'=8,'y'=4,'x'=4,'c'=2] {'x'}, dimensions={0} | all-to-all | bytes 2097152 | tf_op jit(solution)/shard_map/all_to_all | solution.py:195
  67.1 4.9 %collective-permute-start = (bf16[4,2,128,512]{3,2,1,0:T(8,128)(2,1)S(1)}, bf16[4,2,128,512]{3,2,1,0:T(8,128)(2,1)S(1)}, u32[]{:S(2)}, u32[]{:S(2)}) collective-permute-start(bf16[4,2,128,512]{3,2,1,0:T(8,128)(2,1)S(1)} %all_to_all.26), channel_id=1, source_target_pairs={{0,1},{1,0},{2,3},{3,2},{4,5},{5,4},{6,7},{7,6},{8,9},{9,8},{10,11... | collective-permute-start | bytes 3145736 | tf_op jit(solution)/shard_map/ppermute | solution.py:231
  75.6 0.0 collective-permute-done
  75.6 0.1 select_bitcast_fusion.1
  75.8 0.0 copy-start.1
  75.8 0.2 maximum_bitcast_fusion
  76.0 0.0 copy-start
  76.0 0.2 copy.9
  76.2 1.8 copy-done.1
  78.0 0.3 copy-done
  78.3 12.8 %features.1 = (bf16[2048,1024]{1,0:T(8,128)(2,1)S(1)}, f32[32,56,128]{2,1,0:T(8,128)S(1)}) custom-call(s32[2]{0:T(128)S(1)} %get-tuple-element.25.place, bf16[2048,1024]{1,0:T(8,128)(2,1)S(1)} %copy-done.1, bf16[2,1024,512]{2,1,0:T(8,128)(2,1)S(1)} %bitcast.25, f32[2,512]{1,0:T(2,128)S(1)} %maximum_convert_fusion.shift_ref, f32[2048,128]{1,0:T(8,128)S(1)} %copy-done), custom_call_target="tpu_custom_call" | custom-call | tf_op jit(solution)/shard_map/features/pallas_call | solution.py:89
  91.1 0.0 copy-start.2
  91.1 1.9 copy-done.2
  93.0 29.0 %all_to_all.27 = f32[32,56,128]{2,1,0:T(8,128)S(1)} all-to-all(f32[32,56,128]{2,1,0:T(8,128)S(1)} %get-tuple-element.6), channel_id=1, replica_groups=mesh['z'=8,'y'=4,'x'=4,'c'=2] {'z','y'}, dimensions={0} | all-to-all | bytes 1835008 | tf_op jit(solution)/shard_map/all_to_all | solution.py:195
  122.1 0.0 copy-start.3
  122.1 0.1 reduce_sum.9
  122.1 0.1 broadcast_in_dim.31
  122.2 28.2 %all_to_all.28.refs_8_ = f32[32,56,128]{2,1,0:T(8,128)S(1)} all-to-all(f32[32,56,128]{2,1,0:T(8,128)S(1)} %broadcast_in_dim.31), channel_id=1, replica_groups=mesh['z'=8,'y'=4,'x'=4,'c'=2] {'z','y'}, dimensions={0} | all-to-all | bytes 1835008 | tf_op jit(solution)/shard_map/all_to_all | solution.py:195
  150.5 1.0 collective-permute-start.6
  151.4 1.2 collective-permute-start.4
  152.6 0.0 collective-permute-start.2
  152.6 3.8 %collective-permute-start.1 = (f32[32,24,128]{2,1,0:T(8,128)S(1)}, f32[32,24,128]{2,1,0:T(8,128)S(1)}, u32[]{:S(2)}, u32[]{:S(2)}) collective-permute-start(f32[32,24,128]{2,1,0:T(8,128)S(1)} %slice.22.refs_0_), channel_id=1, source_target_pairs={{0,1},{1,0},{2,3},{3,2},{4,5},{5,4},{6,7},{7,6},{8,9},{9,8},{10,11... | collective-permute-start | bytes 1179656 | tf_op jit(solution)/shard_map/ppermute | solution.py:248
  156.4 1.6 collective-permute-done.6.refs_6_
  158.0 7.8 %collective-permute-start.7 = (f32[32,24,128]{2,1,0:T(8,128)S(1)}, f32[32,24,128]{2,1,0:T(8,128)S(1)}, u32[]{:S(2)}, u32[]{:S(2)}) collective-permute-start(f32[32,24,128]{2,1,0:T(8,128)S(1)} %collective-permute-done.6.refs_6_), channel_id=1, source_target_pairs={{0,1},{1,0},{2,3},{3,2},{4,5},{5,4},{6,7},{7,6},{8,9},{9,8},{10,11... | collective-permute-start | bytes 1179656 | tf_op jit(solution)/shard_map/ppermute | solution.py:248
  165.8 0.0 collective-permute-done.4.refs_4_
  165.8 2.7 %collective-permute-start.5 = (f32[32,24,128]{2,1,0:T(8,128)S(1)}, f32[32,24,128]{2,1,0:T(8,128)S(1)}, u32[]{:S(2)}, u32[]{:S(2)}) collective-permute-start(f32[32,24,128]{2,1,0:T(8,128)S(1)} %collective-permute-done.4.refs_4_), channel_id=1, source_target_pairs={{0,1},{1,0},{2,3},{3,2},{4,5},{5,4},{6,7},{7,6},{8,9},{9,8},{10,11... | collective-permute-start | bytes 1179656 | tf_op jit(solution)/shard_map/ppermute | solution.py:248
  168.4 3.7 %collective-permute-done.2.refs_2_ = f32[32,24,128]{2,1,0:T(8,128)S(1)} collective-permute-done((f32[32,24,128]{2,1,0:T(8,128)S(1)}, f32[32,24,128]{2,1,0:T(8,128)S(1)}, u32[]{:S(2)}, u32[]{:S(2)}) %collective-permute-start.2) | collective-permute-done | bytes 393248 | tf_op jit(solution)/shard_map/ppermute | solution.py:247
  172.2 0.7 collective-permute-start.3
  172.9 0.0 collective-permute-done.1.refs_1_
  172.9 0.0 collective-permute-done.7.refs_7_
  172.9 0.0 collective-permute-done.5.refs_5_
  172.9 1.3 collective-permute-done.3.refs_3_
  174.2 0.0 copy-done.3
  174.3 36.3 %solve.1 = (f32[2,512,128]{2,1,0:T(8,128)}, f32[2048,128]{1,0:T(8,128)}) custom-call(s32[2]{0:T(128)S(1)} %get-tuple-element.25.place, f32[32,24,128]{2,1,0:T(8,128)S(1)} %slice.22.refs_0_, f32[32,24,128]{2,1,0:T(8,128)S(1)} %collective-permute-done.1.refs_1_, f32[32,24,128]{2,1,0:T(8,128)S(1)} %collective-permute-done.2.refs_2_, ...), custom_call_target="tpu_custom_call" | custom-call | tf_op jit(solution)/shard_map/solve/pallas_call | solution.py:180
  (7 shorter events, 0.1 us)
Async XLA Ops:
  8.3 28.3 %all-to-all-start = ((bf16[32,16,512]{2,1,0:T(8,128)(2,1)}), bf16[32,16,512]{2,1,0:T(8,128)(2,1)S(1)}, u32[]{:S(2)}, u32[]{:S(2)}) async-start(bf16[32,16,512]{2,1,0:T(8,128)(2,1)} %pad_maximum_fusion), calls=%async_computation | async-start | bytes 1048576 | tf_op jit(solution)/shard_map/all_to_all | solution.py:195
  67.1 8.5 %collective-permute-start = (bf16[4,2,128,512]{3,2,1,0:T(8,128)(2,1)S(1)}, bf16[4,2,128,512]{3,2,1,0:T(8,128)(2,1)S(1)}, u32[]{:S(2)}, u32[]{:S(2)}) collective-permute-start(bf16[4,2,128,512]{3,2,1,0:T(8,128)(2,1)S(1)} %all_to_all.26), channel_id=1, source_target_pairs={{0,1},{1,0},{2,3},{3,2},{4,5},{5,4},{6,7},{7,6},{8,9},{9,8},{10,11... | collective-permute-start | bytes 3145736 | tf_op jit(solution)/shard_map/ppermute | solution.py:231
  75.8 2.2 %copy-start.1 = (bf16[2048,1024]{1,0:T(8,128)(2,1)S(1)}, bf16[2048,1024]{1,0:T(8,128)(2,1)}, u32[]{:S(2)}) copy-start(bf16[2048,1024]{1,0:T(8,128)(2,1)} %e_ref.1) | copy-start | bytes 12582916
  76.0 2.3 %copy-start = (f32[2048,128]{1,0:T(8,128)S(1)}, f32[2048,128]{1,0:T(8,128)}, u32[]{:S(2)}) copy-start(f32[2048,128]{1,0:T(8,128)} %refs_11_.1) | copy-start | bytes 3145732
  91.1 1.9 copy-start.2
  122.1 52.2 %copy-start.3 = (f32[2,512,128]{2,1,0:T(8,128)S(1)}, f32[2,512,128]{2,1,0:T(8,128)}, u32[]{:S(2)}) copy-start(f32[2,512,128]{2,1,0:T(8,128)} %refs_9_.1) | copy-start | bytes 1572868
  150.5 7.5 %collective-permute-start.6 = (f32[32,24,128]{2,1,0:T(8,128)S(1)}, f32[32,24,128]{2,1,0:T(8,128)S(1)}, u32[]{:S(2)}, u32[]{:S(2)}) collective-permute-start(f32[32,24,128]{2,1,0:T(8,128)S(1)} %slice.22.refs_0_), channel_id=1, source_target_pairs={{0,6},{2,0},{4,2},{6,4},{1,7},{3,1},{5,3},{7,5},{8,14},{10,8},{12,... | collective-permute-start | bytes 1179656 | tf_op jit(solution)/shard_map/ppermute | solution.py:247
  151.4 14.3 %collective-permute-start.4 = (f32[32,24,128]{2,1,0:T(8,128)S(1)}, f32[32,24,128]{2,1,0:T(8,128)S(1)}, u32[]{:S(2)}, u32[]{:S(2)}) collective-permute-start(f32[32,24,128]{2,1,0:T(8,128)S(1)} %slice.22.refs_0_), channel_id=1, source_target_pairs={{0,4},{2,6},{4,0},{6,2},{1,5},{3,7},{5,1},{7,3},{8,12},{10,14},{12... | collective-permute-start | bytes 1179656 | tf_op jit(solution)/shard_map/ppermute | solution.py:247
  152.6 19.5 %collective-permute-start.2 = (f32[32,24,128]{2,1,0:T(8,128)S(1)}, f32[32,24,128]{2,1,0:T(8,128)S(1)}, u32[]{:S(2)}, u32[]{:S(2)}) collective-permute-start(f32[32,24,128]{2,1,0:T(8,128)S(1)} %slice.22.refs_0_), channel_id=1, source_target_pairs={{0,2},{2,4},{4,6},{6,0},{1,3},{3,5},{5,7},{7,1},{8,10},{10,12},{12... | collective-permute-start | bytes 1179656 | tf_op jit(solution)/shard_map/ppermute | solution.py:247
  152.6 20.3 %collective-permute-start.1 = (f32[32,24,128]{2,1,0:T(8,128)S(1)}, f32[32,24,128]{2,1,0:T(8,128)S(1)}, u32[]{:S(2)}, u32[]{:S(2)}) collective-permute-start(f32[32,24,128]{2,1,0:T(8,128)S(1)} %slice.22.refs_0_), channel_id=1, source_target_pairs={{0,1},{1,0},{2,3},{3,2},{4,5},{5,4},{6,7},{7,6},{8,9},{9,8},{10,11... | collective-permute-start | bytes 1179656 | tf_op jit(solution)/shard_map/ppermute | solution.py:248
  158.0 14.9 %collective-permute-start.7 = (f32[32,24,128]{2,1,0:T(8,128)S(1)}, f32[32,24,128]{2,1,0:T(8,128)S(1)}, u32[]{:S(2)}, u32[]{:S(2)}) collective-permute-start(f32[32,24,128]{2,1,0:T(8,128)S(1)} %collective-permute-done.6.refs_6_), channel_id=1, source_target_pairs={{0,1},{1,0},{2,3},{3,2},{4,5},{5,4},{6,7},{7,6},{8,9},{9,8},{10,11... | collective-permute-start | bytes 1179656 | tf_op jit(solution)/shard_map/ppermute | solution.py:248
  165.8 7.2 %collective-permute-start.5 = (f32[32,24,128]{2,1,0:T(8,128)S(1)}, f32[32,24,128]{2,1,0:T(8,128)S(1)}, u32[]{:S(2)}, u32[]{:S(2)}) collective-permute-start(f32[32,24,128]{2,1,0:T(8,128)S(1)} %collective-permute-done.4.refs_4_), channel_id=1, source_target_pairs={{0,1},{1,0},{2,3},{3,2},{4,5},{5,4},{6,7},{7,6},{8,9},{9,8},{10,11... | collective-permute-start | bytes 1179656 | tf_op jit(solution)/shard_map/ppermute | solution.py:248
  172.2 2.1 collective-permute-start.3

commit v2 on v1

v2 whole, which is shorter than its diff:
```python
import functools
import math

import jax
import jax.numpy as jnp
from jax import lax
from jax.experimental import pallas as pl
from jax.experimental.pallas import tpu as pltpu
from jax.sharding import Mesh
from jax.sharding import PartitionSpec as P

STEPS = 2
BF = jnp.bfloat16
F32 = jnp.float32
ROWS = ("z", "y")
CLS = ("x", "c")

SINE = (
    6.283185160088491,
    -41.34165503116555,
    81.60100405640866,
    -76.54978188256763,
    39.536702776697375,
)
TOLERANCE = 1e-6
MAX_LOOPS = 2000


def cosine(angle, scale):
    turns = angle * (1.0 / (2.0 * math.pi))
    offset = turns - lax.round(turns, lax.RoundingMethod.TO_NEAREST_EVEN)
    q = 0.25 - jnp.abs(offset)
    z = q * q
    total = SINE[-1] * scale
    for coefficient in SINE[-2::-1]:
        total = total * z + coefficient * scale
    return total * q


def split_two(values):
    upper = values.astype(BF)
    return upper, (values - upper.astype(F32)).astype(BF)


def offsets(shift, other):
    return lax.rem(lax.axis_index("x") + 4 - shift, 4), lax.rem(lax.axis_index("c") + other, 2)


def payload_kernel(local_blocks, order, proj_ref, phase_ref, out_ref):
    part = 128
    width = proj_ref.shape[2]
    share = out_ref.shape[0] // STEPS
    at = pl.multiple_of((lax.axis_index("x") * 2 + lax.axis_index("c")) * part, part)
    for s in range(STEPS):
        slot = lax.rem(order[s], local_blocks)
        mine = proj_ref[pl.ds(slot, 1), pl.ds(at, part), :]
        out_ref[s * share : (s + 1) * share, :, :width] = mine.reshape(share, part // share, width)
    bands = []
    for s in range(STEPS):
        slot = lax.rem(order[s], local_blocks)
        shift = phase_ref[0:1, :].astype(F32)
        for k in range(1, phase_ref.shape[0]):
            shift = jnp.where(slot == k, phase_ref[k : k + 1, :].astype(F32), shift)
        bands += [shift[:, q * 128 : (q + 1) * 128] for q in range(width // 128)]
    band = jnp.concatenate(bands, axis=0).astype(BF)
    out_ref[:, :, width:] = jnp.broadcast_to(band[None], (out_ref.shape[0],) + band.shape)


def payload(order, projections, phases, nrows):
    local_blocks, depth, width = projections.shape
    whole = pl.BlockSpec(memory_space=pltpu.VMEM)
    return pl.pallas_call(
        functools.partial(payload_kernel, local_blocks),
        in_specs=[pl.BlockSpec(memory_space=pltpu.SMEM), whole, whole],
        out_specs=whole,
        out_shape=jax.ShapeDtypeStruct((nrows, 8, width + 128), BF),
        name="payload",
    )(order, projections, phases)


def pick_kernel(local_blocks, order, got_ref, piece_ref, shift_ref):
    nrows, _, width = piece_ref.shape
    row = lax.axis_index("z") * 4 + lax.axis_index("y")
    source = jnp.where(row < nrows // STEPS, order[0], order[1]) // local_blocks
    piece = got_ref[pl.ds(source, 1), :, :width]
    piece_ref[...] = jnp.broadcast_to(piece, piece_ref.shape)
    for s in range(STEPS):
        band = got_ref[pl.ds(order[s] // local_blocks, 1), :, width:][0].astype(F32)
        for q in range(width // 128):
            row = s * (width // 128) + q
            shift_ref[s : s + 1, q * 128 : (q + 1) * 128] = band[row : row + 1, :]


def pick(order, got, local_blocks):
    nrows, eight, wide = got.shape
    width = wide - 128
    whole = pl.BlockSpec(memory_space=pltpu.VMEM)
    return pl.pallas_call(
        functools.partial(pick_kernel, local_blocks),
        in_specs=[pl.BlockSpec(memory_space=pltpu.SMEM), whole],
        out_specs=[whole, whole],
        out_shape=[
            jax.ShapeDtypeStruct((nrows, eight, width), BF),
            jax.ShapeDtypeStruct((STEPS, width), F32),
        ],
        name="pick",
    )(order, got)


def feature_kernel(*refs):
    pieces = refs[:8]
    e_ref, shift_ref, r_ref, f_ref, out_ref, w_ref, acc_ref = refs[8:]
    step = pl.program_id(0)
    width = w_ref.shape[2]
    scale = 1.0 / width**0.5
    chunk = 256

    @pl.when(step == 0)
    def _():
        for shift in range(4):
            for other in range(2):
                px, pc = offsets(shift, other)
                at = pl.multiple_of(px * 256 + pc * 128, 128)
                for s in range(STEPS):
                    part = pieces[shift * 2 + other][s * 16 : s * 16 + 16, :, :]
                    w_ref[s, pl.ds(at, 128), :] = part.reshape(128, width)

    e = e_ref[...]
    for s in range(STEPS):
        for col in range(0, width, chunk):
            angle = jnp.dot(e, w_ref[s, :, col : col + chunk], preferred_element_type=F32)
            angle = angle + shift_ref[s : s + 1, col : col + chunk]
            f_ref[:, s * width + col : s * width + col + chunk] = cosine(angle, scale).astype(BF)
    lane = lax.axis_index("x") * 128
    upper, lower = split_two(r_ref[...].T)
    left = [upper, lower]
    for s in range(STEPS):
        left.append(f_ref[:, pl.ds(pl.multiple_of(s * width + lane, 128), 128)].T)
    left = jnp.concatenate(left, axis=0)
    part = jnp.dot(left, f_ref[...], preferred_element_type=F32)

    @pl.when(step == 0)
    def _():
        acc_ref[...] = part

    @pl.when(step > 0)
    def _():
        acc_ref[...] += part

    @pl.when(step == pl.num_programs(0) - 1)
    def _():
        half = lax.axis_index("c") * 256
        for group, (row, first) in enumerate(((256, 0), (384, width), (384, 0))):
            for side in range(2):
                lanes = pl.ds(pl.multiple_of(first + half + side * 128, 128), 128)
                block = acc_ref[row : row + 128, lanes]
                out_ref[side * 16 : side * 16 + 16, group * 8 : group * 8 + 8, :] = block.reshape(16, 8, 128)
        cross = acc_ref[0:128, :] + acc_ref[128:256, :]
        out_ref[:, 24:56, :] = cross.T.reshape(32, 32, 128)


def features(pieces, embeddings, shifts, residuals):
    total, depth = embeddings.shape
    width = shifts.shape[1]
    tile = 512
    whole = pl.BlockSpec(memory_space=pltpu.VMEM)
    return pl.pallas_call(
        feature_kernel,
        grid=(total // tile,),
        in_specs=[whole] * 8
        + [
            pl.BlockSpec((tile, depth), lambda i: (i, 0)),
            whole,
            pl.BlockSpec((tile, 128), lambda i: (i, 0)),
        ],
        out_specs=[pl.BlockSpec((tile, STEPS * width), lambda i: (i, 0)), whole],
        out_shape=[
            jax.ShapeDtypeStruct((total, STEPS * width), BF),
            jax.ShapeDtypeStruct((32, 56, 128), F32),
        ],
        scratch_shapes=[pltpu.VMEM((STEPS, depth, width), BF), pltpu.VMEM((512, STEPS * width), F32)],
        compiler_params=pltpu.CompilerParams(vmem_limit_bytes=52 << 20),
        name="features",
    )(*pieces, embeddings, shifts, residuals)


def times(upper, lower, values):
    high, low = split_two(values)
    both = jnp.dot(upper, jnp.concatenate([high, low], axis=1), preferred_element_type=F32)
    return both[:, :128] + both[:, 128:] + jnp.dot(lower, high, preferred_element_type=F32)


def conjugate_gradients(upper_ref, lower_ref, right, ridge):
    size = jnp.sum(right * right, axis=0, keepdims=True)
    floor = size * (TOLERANCE * TOLERANCE)

    def one(x, r, p, rr):
        ap = times(upper_ref[...], lower_ref[...], p) + ridge * p
        curve = jnp.sum(p * ap, axis=0, keepdims=True)
        alpha = jnp.where(curve > 0.0, rr / curve, 0.0)
        x = x + alpha * p
        r = r - alpha * ap
        new = jnp.sum(r * r, axis=0, keepdims=True)
        beta = jnp.where(rr > 0.0, new / rr, 0.0)
        return x, r, r + beta * p, new

    def body(state):
        count, x, r, p, rr = state
        for _ in range(2):
            x, r, p, rr = one(x, r, p, rr)
        return count + 1, x, r, p, rr

    def open_still(state):
        return jnp.logical_and(state[0] < MAX_LOOPS, jnp.max(state[4] - floor) > 0.0)

    state = (jnp.int32(0), jnp.zeros_like(right), right, right, size)
    return lax.while_loop(open_still, body, state)[1]


def solve_kernel(ridge, *refs):
    pieces = refs[:8]
    cross_ref, old_ref, f_hbm, r_hbm, coef_ref, out_ref, upper, lower, f_ref, r_ref, sems = refs[8:]
    loads = [
        pltpu.make_async_copy(f_hbm, f_ref, sems.at[0]),
        pltpu.make_async_copy(r_hbm, r_ref, sems.at[1]),
    ]
    for load in loads:
        load.start()
    for shift in range(4):
        for other in range(2):
            ref = pieces[shift * 2 + other]
            px, pc = offsets(shift, other)
            row = pl.multiple_of(px * 128, 128)
            for group in range(3):
                for side in range(2):
                    lanes = pl.ds(pl.multiple_of(pc * 256 + side * 128, 128), 128)
                    block = ref[side * 16 : side * 16 + 16, group * 8 : group * 8 + 8, :].reshape(128, 128)
                    high, low = split_two(block)
                    upper[group, pl.ds(row, 128), lanes] = high
                    lower[group, pl.ds(row, 128), lanes] = low
    cross = cross_ref[...].reshape(1024, 128)
    first = conjugate_gradients(upper.at[0], lower.at[0], cross[:512] - ridge * old_ref[0], ridge)
    coef_ref[0] = old_ref[0] + first
    cross = cross[512:] - times(upper[2], lower[2], first)
    second = conjugate_gradients(upper.at[1], lower.at[1], cross - ridge * old_ref[1], ridge)
    coef_ref[1] = old_ref[1] + second
    high, low = split_two(jnp.concatenate([first, second], axis=0))
    delta = jnp.concatenate([high, low], axis=1)
    tile = 256
    for load in loads:
        load.wait()
    for row in range(0, f_ref.shape[0], tile):
        both = jnp.dot(f_ref[row : row + tile, :], delta, preferred_element_type=F32)
        out_ref[row : row + tile, :] = r_ref[row : row + tile, :] - both[:, :128] - both[:, 128:]


def solve(pieces, cross, old, feats, residuals, ridge):
    def full(array):
        return pl.BlockSpec(array.shape, lambda: (0,) * array.ndim)

    return pl.pallas_call(
        functools.partial(solve_kernel, ridge),
        in_specs=[full(piece) for piece in pieces]
        + [full(cross), full(old), pl.BlockSpec(memory_space=pl.ANY), pl.BlockSpec(memory_space=pl.ANY)],
        out_specs=[full(old), full(residuals)],
        out_shape=[
            jax.ShapeDtypeStruct(old.shape, F32),
            jax.ShapeDtypeStruct(residuals.shape, F32),
        ],
        scratch_shapes=[
            pltpu.VMEM((3, 512, 512), BF),
            pltpu.VMEM((3, 512, 512), BF),
            pltpu.VMEM(feats.shape, BF),
            pltpu.VMEM(residuals.shape, F32),
            pltpu.SemaphoreType.DMA((2,)),
        ],
        compiler_params=pltpu.CompilerParams(vmem_limit_bytes=36 << 20),
        name="solve",
    )(*pieces, cross, old, feats, residuals)


def exchange(values, axes):
    return lax.all_to_all(values, axes, split_axis=0, concat_axis=0, tiled=True)


def gather(values, axes, count):
    return exchange(jnp.broadcast_to(values[None], (count,) + values.shape), axes)


def spread(values):
    nx, nc = lax.axis_size("x"), lax.axis_size("c")
    moved = [values]
    for shift in range(1, nx):
        moved.append(lax.ppermute(values, "x", [(i, (i + shift) % nx) for i in range(nx)]))
    pieces = []
    for value in moved:
        pieces += [value, lax.ppermute(value, "c", [(i, (i + 1) % nc) for i in range(nc)])]
    return pieces


def body(embeddings, residuals, projections, phases, old_coef, block_order):
    local_blocks, depth, width = projections.shape
    nrows = lax.axis_size("z") * lax.axis_size("y")
    ridge = 0.25 * (embeddings.shape[0] * nrows) / width

    got = exchange(payload(block_order, projections, phases, nrows), ROWS)
    copies, shifts = pick(block_order, got, local_blocks)
    weights = spread(exchange(copies, ROWS))
    feats, parts = features(weights, embeddings, shifts, residuals)

    summed = jnp.sum(exchange(parts, ROWS), axis=0)
    grams = gather(summed[:24], ROWS, nrows)
    cross, grams = lax.optimization_barrier((summed[24:], grams))
    pieces = spread(grams)
    cross = gather(cross, ROWS, nrows)
    coef, current = solve(pieces, cross, old_coef, feats, residuals, ridge)
    return current, coef


def solution(mesh):
    grid = Mesh(mesh.devices.reshape(8, 4, 4, 2), ROWS + CLS)
    in_specs = (
        P(ROWS, None),
        P(ROWS, CLS),
        P(ROWS, None, None),
        P(ROWS, None),
        P(None, None, CLS),
        P(),
    )
    out_specs = (P(ROWS, CLS), P(None, None, CLS))
    return jax.shard_map(body, mesh=grid, in_specs=in_specs, out_specs=out_specs, check_vma=False)
```

time: 212 us -> 203 us (0.958)
  blocking collectives: 87.7 us -> 69.4 us
  between operations: 9.88 us -> 0.89 us
  starting transfers between devices: 34 us -> 40.8 us
  local copies, waits for them, and re-layouts: 7.47 us -> 13.3 us
  waiting for transfers between devices: 20.4 us -> 25 us
  Pallas kernels: 49.1 us -> 52.1 us
    all_to_all x4 -> x3, blocking collectives: 87.7 us -> 69.4 us  [exchange(): return lax.all_to_all(values, axes, split_axis=0, concat_axis=0, tiled=True)]
    unnamed x8 -> x30, local copies, waits for them, and re-layouts: 4.08 us -> 11.7 us
    ppermute x8 -> x14, starting transfers between devices: 22 us -> 29.4 us  [the longest x8 24.2 us: spread(): lax.ppermute(value, 'c', [(i, (i + 1) % nc) for i in range(nc)])]
    ppermute x8 -> x14, waiting for transfers between devices: 6.67 us -> 12.1 us  [the longest x6 10.9 us: spread(): lax.ppermute(values, 'x', [(i, (i + shift) % nx) for i in range(nx)])]
    pallas_call x2 -> x4, Pallas kernels: 49.1 us -> 52.1 us  [the longest x1 32.9 us: solve(): pl.pallas_call(functools.partial(solve_kernel, ridge), in_specs=[full(pie...]
    all_to_all x1 -> x2, waiting for transfers between devices: 13.7 us -> 12.9 us  [exchange(): return lax.all_to_all(values, axes, split_axis=0, concat_axis=0, tiled=True)]
    all_to_all x1 -> x2, starting transfers between devices: 12 us -> 11.5 us  [exchange(): return lax.all_to_all(values, axes, split_axis=0, concat_axis=0, tiled=True)]
  transfers between devices with their start and end apart: 9 -> 16, of which waited for: 4 -> 6; matrix products, arithmetic and copies ran while one was open for 0% -> 0% of each run, Pallas kernels for 0% -> 0%
where the time goes in v2:
time: 203 us; the launch traced here: 202 us
  blocking collectives  69.4 us (34%)
  Pallas kernels  52.1 us (26%)
  starting transfers between devices  40.8 us (20%)
  waiting for transfers between devices  25 us (12%)
  local copies, waits for them, and re-layouts  13.3 us (7%)
    all_to_all x3, blocking collectives, exchange(): return lax.all_to_all(values, axes, split_axis=0, concat_axis=0, tiled=True)  69.4 us
    pallas_call x1, Pallas kernels, solve(): pl.pallas_call(functools.partial(solve_kernel, ridge), in_specs=[full(pie...  32.9 us
    ppermute x8, starting transfers between devices, spread(): lax.ppermute(value, 'c', [(i, (i + 1) % nc) for i in range(nc)])  24.2 us
    pallas_call x1, Pallas kernels, features(): pl.pallas_call(feature_kernel, grid=(total // tile,), in_specs=[whole] *...  15.1 us
    all_to_all x2, waiting for transfers between devices, exchange(): return lax.all_to_all(values, axes, split_axis=0, concat_axis=0, tiled=True)  12.9 us
    unnamed x30, local copies, waits for them, and re-layouts  11.7 us
    all_to_all x2, starting transfers between devices, exchange(): return lax.all_to_all(values, axes, split_axis=0, concat_axis=0, tiled=True)  11.5 us
    ppermute x6, waiting for transfers between devices, spread(): lax.ppermute(values, 'x', [(i, (i + shift) % nx) for i in range(nx)])  10.9 us
  transfers between devices with their start and end apart: 16, of which 6 were waited for; matrix products, arithmetic and copies ran while one was open for 0% of the time, Pallas kernels for 0%

profile of v2, /device:TPU:1, one launch (start us, length us, event | category | flops | bytes accessed | tf_op | source)
XLA Modules:
  0.0 201.6 jit_solution(9103831657465871089)
XLA Ops:
  0.6 2.4 %payload.1 = bf16[32,8,640]{2,1,0:T(8,128)(2,1)} custom-call(s32[2]{0:T(128)} %order.3, bf16[2,1024,512]{2,1,0:T(8,128)(2,1)} %proj_ref.1, bf16[2,512]{1,0:T(2,128)(2,1)} %phase_ref.1), custom_call_target="tpu_custom_call" | custom-call | tf_op jit(solution)/shard_map/payload/pallas_call | solution.py:72
  3.0 24.8 %all_to_all.25.got_ref = bf16[32,8,640]{2,1,0:T(8,128)(2,1)} all-to-all(bf16[32,8,640]{2,1,0:T(8,128)(2,1)} %payload.1), channel_id=1, replica_groups=mesh['z'=8,'y'=4,'x'=4,'c'=2] {'z','y'}, dimensions={0} | all-to-all | bytes 655360 | tf_op jit(solution)/shard_map/all_to_all | solution.py:283
  27.8 1.7 pick.1
  29.6 15.3 %all_to_all.26.refs_0_ = bf16[32,8,512]{2,1,0:T(8,128)(2,1)S(1)} all-to-all(bf16[32,8,512]{2,1,0:T(8,128)(2,1)} %get-tuple-element.10), channel_id=1, replica_groups=mesh['z'=8,'y'=4,'x'=4,'c'=2] {'z','y'}, dimensions={0} | all-to-all | bytes 524288 | tf_op jit(solution)/shard_map/all_to_all | solution.py:283
  44.8 2.5 %collective-permute-start.5 = (bf16[32,8,512]{2,1,0:T(8,128)(2,1)S(1)}, bf16[32,8,512]{2,1,0:T(8,128)(2,1)S(1)}, u32[]{:S(2)}, u32[]{:S(2)}) collective-permute-start(bf16[32,8,512]{2,1,0:T(8,128)(2,1)S(1)} %all_to_all.26.refs_0_), channel_id=1, source_target_pairs={{0,6},{2,0},{4,2},{6,4},{1,7},{3,1},{5,3},{7,5},{8,14},{10,8},{12,... | collective-permute-start | bytes 786440 | tf_op jit(solution)/shard_map/ppermute | solution.py:294
  47.3 0.5 collective-permute-start.3
  47.8 0.6 collective-permute-start.1
  48.4 4.3 %collective-permute-start = (bf16[32,8,512]{2,1,0:T(8,128)(2,1)S(1)}, bf16[32,8,512]{2,1,0:T(8,128)(2,1)S(1)}, u32[]{:S(2)}, u32[]{:S(2)}) collective-permute-start(bf16[32,8,512]{2,1,0:T(8,128)(2,1)S(1)} %all_to_all.26.refs_0_), channel_id=1, source_target_pairs={{0,1},{1,0},{2,3},{3,2},{4,5},{5,4},{6,7},{7,6},{8,9},{9,8},{10,11... | collective-permute-start | bytes 786440 | tf_op jit(solution)/shard_map/ppermute | solution.py:297
  52.8 0.9 collective-permute-done.5.refs_6_
  53.7 5.8 %collective-permute-start.6 = (bf16[32,8,512]{2,1,0:T(8,128)(2,1)S(1)}, bf16[32,8,512]{2,1,0:T(8,128)(2,1)S(1)}, u32[]{:S(2)}, u32[]{:S(2)}) collective-permute-start(bf16[32,8,512]{2,1,0:T(8,128)(2,1)S(1)} %collective-permute-done.5.refs_6_), channel_id=1, source_target_pairs={{0,1},{1,0},{2,3},{3,2},{4,5},{5,4},{6,7},{7,6},{8,9},{9,8},{10,11... | collective-permute-start | bytes 786440 | tf_op jit(solution)/shard_map/ppermute | solution.py:297
  59.5 0.0 collective-permute-done.3.refs_4_
  59.5 1.0 collective-permute-start.4
  60.5 0.6 collective-permute-done.1.refs_2_
  61.1 2.1 %collective-permute-start.2 = (bf16[32,8,512]{2,1,0:T(8,128)(2,1)S(1)}, bf16[32,8,512]{2,1,0:T(8,128)(2,1)S(1)}, u32[]{:S(2)}, u32[]{:S(2)}) collective-permute-start(bf16[32,8,512]{2,1,0:T(8,128)(2,1)S(1)} %collective-permute-done.1.refs_2_), channel_id=1, source_target_pairs={{0,1},{1,0},{2,3},{3,2},{4,5},{5,4},{6,7},{7,6},{8,9},{9,8},{10,11... | collective-permute-start | bytes 786440 | tf_op jit(solution)/shard_map/ppermute | solution.py:297
  63.2 0.0 collective-permute-done.refs_1_
  63.2 0.0 collective-permute-done.6.refs_7_
  63.2 0.0 copy-start.14
  63.2 0.0 collective-permute-done.4.refs_5_
  63.2 1.1 collective-permute-done.2.refs_3_
  64.3 0.0 copy-done.14
  64.3 0.0 copy-start.13
  64.3 0.7 copy-done.13
  65.0 15.1 %features.1 = (bf16[2048,1024]{1,0:T(8,128)(2,1)}, f32[32,56,128]{2,1,0:T(8,128)}) custom-call(bf16[32,8,512]{2,1,0:T(8,128)(2,1)S(1)} %all_to_all.26.refs_0_, bf16[32,8,512]{2,1,0:T(8,128)(2,1)S(1)} %collective-permute-done.refs_1_, bf16[32,8,512]{2,1,0:T(8,128)(2,1)S(1)} %collective-permute-done.1.refs_2_, ...), custom_call_target="tpu_custom_call" | custom-call | tf_op jit(solution)/shard_map/features/pallas_call | solution.py:167
  80.1 0.0 copy-start
  80.1 0.0 copy-start.2
  80.1 29.3 %all_to_all.27 = f32[32,56,128]{2,1,0:T(8,128)S(1)} all-to-all(f32[32,56,128]{2,1,0:T(8,128)} %get-tuple-element.12), channel_id=1, replica_groups=mesh['z'=8,'y'=4,'x'=4,'c'=2] {'z','y'}, dimensions={0} | all-to-all | bytes 1835008 | tf_op jit(solution)/shard_map/all_to_all | solution.py:283
  109.4 0.1 reduce_sum.9
  109.5 0.8 broadcast_in_dim.4
  110.3 5.9 %all-to-all-start.3 = ((f32[32,24,128]{2,1,0:T(8,128)}), f32[32,24,128]{2,1,0:T(8,128)S(1)}, u32[]{:S(2)}, u32[]{:S(2)}) async-start(f32[32,24,128]{2,1,0:T(8,128)} %broadcast_in_dim.4), calls=%async_computation.3 | async-start | bytes 786432 | tf_op jit(solution)/shard_map/all_to_all | solution.py:283
  116.2 12.9 %all-to-all-done.3.refs_0_ = f32[32,24,128]{2,1,0:T(8,128)S(1)} async-done(((f32[32,24,128]{2,1,0:T(8,128)}), f32[32,24,128]{2,1,0:T(8,128)S(1)}, u32[]{:S(2)}, u32[]{:S(2)}) %all-to-all-start.3) | async-done | bytes 393248 | tf_op jit(solution)/shard_map/all_to_all | solution.py:283
  129.1 0.9 broadcast_in_dim.5
  130.0 5.5 %all-to-all-start.4 = ((f32[32,32,128]{2,1,0:T(8,128)}), f32[32,32,128]{2,1,0:T(8,128)S(1)}, u32[]{:S(2)}, u32[]{:S(2)}) async-start(f32[32,32,128]{2,1,0:T(8,128)} %broadcast_in_dim.5), calls=%async_computation.4 | async-start | bytes 1048576 | tf_op jit(solution)/shard_map/all_to_all | solution.py:283
  135.6 0.5 collective-permute-start.12
  136.1 0.4 collective-permute-start.10
  136.5 0.6 collective-permute-start.8
  137.1 2.8 %collective-permute-start.7 = (f32[32,24,128]{2,1,0:T(8,128)S(1)}, f32[32,24,128]{2,1,0:T(8,128)S(1)}, u32[]{:S(2)}, u32[]{:S(2)}) collective-permute-start(f32[32,24,128]{2,1,0:T(8,128)S(1)} %all-to-all-done.3.refs_0_), channel_id=1, source_target_pairs={{0,1},{1,0},{2,3},{3,2},{4,5},{5,4},{6,7},{7,6},{8,9},{9,8},{10,11... | collective-permute-start | bytes 1179656 | tf_op jit(solution)/shard_map/ppermute | solution.py:297
  139.9 4.3 %collective-permute-done.12.refs_6_ = f32[32,24,128]{2,1,0:T(8,128)S(1)} collective-permute-done((f32[32,24,128]{2,1,0:T(8,128)S(1)}, f32[32,24,128]{2,1,0:T(8,128)S(1)}, u32[]{:S(2)}, u32[]{:S(2)}) %collective-permute-start.12) | collective-permute-done | bytes 393248 | tf_op jit(solution)/shard_map/ppermute | solution.py:294
  144.2 5.5 %collective-permute-start.13 = (f32[32,24,128]{2,1,0:T(8,128)S(1)}, f32[32,24,128]{2,1,0:T(8,128)S(1)}, u32[]{:S(2)}, u32[]{:S(2)}) collective-permute-start(f32[32,24,128]{2,1,0:T(8,128)S(1)} %collective-permute-done.12.refs_6_), channel_id=1, source_target_pairs={{0,1},{1,0},{2,3},{3,2},{4,5},{5,4},{6,7},{7,6},{8,9},{9,8},{10,11... | collective-permute-start | bytes 1179656 | tf_op jit(solution)/shard_map/ppermute | solution.py:297
  149.7 0.0 collective-permute-done.10.refs_4_
  149.7 2.2 %collective-permute-start.11 = (f32[32,24,128]{2,1,0:T(8,128)S(1)}, f32[32,24,128]{2,1,0:T(8,128)S(1)}, u32[]{:S(2)}, u32[]{:S(2)}) collective-permute-start(f32[32,24,128]{2,1,0:T(8,128)S(1)} %collective-permute-done.10.refs_4_), channel_id=1, source_target_pairs={{0,1},{1,0},{2,3},{3,2},{4,5},{5,4},{6,7},{7,6},{8,9},{9,8},{10,11... | collective-permute-start | bytes 1179656 | tf_op jit(solution)/shard_map/ppermute | solution.py:297
  151.9 5.1 %collective-permute-done.8.refs_2_ = f32[32,24,128]{2,1,0:T(8,128)S(1)} collective-permute-done((f32[32,24,128]{2,1,0:T(8,128)S(1)}, f32[32,24,128]{2,1,0:T(8,128)S(1)}, u32[]{:S(2)}, u32[]{:S(2)}) %collective-permute-start.8) | collective-permute-done | bytes 393248 | tf_op jit(solution)/shard_map/ppermute | solution.py:294
  157.0 0.5 collective-permute-start.9
  157.5 0.0 copy-start.3
  157.5 0.8 copy-done.3
  158.3 0.0 collective-permute-done.7.refs_1_
  158.3 0.0 copy-start.5
  158.3 0.7 copy-done.5
  159.0 0.0 collective-permute-done.13.refs_7_
  159.0 0.8 copy-done.7
  159.8 0.0 collective-permute-done.11.refs_5_
  159.8 0.8 copy-done.9
  160.6 0.0 collective-permute-done.9.refs_3_
  160.6 0.8 copy-done.11
  161.4 0.0 all-to-all-done.4.refs_8_
  161.4 0.0 copy-done
  161.4 0.0 copy-done.2
  161.4 0.0 copy-start.1
  161.4 2.2 %copy-done.1 = bf16[2048,1024]{1,0:T(8,128)(2,1)S(1)} copy-done((bf16[2048,1024]{1,0:T(8,128)(2,1)S(1)}, bf16[2048,1024]{1,0:T(8,128)(2,1)}, u32[]{:S(2)}) %copy-start.1) | copy-done | bytes 4194328
  163.6 1.0 copy-done.4
  164.6 1.0 copy-done.6
  165.5 1.0 copy-done.8
  166.5 1.0 copy-done.10
  167.5 1.0 copy-done.12
  168.5 32.9 %solve.1 = (f32[2,512,128]{2,1,0:T(8,128)}, f32[2048,128]{1,0:T(8,128)}) custom-call(f32[32,24,128]{2,1,0:T(8,128)S(1)} %all-to-all-done.3.refs_0_, f32[32,24,128]{2,1,0:T(8,128)S(1)} %copy-done.6, f32[32,24,128]{2,1,0:T(8,128)S(1)} %copy-done.4, f32[32,24,128]{2,1,0:T(8,128)S(1)} %copy-done.12, f32[32,24,128]{2,1,0:T(8,128)S(1)} %collective-permute-done.10.refs_4_, ...), custom_call_target="tpu_custom_call" | custom-call | tf_op jit(solution)/shard_map/solve/pallas_call | solution.py:261
  (10 shorter events, 0.0 us)
Async XLA Ops:
  44.8 8.9 %collective-permute-start.5 = (bf16[32,8,512]{2,1,0:T(8,128)(2,1)S(1)}, bf16[32,8,512]{2,1,0:T(8,128)(2,1)S(1)}, u32[]{:S(2)}, u32[]{:S(2)}) collective-permute-start(bf16[32,8,512]{2,1,0:T(8,128)(2,1)S(1)} %all_to_all.26.refs_0_), channel_id=1, source_target_pairs={{0,6},{2,0},{4,2},{6,4},{1,7},{3,1},{5,3},{7,5},{8,14},{10,8},{12,... | collective-permute-start | bytes 786440 | tf_op jit(solution)/shard_map/ppermute | solution.py:294
  47.3 12.2 %collective-permute-start.3 = (bf16[32,8,512]{2,1,0:T(8,128)(2,1)S(1)}, bf16[32,8,512]{2,1,0:T(8,128)(2,1)S(1)}, u32[]{:S(2)}, u32[]{:S(2)}) collective-permute-start(bf16[32,8,512]{2,1,0:T(8,128)(2,1)S(1)} %all_to_all.26.refs_0_), channel_id=1, source_target_pairs={{0,4},{2,6},{4,0},{6,2},{1,5},{3,7},{5,1},{7,3},{8,12},{10,14},{12... | collective-permute-start | bytes 786440 | tf_op jit(solution)/shard_map/ppermute | solution.py:294
  47.8 13.2 %collective-permute-start.1 = (bf16[32,8,512]{2,1,0:T(8,128)(2,1)S(1)}, bf16[32,8,512]{2,1,0:T(8,128)(2,1)S(1)}, u32[]{:S(2)}, u32[]{:S(2)}) collective-permute-start(bf16[32,8,512]{2,1,0:T(8,128)(2,1)S(1)} %all_to_all.26.refs_0_), channel_id=1, source_target_pairs={{0,2},{2,4},{4,6},{6,0},{1,3},{3,5},{5,7},{7,1},{8,10},{10,12},{12... | collective-permute-start | bytes 786440 | tf_op jit(solution)/shard_map/ppermute | solution.py:294
  48.4 14.7 %collective-permute-start = (bf16[32,8,512]{2,1,0:T(8,128)(2,1)S(1)}, bf16[32,8,512]{2,1,0:T(8,128)(2,1)S(1)}, u32[]{:S(2)}, u32[]{:S(2)}) collective-permute-start(bf16[32,8,512]{2,1,0:T(8,128)(2,1)S(1)} %all_to_all.26.refs_0_), channel_id=1, source_target_pairs={{0,1},{1,0},{2,3},{3,2},{4,5},{5,4},{6,7},{7,6},{8,9},{9,8},{10,11... | collective-permute-start | bytes 786440 | tf_op jit(solution)/shard_map/ppermute | solution.py:297
  53.7 9.5 %collective-permute-start.6 = (bf16[32,8,512]{2,1,0:T(8,128)(2,1)S(1)}, bf16[32,8,512]{2,1,0:T(8,128)(2,1)S(1)}, u32[]{:S(2)}, u32[]{:S(2)}) collective-permute-start(bf16[32,8,512]{2,1,0:T(8,128)(2,1)S(1)} %collective-permute-done.5.refs_6_), channel_id=1, source_target_pairs={{0,1},{1,0},{2,3},{3,2},{4,5},{5,4},{6,7},{7,6},{8,9},{9,8},{10,11... | collective-permute-start | bytes 786440 | tf_op jit(solution)/shard_map/ppermute | solution.py:297
  59.5 3.7 %collective-permute-start.4 = (bf16[32,8,512]{2,1,0:T(8,128)(2,1)S(1)}, bf16[32,8,512]{2,1,0:T(8,128)(2,1)S(1)}, u32[]{:S(2)}, u32[]{:S(2)}) collective-permute-start(bf16[32,8,512]{2,1,0:T(8,128)(2,1)S(1)} %collective-permute-done.3.refs_4_), channel_id=1, source_target_pairs={{0,1},{1,0},{2,3},{3,2},{4,5},{5,4},{6,7},{7,6},{8,9},{9,8},{10,11... | collective-permute-start | bytes 786440 | tf_op jit(solution)/shard_map/ppermute | solution.py:297
  61.1 3.2 %collective-permute-start.2 = (bf16[32,8,512]{2,1,0:T(8,128)(2,1)S(1)}, bf16[32,8,512]{2,1,0:T(8,128)(2,1)S(1)}, u32[]{:S(2)}, u32[]{:S(2)}) collective-permute-start(bf16[32,8,512]{2,1,0:T(8,128)(2,1)S(1)} %collective-permute-done.1.refs_2_), channel_id=1, source_target_pairs={{0,1},{1,0},{2,3},{3,2},{4,5},{5,4},{6,7},{7,6},{8,9},{9,8},{10,11... | collective-permute-start | bytes 786440 | tf_op jit(solution)/shard_map/ppermute | solution.py:297
  63.2 1.2 copy-start.14
  64.3 0.7 copy-start.13
  80.1 81.3 %copy-start = (f32[2048,128]{1,0:T(8,128)S(1)}, f32[2048,128]{1,0:T(8,128)}, u32[]{:S(2)}) copy-start(f32[2048,128]{1,0:T(8,128)} %refs_11_.1) | copy-start | bytes 3145732
  80.1 81.3 %copy-start.2 = (f32[2,512,128]{2,1,0:T(8,128)S(1)}, f32[2,512,128]{2,1,0:T(8,128)}, u32[]{:S(2)}) copy-start(f32[2,512,128]{2,1,0:T(8,128)} %refs_9_.1) | copy-start | bytes 1572868
  110.3 18.9 %all-to-all-start.3 = ((f32[32,24,128]{2,1,0:T(8,128)}), f32[32,24,128]{2,1,0:T(8,128)S(1)}, u32[]{:S(2)}, u32[]{:S(2)}) async-start(f32[32,24,128]{2,1,0:T(8,128)} %broadcast_in_dim.4), calls=%async_computation.3 | async-start | bytes 786432 | tf_op jit(solution)/shard_map/all_to_all | solution.py:283
  130.0 31.4 %all-to-all-start.4 = ((f32[32,32,128]{2,1,0:T(8,128)}), f32[32,32,128]{2,1,0:T(8,128)S(1)}, u32[]{:S(2)}, u32[]{:S(2)}) async-start(f32[32,32,128]{2,1,0:T(8,128)} %broadcast_in_dim.5), calls=%async_computation.4 | async-start | bytes 1048576 | tf_op jit(solution)/shard_map/all_to_all | solution.py:283
  135.6 8.7 %collective-permute-start.12 = (f32[32,24,128]{2,1,0:T(8,128)S(1)}, f32[32,24,128]{2,1,0:T(8,128)S(1)}, u32[]{:S(2)}, u32[]{:S(2)}) collective-permute-start(f32[32,24,128]{2,1,0:T(8,128)S(1)} %all-to-all-done.3.refs_0_), channel_id=1, source_target_pairs={{0,6},{2,0},{4,2},{6,4},{1,7},{3,1},{5,3},{7,5},{8,14},{10,8},{12,... | collective-permute-start | bytes 1179656 | tf_op jit(solution)/shard_map/ppermute | solution.py:294
  136.1 13.6 %collective-permute-start.10 = (f32[32,24,128]{2,1,0:T(8,128)S(1)}, f32[32,24,128]{2,1,0:T(8,128)S(1)}, u32[]{:S(2)}, u32[]{:S(2)}) collective-permute-start(f32[32,24,128]{2,1,0:T(8,128)S(1)} %all-to-all-done.3.refs_0_), channel_id=1, source_target_pairs={{0,4},{2,6},{4,0},{6,2},{1,5},{3,7},{5,1},{7,3},{8,12},{10,14},{12... | collective-permute-start | bytes 1179656 | tf_op jit(solution)/shard_map/ppermute | solution.py:294
  136.5 20.6 %collective-permute-start.8 = (f32[32,24,128]{2,1,0:T(8,128)S(1)}, f32[32,24,128]{2,1,0:T(8,128)S(1)}, u32[]{:S(2)}, u32[]{:S(2)}) collective-permute-start(f32[32,24,128]{2,1,0:T(8,128)S(1)} %all-to-all-done.3.refs_0_), channel_id=1, source_target_pairs={{0,2},{2,4},{4,6},{6,0},{1,3},{3,5},{5,7},{7,1},{8,10},{10,12},{12... | collective-permute-start | bytes 1179656 | tf_op jit(solution)/shard_map/ppermute | solution.py:294
  137.1 21.2 %collective-permute-start.7 = (f32[32,24,128]{2,1,0:T(8,128)S(1)}, f32[32,24,128]{2,1,0:T(8,128)S(1)}, u32[]{:S(2)}, u32[]{:S(2)}) collective-permute-start(f32[32,24,128]{2,1,0:T(8,128)S(1)} %all-to-all-done.3.refs_0_), channel_id=1, source_target_pairs={{0,1},{1,0},{2,3},{3,2},{4,5},{5,4},{6,7},{7,6},{8,9},{9,8},{10,11... | collective-permute-start | bytes 1179656 | tf_op jit(solution)/shard_map/ppermute | solution.py:297
  144.2 14.8 %collective-permute-start.13 = (f32[32,24,128]{2,1,0:T(8,128)S(1)}, f32[32,24,128]{2,1,0:T(8,128)S(1)}, u32[]{:S(2)}, u32[]{:S(2)}) collective-permute-start(f32[32,24,128]{2,1,0:T(8,128)S(1)} %collective-permute-done.12.refs_6_), channel_id=1, source_target_pairs={{0,1},{1,0},{2,3},{3,2},{4,5},{5,4},{6,7},{7,6},{8,9},{9,8},{10,11... | collective-permute-start | bytes 1179656 | tf_op jit(solution)/shard_map/ppermute | solution.py:297
  149.7 10.1 %collective-permute-start.11 = (f32[32,24,128]{2,1,0:T(8,128)S(1)}, f32[32,24,128]{2,1,0:T(8,128)S(1)}, u32[]{:S(2)}, u32[]{:S(2)}) collective-permute-start(f32[32,24,128]{2,1,0:T(8,128)S(1)} %collective-permute-done.10.refs_4_), channel_id=1, source_target_pairs={{0,1},{1,0},{2,3},{3,2},{4,5},{5,4},{6,7},{7,6},{8,9},{9,8},{10,11... | collective-permute-start | bytes 1179656 | tf_op jit(solution)/shard_map/ppermute | solution.py:297
  157.0 3.5 %collective-permute-start.9 = (f32[32,24,128]{2,1,0:T(8,128)S(1)}, f32[32,24,128]{2,1,0:T(8,128)S(1)}, u32[]{:S(2)}, u32[]{:S(2)}) collective-permute-start(f32[32,24,128]{2,1,0:T(8,128)S(1)} %collective-permute-done.8.refs_2_), channel_id=1, source_target_pairs={{0,1},{1,0},{2,3},{3,2},{4,5},{5,4},{6,7},{7,6},{8,9},{9,8},{10,11... | collective-permute-start | bytes 1179656 | tf_op jit(solution)/shard_map/ppermute | solution.py:297
  157.5 0.8 copy-start.3
  158.3 0.7 copy-start.5
  159.0 0.8 copy-start.7
  159.8 0.8 copy-start.9
  160.6 0.8 copy-start.11
  161.4 2.2 %copy-start.1 = (bf16[2048,1024]{1,0:T(8,128)(2,1)S(1)}, bf16[2048,1024]{1,0:T(8,128)(2,1)}, u32[]{:S(2)}) copy-start(bf16[2048,1024]{1,0:T(8,128)(2,1)} %get-tuple-element.15.refs_10_) | copy-start | bytes 12582916
  163.6 1.0 copy-start.4
  164.5 1.0 copy-start.6
  165.5 1.0 copy-start.8
  166.5 1.0 copy-start.10
  167.5 1.0 copy-start.12

commit v3 on v2

--- a/solution.py
+++ b/solution.py
@@ -15,15 +15,10 @@
 ROWS = ("z", "y")
 CLS = ("x", "c")
 
-SINE = (
-    6.283185160088491,
-    -41.34165503116555,
-    81.60100405640866,
-    -76.54978188256763,
-    39.536702776697375,
-)
-TOLERANCE = 1e-6
+SINE = (6.28316404416301, -41.33714234877015, 81.3407680297695, -70.99342411797343)
+TOLERANCE = 5e-5
 MAX_LOOPS = 2000
+UNROLL = 2
 
 
 def cosine(angle, scale):
@@ -109,11 +104,10 @@
 
 def feature_kernel(*refs):
     pieces = refs[:8]
-    e_ref, shift_ref, r_ref, f_ref, out_ref, w_ref, acc_ref = refs[8:]
+    e_ref, shift_ref, r_ref, f_ref, out_ref, w_ref, left_ref, all_ref = refs[8:]
     step = pl.program_id(0)
     width = w_ref.shape[2]
     scale = 1.0 / width**0.5
-    chunk = 256
 
     @pl.when(step == 0)
     def _():
@@ -125,38 +119,56 @@
                     part = pieces[shift * 2 + other][s * 16 : s * 16 + 16, :, :]
                     w_ref[s, pl.ds(at, 128), :] = part.reshape(128, width)
 
-    e = e_ref[...]
-    for s in range(STEPS):
-        for col in range(0, width, chunk):
-            angle = jnp.dot(e, w_ref[s, :, col : col + chunk], preferred_element_type=F32)
-            angle = angle + shift_ref[s : s + 1, col : col + chunk]
-            f_ref[:, s * width + col : s * width + col + chunk] = cosine(angle, scale).astype(BF)
+    spots = [
+        (row, s, col)
+        for row in range(0, e_ref.shape[0], 512)
+        for s in range(STEPS)
+        for col in range(0, width, 256)
+    ]
+
+    def angles(row, s, col):
+        return jnp.dot(e_ref[row : row + 512, :], w_ref[s, :, col : col + 256], preferred_element_type=F32)
+
+    ahead = [angles(*spot) for spot in spots[:1]]
+    for index, (row, s, col) in enumerate(spots):
+        if index + 1 < len(spots):
+            ahead.append(angles(*spots[index + 1]))
+        angle = ahead.pop(0) + shift_ref[s : s + 1, col : col + 256]
+        f_ref[row : row + 512, s * width + col : s * width + col + 256] = cosine(angle, scale).astype(BF)
     lane = lax.axis_index("x") * 128
     upper, lower = split_two(r_ref[...].T)
     left = [upper, lower]
     for s in range(STEPS):
         left.append(f_ref[:, pl.ds(pl.multiple_of(s * width + lane, 128), 128)].T)
-    left = jnp.concatenate(left, axis=0)
-    part = jnp.dot(left, f_ref[...], preferred_element_type=F32)
-
-    @pl.when(step == 0)
-    def _():
-        acc_ref[...] = part
-
-    @pl.when(step > 0)
-    def _():
-        acc_ref[...] += part
+    rows = e_ref.shape[0]
+    here = pl.multiple_of(step * rows, rows)
+    left_ref[:, pl.ds(here, rows)] = jnp.concatenate(left, axis=0)
+    all_ref[pl.ds(here, rows), :] = f_ref[...]
 
     @pl.when(step == pl.num_programs(0) - 1)
     def _():
-        half = lax.axis_index("c") * 256
-        for group, (row, first) in enumerate(((256, 0), (384, width), (384, 0))):
-            for side in range(2):
-                lanes = pl.ds(pl.multiple_of(first + half + side * 128, 128), 128)
-                block = acc_ref[row : row + 128, lanes]
-                out_ref[side * 16 : side * 16 + 16, group * 8 : group * 8 + 8, :] = block.reshape(16, 8, 128)
-        cross = acc_ref[0:128, :] + acc_ref[128:256, :]
-        out_ref[:, 24:56, :] = cross.T.reshape(32, 32, 128)
+        half = lax.axis_index("c")
+
+        def products(n, count):
+            right = all_ref[:, n * 256 : n * 256 + 256]
+            part = jnp.dot(left_ref[:count, :], right, preferred_element_type=F32)
+            cross = part[0:128] + part[128:256]
+            out_ref[n * 8 : n * 8 + 8, 24:56, :] = cross.T.reshape(8, 32, 128)
+            return part
+
+        for n in range(4):
+
+            @pl.when(half == n % 2)
+            def _():
+                part = products(n, 512)
+                for group, row in ((0, 256), (2, 384)) if n < 2 else ((1, 384),):
+                    for side in range(2):
+                        block = part[row : row + 128, side * 128 : side * 128 + 128].reshape(16, 8, 128)
+                        out_ref[side * 16 : side * 16 + 16, group * 8 : group * 8 + 8, :] = block
+
+            @pl.when(half != n % 2)
+            def _():
+                products(n, 256)
 
 
 def features(pieces, embeddings, shifts, residuals):
@@ -178,7 +190,11 @@
             jax.ShapeDtypeStruct((total, STEPS * width), BF),
             jax.ShapeDtypeStruct((32, 56, 128), F32),
         ],
-        scratch_shapes=[pltpu.VMEM((STEPS, depth, width), BF), pltpu.VMEM((512, STEPS * width), F32)],
+        scratch_shapes=[
+            pltpu.VMEM((STEPS, depth, width), BF),
+            pltpu.VMEM((512, total), BF),
+            pltpu.VMEM((total, STEPS * width), BF),
+        ],
         compiler_params=pltpu.CompilerParams(vmem_limit_bytes=52 << 20),
         name="features",
     )(*pieces, embeddings, shifts, residuals)
@@ -190,36 +206,75 @@
     return both[:, :128] + both[:, 128:] + jnp.dot(lower, high, preferred_element_type=F32)
 
 
-def conjugate_gradients(upper_ref, lower_ref, right, ridge):
-    size = jnp.sum(right * right, axis=0, keepdims=True)
-    floor = size * (TOLERANCE * TOLERANCE)
-
-    def one(x, r, p, rr):
-        ap = times(upper_ref[...], lower_ref[...], p) + ridge * p
-        curve = jnp.sum(p * ap, axis=0, keepdims=True)
+def folded(values):
+    part = [values[row : row + 8] for row in range(0, values.shape[0], 8)]
+    while len(part) > 1:
+        part = [part[i] + part[i + 1] for i in range(0, len(part), 2)]
+    return part[0]
+
+
+def total(parts):
+    while len(parts) > 1:
+        parts = [parts[i] + parts[i + 1] for i in range(0, len(parts), 2)]
+    return jnp.sum(parts[0], axis=0, keepdims=True)
+
+
+def conjugate_gradients(upper_ref, lower_ref, x_ref, r_ref, p_ref, ap_ref, parts_ref, ridge):
+    n = r_ref.shape[0]
+    bound = (TOLERANCE * ridge) ** 2
+    bands = [slice(row, row + 128) for row in range(0, n, 128)]
+
+    def direct(band, p):
+        p_ref[band] = p
+        high, low = split_two(p)
+        parts_ref[band, :128] = high
+        parts_ref[band, 128:] = low
+
+    def one(rr):
+        sums = []
+        for row in range(0, n, 512):
+            band = slice(row, row + 512)
+            both = jnp.dot(upper_ref[band, :], parts_ref[...], preferred_element_type=F32)
+            rest = jnp.dot(lower_ref[band, :], parts_ref[:, :128], preferred_element_type=F32)
+            p = p_ref[band]
+            ap = both[:, :128] + both[:, 128:] + rest + ridge * p
+            ap_ref[band] = ap
+            sums.append(folded(p * ap))
+        curve = total(sums)
         alpha = jnp.where(curve > 0.0, rr / curve, 0.0)
-        x = x + alpha * p
-        r = r - alpha * ap
-        new = jnp.sum(r * r, axis=0, keepdims=True)
+        sums = []
+        for band in bands:
+            r = r_ref[band] - alpha * ap_ref[band]
+            r_ref[band] = r
+            sums.append(folded(r * r))
+        new = total(sums)
         beta = jnp.where(rr > 0.0, new / rr, 0.0)
-        return x, r, r + beta * p, new
+        for band in bands:
+            p = p_ref[band]
+            x_ref[band] += alpha * p
+            direct(band, r_ref[band] + beta * p)
+        return new
+
+    def open_still(state):
+        return jnp.logical_and(state[0] < MAX_LOOPS, state[1] > 0.0)
 
     def body(state):
-        count, x, r, p, rr = state
-        for _ in range(2):
-            x, r, p, rr = one(x, r, p, rr)
-        return count + 1, x, r, p, rr
-
-    def open_still(state):
-        return jnp.logical_and(state[0] < MAX_LOOPS, jnp.max(state[4] - floor) > 0.0)
-
-    state = (jnp.int32(0), jnp.zeros_like(right), right, right, size)
-    return lax.while_loop(open_still, body, state)[1]
+        rr = state[2]
+        for _ in range(UNROLL):
+            rr = one(rr)
+        size = total([folded(x_ref[band] * x_ref[band]) for band in bands])
+        return state[0] + 1, jnp.max(rr - bound * size), rr
+
+    for band in bands:
+        x_ref[band] = jnp.zeros_like(r_ref[band])
+        direct(band, r_ref[band])
+    size = total([folded(r_ref[band] * r_ref[band]) for band in bands])
+    lax.while_loop(open_still, body, (jnp.int32(0), jnp.float32(1.0), size))
 
 
 def solve_kernel(ridge, *refs):
     pieces = refs[:8]
-    cross_ref, old_ref, f_hbm, r_hbm, coef_ref, out_ref, upper, lower, f_ref, r_ref, sems = refs[8:]
+    cross_ref, old_ref, f_hbm, r_hbm, coef_ref, out_ref, upper, lower, f_ref, r_ref, x_ref, res_ref, p_ref, ap_ref, parts_ref, delta_ref, sems = refs[8:]
     loads = [
         pltpu.make_async_copy(f_hbm, f_ref, sems.at[0]),
         pltpu.make_async_copy(r_hbm, r_ref, sems.at[1]),
@@ -238,14 +293,24 @@
                     high, low = split_two(block)
                     upper[group, pl.ds(row, 128), lanes] = high
                     lower[group, pl.ds(row, 128), lanes] = low
-    cross = cross_ref[...].reshape(1024, 128)
-    first = conjugate_gradients(upper.at[0], lower.at[0], cross[:512] - ridge * old_ref[0], ridge)
+    n = upper.shape[1]
+    per = 32 // STEPS
+    work = (x_ref, res_ref, p_ref, ap_ref, parts_ref)
+    res_ref[...] = cross_ref[:per].reshape(n, 128) - ridge * old_ref[0]
+    conjugate_gradients(upper.at[0], lower.at[0], *work, ridge)
+    first = x_ref[...]
     coef_ref[0] = old_ref[0] + first
-    cross = cross[512:] - times(upper[2], lower[2], first)
-    second = conjugate_gradients(upper.at[1], lower.at[1], cross - ridge * old_ref[1], ridge)
+    res_ref[...] = cross_ref[per:].reshape(n, 128) - ridge * old_ref[1] - times(upper[2], lower[2], first)
+    high_first, low_first = split_two(first)
+    delta_ref[:n, :128] = high_first
+    delta_ref[:n, 128:] = low_first
+    conjugate_gradients(upper.at[1], lower.at[1], *work, ridge)
+    second = x_ref[...]
     coef_ref[1] = old_ref[1] + second
-    high, low = split_two(jnp.concatenate([first, second], axis=0))
-    delta = jnp.concatenate([high, low], axis=1)
+    high, low = split_two(second)
+    delta_ref[n:, :128] = high
+    delta_ref[n:, 128:] = low
+    delta = delta_ref[...]
     tile = 256
     for load in loads:
         load.wait()
@@ -272,9 +337,15 @@
             pltpu.VMEM((3, 512, 512), BF),
             pltpu.VMEM(feats.shape, BF),
             pltpu.VMEM(residuals.shape, F32),
+            pltpu.VMEM((512, 128), F32),
+            pltpu.VMEM((512, 128), F32),
+            pltpu.VMEM((512, 128), F32),
+            pltpu.VMEM((512, 128), F32),
+            pltpu.VMEM((512, 256), BF),
+            pltpu.VMEM((1024, 256), BF),
             pltpu.SemaphoreType.DMA((2,)),
         ],
-        compiler_params=pltpu.CompilerParams(vmem_limit_bytes=36 << 20),
+        compiler_params=pltpu.CompilerParams(vmem_limit_bytes=52 << 20),
         name="solve",
     )(*pieces, cross, old, feats, residuals)
 

time: 203 us -> 187 us (0.921); the launches traced: 202 us -> 191 us
  local copies, waits for them, and re-layouts: 13.3 us -> 3.92 us
  Pallas kernels: 52.1 us -> 50 us
    unnamed x30 -> x12, local copies, waits for them, and re-layouts: 11.7 us -> 2.29 us
  transfers between devices with their start and end apart: 16 -> 16, of which waited for: 6 -> 7; matrix products, arithmetic and copies ran while one was open for 0% -> 0% of each run, Pallas kernels for 0% -> 0%
where the time goes in v3:
time: 187 us; the launch traced here: 191 us
  blocking collectives  69.3 us (37%)
  Pallas kernels  50 us (27%)
  starting transfers between devices  40.9 us (22%)
  waiting for transfers between devices  25.5 us (14%)
  local copies, waits for them, and re-layouts  3.92 us (2%)
    all_to_all x3, blocking collectives, exchange(): return lax.all_to_all(values, axes, split_axis=0, concat_axis=0, tiled=True)  69.3 us
    pallas_call x1, Pallas kernels, solve(): pl.pallas_call(functools.partial(solve_kernel, ridge), in_specs=[full(pie...  32 us
    ppermute x8, starting transfers between devices, spread(): lax.ppermute(value, 'c', [(i, (i + 1) % nc) for i in range(nc)])  24.2 us
    pallas_call x1, Pallas kernels, features(): pl.pallas_call(feature_kernel, grid=(total // tile,), in_specs=[whole] *...  14 us
    all_to_all x2, waiting for transfers between devices, exchange(): return lax.all_to_all(values, axes, split_axis=0, concat_axis=0, tiled=True)  12.9 us
    all_to_all x2, starting transfers between devices, exchange(): return lax.all_to_all(values, axes, split_axis=0, concat_axis=0, tiled=True)  11.5 us
    ppermute x6, waiting for transfers between devices, spread(): lax.ppermute(values, 'x', [(i, (i + shift) % nx) for i in range(nx)])  10.9 us
    ppermute x6, starting transfers between devices, spread(): lax.ppermute(values, 'x', [(i, (i + shift) % nx) for i in range(nx)])  5.15 us
  transfers between devices with their start and end apart: 16, of which 7 were waited for; matrix products, arithmetic and copies ran while one was open for 0% of the time, Pallas kernels for 0%

profile of v3, /device:TPU:1, one launch (start us, length us, event | category | flops | bytes accessed | tf_op | source)
XLA Modules:
  0.0 190.6 jit_solution(9390201566228202229)
XLA Ops:
  0.6 2.4 %payload.1 = bf16[32,8,640]{2,1,0:T(8,128)(2,1)} custom-call(s32[2]{0:T(128)} %order.3, bf16[2,1024,512]{2,1,0:T(8,128)(2,1)} %proj_ref.1, bf16[2,512]{1,0:T(2,128)(2,1)} %phase_ref.1), custom_call_target="tpu_custom_call" | custom-call | tf_op jit(solution)/shard_map/payload/pallas_call | solution.py:67
  3.0 24.8 %all_to_all.25.got_ref = bf16[32,8,640]{2,1,0:T(8,128)(2,1)} all-to-all(bf16[32,8,640]{2,1,0:T(8,128)(2,1)} %payload.1), channel_id=1, replica_groups=mesh['z'=8,'y'=4,'x'=4,'c'=2] {'z','y'}, dimensions={0} | all-to-all | bytes 655360 | tf_op jit(solution)/shard_map/all_to_all | solution.py:354
  27.8 1.7 pick.1
  29.6 15.3 %all_to_all.26.refs_0_ = bf16[32,8,512]{2,1,0:T(8,128)(2,1)S(1)} all-to-all(bf16[32,8,512]{2,1,0:T(8,128)(2,1)} %get-tuple-element.10), channel_id=1, replica_groups=mesh['z'=8,'y'=4,'x'=4,'c'=2] {'z','y'}, dimensions={0} | all-to-all | bytes 524288 | tf_op jit(solution)/shard_map/all_to_all | solution.py:354
  44.8 2.5 %collective-permute-start.5 = (bf16[32,8,512]{2,1,0:T(8,128)(2,1)S(1)}, bf16[32,8,512]{2,1,0:T(8,128)(2,1)S(1)}, u32[]{:S(2)}, u32[]{:S(2)}) collective-permute-start(bf16[32,8,512]{2,1,0:T(8,128)(2,1)S(1)} %all_to_all.26.refs_0_), channel_id=1, source_target_pairs={{0,6},{2,0},{4,2},{6,4},{1,7},{3,1},{5,3},{7,5},{8,14},{10,8},{12,... | collective-permute-start | bytes 786440 | tf_op jit(solution)/shard_map/ppermute | solution.py:365
  47.3 0.5 collective-permute-start.3
  47.8 0.6 collective-permute-start.1
  48.4 4.3 %collective-permute-start = (bf16[32,8,512]{2,1,0:T(8,128)(2,1)S(1)}, bf16[32,8,512]{2,1,0:T(8,128)(2,1)S(1)}, u32[]{:S(2)}, u32[]{:S(2)}) collective-permute-start(bf16[32,8,512]{2,1,0:T(8,128)(2,1)S(1)} %all_to_all.26.refs_0_), channel_id=1, source_target_pairs={{0,1},{1,0},{2,3},{3,2},{4,5},{5,4},{6,7},{7,6},{8,9},{9,8},{10,11... | collective-permute-start | bytes 786440 | tf_op jit(solution)/shard_map/ppermute | solution.py:368
  52.8 0.9 collective-permute-done.5.refs_6_
  53.7 5.8 %collective-permute-start.6 = (bf16[32,8,512]{2,1,0:T(8,128)(2,1)S(1)}, bf16[32,8,512]{2,1,0:T(8,128)(2,1)S(1)}, u32[]{:S(2)}, u32[]{:S(2)}) collective-permute-start(bf16[32,8,512]{2,1,0:T(8,128)(2,1)S(1)} %collective-permute-done.5.refs_6_), channel_id=1, source_target_pairs={{0,1},{1,0},{2,3},{3,2},{4,5},{5,4},{6,7},{7,6},{8,9},{9,8},{10,11... | collective-permute-start | bytes 786440 | tf_op jit(solution)/shard_map/ppermute | solution.py:368
  59.5 0.0 collective-permute-done.3.refs_4_
  59.5 1.0 collective-permute-start.4
  60.5 0.6 collective-permute-done.1.refs_2_
  61.1 2.1 %collective-permute-start.2 = (bf16[32,8,512]{2,1,0:T(8,128)(2,1)S(1)}, bf16[32,8,512]{2,1,0:T(8,128)(2,1)S(1)}, u32[]{:S(2)}, u32[]{:S(2)}) collective-permute-start(bf16[32,8,512]{2,1,0:T(8,128)(2,1)S(1)} %collective-permute-done.1.refs_2_), channel_id=1, source_target_pairs={{0,1},{1,0},{2,3},{3,2},{4,5},{5,4},{6,7},{7,6},{8,9},{9,8},{10,11... | collective-permute-start | bytes 786440 | tf_op jit(solution)/shard_map/ppermute | solution.py:368
  63.2 0.0 collective-permute-done.refs_1_
  63.2 0.0 collective-permute-done.6.refs_7_
  63.2 0.0 copy-start.5
  63.2 0.0 collective-permute-done.4.refs_5_
  63.2 1.1 collective-permute-done.2.refs_3_
  64.3 0.0 copy-done.5
  64.3 0.0 copy-start
  64.3 0.7 copy-done
  65.0 14.0 %features.1 = (bf16[2048,1024]{1,0:T(8,128)(2,1)}, f32[32,56,128]{2,1,0:T(8,128)}) custom-call(bf16[32,8,512]{2,1,0:T(8,128)(2,1)S(1)} %all_to_all.26.refs_0_, bf16[32,8,512]{2,1,0:T(8,128)(2,1)S(1)} %collective-permute-done.refs_1_, bf16[32,8,512]{2,1,0:T(8,128)(2,1)S(1)} %collective-permute-done.1.refs_2_, ...), custom_call_target="tpu_custom_call" | custom-call | tf_op jit(solution)/shard_map/features/pallas_call | solution.py:179
  79.0 29.2 %all_to_all.27 = f32[32,56,128]{2,1,0:T(8,128)S(1)} all-to-all(f32[32,56,128]{2,1,0:T(8,128)} %get-tuple-element.12), channel_id=1, replica_groups=mesh['z'=8,'y'=4,'x'=4,'c'=2] {'z','y'}, dimensions={0} | all-to-all | bytes 1835008 | tf_op jit(solution)/shard_map/all_to_all | solution.py:354
  108.2 0.1 reduce_sum.9
  108.2 0.8 broadcast_in_dim.4
  109.0 5.9 %all-to-all-start.3 = ((f32[32,24,128]{2,1,0:T(8,128)}), f32[32,24,128]{2,1,0:T(8,128)S(1)}, u32[]{:S(2)}, u32[]{:S(2)}) async-start(f32[32,24,128]{2,1,0:T(8,128)} %broadcast_in_dim.4), calls=%async_computation.3 | async-start | bytes 786432 | tf_op jit(solution)/shard_map/all_to_all | solution.py:354
  115.0 12.9 %all-to-all-done.3.refs_0_ = f32[32,24,128]{2,1,0:T(8,128)S(1)} async-done(((f32[32,24,128]{2,1,0:T(8,128)}), f32[32,24,128]{2,1,0:T(8,128)S(1)}, u32[]{:S(2)}, u32[]{:S(2)}) %all-to-all-start.3) | async-done | bytes 393248 | tf_op jit(solution)/shard_map/all_to_all | solution.py:354
  127.9 0.9 broadcast_in_dim.5
  128.7 5.5 %all-to-all-start.4 = ((f32[32,32,128]{2,1,0:T(8,128)}), f32[32,32,128]{2,1,0:T(8,128)S(1)}, u32[]{:S(2)}, u32[]{:S(2)}) async-start(f32[32,32,128]{2,1,0:T(8,128)} %broadcast_in_dim.5), calls=%async_computation.4 | async-start | bytes 1048576 | tf_op jit(solution)/shard_map/all_to_all | solution.py:354
  134.3 0.5 collective-permute-start.12
  134.8 0.4 collective-permute-start.10
  135.2 0.6 collective-permute-start.8
  135.8 2.8 %collective-permute-start.7 = (f32[32,24,128]{2,1,0:T(8,128)S(1)}, f32[32,24,128]{2,1,0:T(8,128)S(1)}, u32[]{:S(2)}, u32[]{:S(2)}) collective-permute-start(f32[32,24,128]{2,1,0:T(8,128)S(1)} %all-to-all-done.3.refs_0_), channel_id=1, source_target_pairs={{0,1},{1,0},{2,3},{3,2},{4,5},{5,4},{6,7},{7,6},{8,9},{9,8},{10,11... | collective-permute-start | bytes 1179656 | tf_op jit(solution)/shard_map/ppermute | solution.py:368
  138.7 4.3 %collective-permute-done.12.refs_6_ = f32[32,24,128]{2,1,0:T(8,128)S(1)} collective-permute-done((f32[32,24,128]{2,1,0:T(8,128)S(1)}, f32[32,24,128]{2,1,0:T(8,128)S(1)}, u32[]{:S(2)}, u32[]{:S(2)}) %collective-permute-start.12) | collective-permute-done | bytes 393248 | tf_op jit(solution)/shard_map/ppermute | solution.py:365
  142.9 0.0 copy-start.2
  143.0 5.5 %collective-permute-start.13 = (f32[32,24,128]{2,1,0:T(8,128)S(1)}, f32[32,24,128]{2,1,0:T(8,128)S(1)}, u32[]{:S(2)}, u32[]{:S(2)}) collective-permute-start(f32[32,24,128]{2,1,0:T(8,128)S(1)} %collective-permute-done.12.refs_6_), channel_id=1, source_target_pairs={{0,1},{1,0},{2,3},{3,2},{4,5},{5,4},{6,7},{7,6},{8,9},{9,8},{10,11... | collective-permute-start | bytes 1179656 | tf_op jit(solution)/shard_map/ppermute | solution.py:368
  148.4 0.0 collective-permute-done.10.refs_4_
  148.4 2.2 %collective-permute-start.11 = (f32[32,24,128]{2,1,0:T(8,128)S(1)}, f32[32,24,128]{2,1,0:T(8,128)S(1)}, u32[]{:S(2)}, u32[]{:S(2)}) collective-permute-start(f32[32,24,128]{2,1,0:T(8,128)S(1)} %collective-permute-done.10.refs_4_), channel_id=1, source_target_pairs={{0,1},{1,0},{2,3},{3,2},{4,5},{5,4},{6,7},{7,6},{8,9},{9,8},{10,11... | collective-permute-start | bytes 1179656 | tf_op jit(solution)/shard_map/ppermute | solution.py:368
  150.7 5.1 %collective-permute-done.8.refs_2_ = f32[32,24,128]{2,1,0:T(8,128)S(1)} collective-permute-done((f32[32,24,128]{2,1,0:T(8,128)S(1)}, f32[32,24,128]{2,1,0:T(8,128)S(1)}, u32[]{:S(2)}, u32[]{:S(2)}) %collective-permute-start.8) | collective-permute-done | bytes 393248 | tf_op jit(solution)/shard_map/ppermute | solution.py:365
  155.8 0.5 collective-permute-start.9
  156.3 0.0 collective-permute-done.7.refs_1_
  156.3 0.0 collective-permute-done.13.refs_7_
  156.3 0.0 copy-start.3
  156.3 0.0 collective-permute-done.11.refs_5_
  156.3 0.0 copy-start.4
  156.3 0.8 copy-done.4
  157.1 0.5 collective-permute-done.9.refs_3_
  157.6 0.0 all-to-all-done.4.refs_8_
  157.6 0.0 copy-start.1
  157.6 0.0 copy-done.2
  157.6 0.0 copy-done.3
  157.6 0.8 copy-done.1
  158.4 32.0 %solve.1 = (f32[2,512,128]{2,1,0:T(8,128)}, f32[2048,128]{1,0:T(8,128)}) custom-call(f32[32,24,128]{2,1,0:T(8,128)S(1)} %all-to-all-done.3.refs_0_, f32[32,24,128]{2,1,0:T(8,128)S(1)} %collective-permute-done.7.refs_1_, f32[32,24,128]{2,1,0:T(8,128)S(1)} %collective-permute-done.8.refs_2_, f32[32,24,128]{2,1,0:T(8,128)S(1)} %collective-permute-done.9.refs_3_, ...), custom_call_target="tpu_custom_call" | custom-call | tf_op jit(solution)/shard_map/solve/pallas_call | solution.py:326
  (2 shorter events, 0.0 us)
Async XLA Ops:
  44.8 8.9 %collective-permute-start.5 = (bf16[32,8,512]{2,1,0:T(8,128)(2,1)S(1)}, bf16[32,8,512]{2,1,0:T(8,128)(2,1)S(1)}, u32[]{:S(2)}, u32[]{:S(2)}) collective-permute-start(bf16[32,8,512]{2,1,0:T(8,128)(2,1)S(1)} %all_to_all.26.refs_0_), channel_id=1, source_target_pairs={{0,6},{2,0},{4,2},{6,4},{1,7},{3,1},{5,3},{7,5},{8,14},{10,8},{12,... | collective-permute-start | bytes 786440 | tf_op jit(solution)/shard_map/ppermute | solution.py:365
  47.3 12.2 %collective-permute-start.3 = (bf16[32,8,512]{2,1,0:T(8,128)(2,1)S(1)}, bf16[32,8,512]{2,1,0:T(8,128)(2,1)S(1)}, u32[]{:S(2)}, u32[]{:S(2)}) collective-permute-start(bf16[32,8,512]{2,1,0:T(8,128)(2,1)S(1)} %all_to_all.26.refs_0_), channel_id=1, source_target_pairs={{0,4},{2,6},{4,0},{6,2},{1,5},{3,7},{5,1},{7,3},{8,12},{10,14},{12... | collective-permute-start | bytes 786440 | tf_op jit(solution)/shard_map/ppermute | solution.py:365
  47.8 13.2 %collective-permute-start.1 = (bf16[32,8,512]{2,1,0:T(8,128)(2,1)S(1)}, bf16[32,8,512]{2,1,0:T(8,128)(2,1)S(1)}, u32[]{:S(2)}, u32[]{:S(2)}) collective-permute-start(bf16[32,8,512]{2,1,0:T(8,128)(2,1)S(1)} %all_to_all.26.refs_0_), channel_id=1, source_target_pairs={{0,2},{2,4},{4,6},{6,0},{1,3},{3,5},{5,7},{7,1},{8,10},{10,12},{12... | collective-permute-start | bytes 786440 | tf_op jit(solution)/shard_map/ppermute | solution.py:365
  48.4 14.7 %collective-permute-start = (bf16[32,8,512]{2,1,0:T(8,128)(2,1)S(1)}, bf16[32,8,512]{2,1,0:T(8,128)(2,1)S(1)}, u32[]{:S(2)}, u32[]{:S(2)}) collective-permute-start(bf16[32,8,512]{2,1,0:T(8,128)(2,1)S(1)} %all_to_all.26.refs_0_), channel_id=1, source_target_pairs={{0,1},{1,0},{2,3},{3,2},{4,5},{5,4},{6,7},{7,6},{8,9},{9,8},{10,11... | collective-permute-start | bytes 786440 | tf_op jit(solution)/shard_map/ppermute | solution.py:368
  53.7 9.5 %collective-permute-start.6 = (bf16[32,8,512]{2,1,0:T(8,128)(2,1)S(1)}, bf16[32,8,512]{2,1,0:T(8,128)(2,1)S(1)}, u32[]{:S(2)}, u32[]{:S(2)}) collective-permute-start(bf16[32,8,512]{2,1,0:T(8,128)(2,1)S(1)} %collective-permute-done.5.refs_6_), channel_id=1, source_target_pairs={{0,1},{1,0},{2,3},{3,2},{4,5},{5,4},{6,7},{7,6},{8,9},{9,8},{10,11... | collective-permute-start | bytes 786440 | tf_op jit(solution)/shard_map/ppermute | solution.py:368
  59.5 3.7 %collective-permute-start.4 = (bf16[32,8,512]{2,1,0:T(8,128)(2,1)S(1)}, bf16[32,8,512]{2,1,0:T(8,128)(2,1)S(1)}, u32[]{:S(2)}, u32[]{:S(2)}) collective-permute-start(bf16[32,8,512]{2,1,0:T(8,128)(2,1)S(1)} %collective-permute-done.3.refs_4_), channel_id=1, source_target_pairs={{0,1},{1,0},{2,3},{3,2},{4,5},{5,4},{6,7},{7,6},{8,9},{9,8},{10,11... | collective-permute-start | bytes 786440 | tf_op jit(solution)/shard_map/ppermute | solution.py:368
  61.1 3.2 %collective-permute-start.2 = (bf16[32,8,512]{2,1,0:T(8,128)(2,1)S(1)}, bf16[32,8,512]{2,1,0:T(8,128)(2,1)S(1)}, u32[]{:S(2)}, u32[]{:S(2)}) collective-permute-start(bf16[32,8,512]{2,1,0:T(8,128)(2,1)S(1)} %collective-permute-done.1.refs_2_), channel_id=1, source_target_pairs={{0,1},{1,0},{2,3},{3,2},{4,5},{5,4},{6,7},{7,6},{8,9},{9,8},{10,11... | collective-permute-start | bytes 786440 | tf_op jit(solution)/shard_map/ppermute | solution.py:368
  63.2 1.2 copy-start.5
  64.3 0.7 copy-start
  109.0 18.9 %all-to-all-start.3 = ((f32[32,24,128]{2,1,0:T(8,128)}), f32[32,24,128]{2,1,0:T(8,128)S(1)}, u32[]{:S(2)}, u32[]{:S(2)}) async-start(f32[32,24,128]{2,1,0:T(8,128)} %broadcast_in_dim.4), calls=%async_computation.3 | async-start | bytes 786432 | tf_op jit(solution)/shard_map/all_to_all | solution.py:354
  128.7 28.9 %all-to-all-start.4 = ((f32[32,32,128]{2,1,0:T(8,128)}), f32[32,32,128]{2,1,0:T(8,128)S(1)}, u32[]{:S(2)}, u32[]{:S(2)}) async-start(f32[32,32,128]{2,1,0:T(8,128)} %broadcast_in_dim.5), calls=%async_computation.4 | async-start | bytes 1048576 | tf_op jit(solution)/shard_map/all_to_all | solution.py:354
  134.3 8.7 %collective-permute-start.12 = (f32[32,24,128]{2,1,0:T(8,128)S(1)}, f32[32,24,128]{2,1,0:T(8,128)S(1)}, u32[]{:S(2)}, u32[]{:S(2)}) collective-permute-start(f32[32,24,128]{2,1,0:T(8,128)S(1)} %all-to-all-done.3.refs_0_), channel_id=1, source_target_pairs={{0,6},{2,0},{4,2},{6,4},{1,7},{3,1},{5,3},{7,5},{8,14},{10,8},{12,... | collective-permute-start | bytes 1179656 | tf_op jit(solution)/shard_map/ppermute | solution.py:365
  134.8 13.6 %collective-permute-start.10 = (f32[32,24,128]{2,1,0:T(8,128)S(1)}, f32[32,24,128]{2,1,0:T(8,128)S(1)}, u32[]{:S(2)}, u32[]{:S(2)}) collective-permute-start(f32[32,24,128]{2,1,0:T(8,128)S(1)} %all-to-all-done.3.refs_0_), channel_id=1, source_target_pairs={{0,4},{2,6},{4,0},{6,2},{1,5},{3,7},{5,1},{7,3},{8,12},{10,14},{12... | collective-permute-start | bytes 1179656 | tf_op jit(solution)/shard_map/ppermute | solution.py:365
  135.2 20.6 %collective-permute-start.8 = (f32[32,24,128]{2,1,0:T(8,128)S(1)}, f32[32,24,128]{2,1,0:T(8,128)S(1)}, u32[]{:S(2)}, u32[]{:S(2)}) collective-permute-start(f32[32,24,128]{2,1,0:T(8,128)S(1)} %all-to-all-done.3.refs_0_), channel_id=1, source_target_pairs={{0,2},{2,4},{4,6},{6,0},{1,3},{3,5},{5,7},{7,1},{8,10},{10,12},{12... | collective-permute-start | bytes 1179656 | tf_op jit(solution)/shard_map/ppermute | solution.py:365
  135.8 20.4 %collective-permute-start.7 = (f32[32,24,128]{2,1,0:T(8,128)S(1)}, f32[32,24,128]{2,1,0:T(8,128)S(1)}, u32[]{:S(2)}, u32[]{:S(2)}) collective-permute-start(f32[32,24,128]{2,1,0:T(8,128)S(1)} %all-to-all-done.3.refs_0_), channel_id=1, source_target_pairs={{0,1},{1,0},{2,3},{3,2},{4,5},{5,4},{6,7},{7,6},{8,9},{9,8},{10,11... | collective-permute-start | bytes 1179656 | tf_op jit(solution)/shard_map/ppermute | solution.py:368
  142.9 14.7 %copy-start.2 = (f32[32,24,128]{2,1,0:T(8,128)}, f32[32,24,128]{2,1,0:T(8,128)S(1)}, u32[]{:S(2)}) copy-start(f32[32,24,128]{2,1,0:T(8,128)S(1)} %collective-permute-done.12.refs_6_) | copy-start | bytes 1179652
  143.0 13.3 %collective-permute-start.13 = (f32[32,24,128]{2,1,0:T(8,128)S(1)}, f32[32,24,128]{2,1,0:T(8,128)S(1)}, u32[]{:S(2)}, u32[]{:S(2)}) collective-permute-start(f32[32,24,128]{2,1,0:T(8,128)S(1)} %collective-permute-done.12.refs_6_), channel_id=1, source_target_pairs={{0,1},{1,0},{2,3},{3,2},{4,5},{5,4},{6,7},{7,6},{8,9},{9,8},{10,11... | collective-permute-start | bytes 1179656 | tf_op jit(solution)/shard_map/ppermute | solution.py:368
  148.4 7.9 %collective-permute-start.11 = (f32[32,24,128]{2,1,0:T(8,128)S(1)}, f32[32,24,128]{2,1,0:T(8,128)S(1)}, u32[]{:S(2)}, u32[]{:S(2)}) collective-permute-start(f32[32,24,128]{2,1,0:T(8,128)S(1)} %collective-permute-done.10.refs_4_), channel_id=1, source_target_pairs={{0,1},{1,0},{2,3},{3,2},{4,5},{5,4},{6,7},{7,6},{8,9},{9,8},{10,11... | collective-permute-start | bytes 1179656 | tf_op jit(solution)/shard_map/ppermute | solution.py:368
  155.8 1.8 collective-permute-start.9
  156.3 1.4 copy-start.3
  156.3 0.8 copy-start.4
  157.6 0.8 copy-start.1

commit v4 on v3

--- a/solution.py
+++ b/solution.py
@@ -102,11 +102,13 @@
     )(order, got)
 
 
-def feature_kernel(*refs):
+def feature_kernel(s, *refs):
     pieces = refs[:8]
+    if s:
+        f_before, refs = refs[11], refs[:11] + refs[12:]
     e_ref, shift_ref, r_ref, f_ref, out_ref, w_ref, left_ref, all_ref = refs[8:]
     step = pl.program_id(0)
-    width = w_ref.shape[2]
+    width = w_ref.shape[1]
     scale = 1.0 / width**0.5
 
     @pl.when(step == 0)
@@ -115,89 +117,84 @@
             for other in range(2):
                 px, pc = offsets(shift, other)
                 at = pl.multiple_of(px * 256 + pc * 128, 128)
-                for s in range(STEPS):
-                    part = pieces[shift * 2 + other][s * 16 : s * 16 + 16, :, :]
-                    w_ref[s, pl.ds(at, 128), :] = part.reshape(128, width)
-
-    spots = [
-        (row, s, col)
-        for row in range(0, e_ref.shape[0], 512)
-        for s in range(STEPS)
-        for col in range(0, width, 256)
-    ]
-
-    def angles(row, s, col):
-        return jnp.dot(e_ref[row : row + 512, :], w_ref[s, :, col : col + 256], preferred_element_type=F32)
-
-    ahead = [angles(*spot) for spot in spots[:1]]
-    for index, (row, s, col) in enumerate(spots):
-        if index + 1 < len(spots):
-            ahead.append(angles(*spots[index + 1]))
-        angle = ahead.pop(0) + shift_ref[s : s + 1, col : col + 256]
-        f_ref[row : row + 512, s * width + col : s * width + col + 256] = cosine(angle, scale).astype(BF)
-    lane = lax.axis_index("x") * 128
+                part = pieces[shift * 2 + other][s * 16 : s * 16 + 16, :, :]
+                w_ref[pl.ds(at, 128), :] = part.reshape(128, width)
+
+    cols = range(0, width, 256)
+    rows = e_ref.shape[0]
+    ahead = [jnp.dot(e_ref[...], w_ref[:, col : col + 256], preferred_element_type=F32) for col in cols]
+    for col, angle in zip(cols, ahead):
+        angle = angle + shift_ref[s : s + 1, col : col + 256]
+        f_ref[:, col : col + 256] = cosine(angle, scale).astype(BF)
+    lane = pl.multiple_of(lax.axis_index("x") * 128, 128)
     upper, lower = split_two(r_ref[...].T)
-    left = [upper, lower]
-    for s in range(STEPS):
-        left.append(f_ref[:, pl.ds(pl.multiple_of(s * width + lane, 128), 128)].T)
-    rows = e_ref.shape[0]
     here = pl.multiple_of(step * rows, rows)
-    left_ref[:, pl.ds(here, rows)] = jnp.concatenate(left, axis=0)
+    left_ref[:, pl.ds(here, rows)] = jnp.concatenate([upper, lower, f_ref[:, pl.ds(lane, 128)].T], axis=0)
     all_ref[pl.ds(here, rows), :] = f_ref[...]
 
     @pl.when(step == pl.num_programs(0) - 1)
     def _():
         half = lax.axis_index("c")
+        first = 16 if s else 8
+
+        def gram(part, row):
+            for side in range(2):
+                block = part[:, side * 128 : side * 128 + 128].reshape(16, 8, 128)
+                out_ref[side * 16 : side * 16 + 16, row : row + 8, :] = block
 
         def products(n, count):
             right = all_ref[:, n * 256 : n * 256 + 256]
             part = jnp.dot(left_ref[:count, :], right, preferred_element_type=F32)
             cross = part[0:128] + part[128:256]
-            out_ref[n * 8 : n * 8 + 8, 24:56, :] = cross.T.reshape(8, 32, 128)
+            out_ref[n * 16 : n * 16 + 16, first : first + 16, :] = cross.T.reshape(16, 16, 128)
             return part
 
-        for n in range(4):
-
-            @pl.when(half == n % 2)
+        for n in range(2):
+
+            @pl.when(half == n)
             def _():
-                part = products(n, 512)
-                for group, row in ((0, 256), (2, 384)) if n < 2 else ((1, 384),):
-                    for side in range(2):
-                        block = part[row : row + 128, side * 128 : side * 128 + 128].reshape(16, 8, 128)
-                        out_ref[side * 16 : side * 16 + 16, group * 8 : group * 8 + 8, :] = block
-
-            @pl.when(half != n % 2)
+                part = products(n, 384)
+                gram(part[256:384], 0)
+
+            @pl.when(half != n)
             def _():
                 products(n, 256)
 
-
-def features(pieces, embeddings, shifts, residuals):
+        if s:
+            right = f_before[:, pl.ds(pl.multiple_of(half * 256, 256), 256)]
+            gram(jnp.dot(left_ref[256:384, :], right, preferred_element_type=F32), 8)
+
+
+def features(s, pieces, embeddings, shifts, residuals, before=()):
     total, depth = embeddings.shape
     width = shifts.shape[1]
     tile = 512
+    count = 32 if s else 24
     whole = pl.BlockSpec(memory_space=pltpu.VMEM)
     return pl.pallas_call(
-        feature_kernel,
+        functools.partial(feature_kernel, s),
         grid=(total // tile,),
         in_specs=[whole] * 8
         + [
             pl.BlockSpec((tile, depth), lambda i: (i, 0)),
             whole,
             pl.BlockSpec((tile, 128), lambda i: (i, 0)),
-        ],
-        out_specs=[pl.BlockSpec((tile, STEPS * width), lambda i: (i, 0)), whole],
+        ]
+        + [pl.BlockSpec((total, width), lambda i: (0, 0)) for _ in before],
+        out_specs=[pl.BlockSpec((tile, width), lambda i: (i, 0)), whole],
         out_shape=[
-            jax.ShapeDtypeStruct((total, STEPS * width), BF),
-            jax.ShapeDtypeStruct((32, 56, 128), F32),
+            jax.ShapeDtypeStruct((total, width), BF),
+            jax.ShapeDtypeStruct((32, count, 128), F32),
         ],
         scratch_shapes=[
-            pltpu.VMEM((STEPS, depth, width), BF),
-            pltpu.VMEM((512, total), BF),
-            pltpu.VMEM((total, STEPS * width), BF),
+            pltpu.VMEM((depth, width), BF),
+            pltpu.VMEM((384, total), BF),
+            pltpu.VMEM((total, width), BF),
         ],
-        compiler_params=pltpu.CompilerParams(vmem_limit_bytes=52 << 20),
+        compiler_params=pltpu.CompilerParams(vmem_limit_bytes=48 << 20),
+        cost_estimate=pl.CostEstimate(flops=4 << 30, bytes_accessed=8 << 20, transcendentals=0),
         name="features",
-    )(*pieces, embeddings, shifts, residuals)
+    )(*pieces, embeddings, shifts, residuals, *before)
 
 
 def times(upper, lower, values):
@@ -272,21 +269,26 @@
     lax.while_loop(open_still, body, (jnp.int32(0), jnp.float32(1.0), size))
 
 
-def solve_kernel(ridge, *refs):
+def solve_kernel(s, ridge, *refs):
     pieces = refs[:8]
-    cross_ref, old_ref, f_hbm, r_hbm, coef_ref, out_ref, upper, lower, f_ref, r_ref, x_ref, res_ref, p_ref, ap_ref, parts_ref, delta_ref, sems = refs[8:]
+    got_ref, old_ref, f_hbm, r_hbm = refs[8:12]
+    refs = refs[12:]
+    if s:
+        before_ref, refs = refs[0], refs[1:]
+    out_ref, delta_out, upper, lower, f_ref, r_ref, x_ref, res_ref, p_ref, ap_ref, parts_ref, sems = refs
     loads = [
         pltpu.make_async_copy(f_hbm, f_ref, sems.at[0]),
         pltpu.make_async_copy(r_hbm, r_ref, sems.at[1]),
     ]
     for load in loads:
         load.start()
+    grams = s + 1
     for shift in range(4):
         for other in range(2):
             ref = pieces[shift * 2 + other]
             px, pc = offsets(shift, other)
             row = pl.multiple_of(px * 128, 128)
-            for group in range(3):
+            for group in range(grams):
                 for side in range(2):
                     lanes = pl.ds(pl.multiple_of(pc * 256 + side * 128, 128), 128)
                     block = ref[side * 16 : side * 16 + 16, group * 8 : group * 8 + 8, :].reshape(128, 128)
@@ -294,23 +296,19 @@
                     upper[group, pl.ds(row, 128), lanes] = high
                     lower[group, pl.ds(row, 128), lanes] = low
     n = upper.shape[1]
-    per = 32 // STEPS
-    work = (x_ref, res_ref, p_ref, ap_ref, parts_ref)
-    res_ref[...] = cross_ref[:per].reshape(n, 128) - ridge * old_ref[0]
-    conjugate_gradients(upper.at[0], lower.at[0], *work, ridge)
-    first = x_ref[...]
-    coef_ref[0] = old_ref[0] + first
-    res_ref[...] = cross_ref[per:].reshape(n, 128) - ridge * old_ref[1] - times(upper[2], lower[2], first)
-    high_first, low_first = split_two(first)
-    delta_ref[:n, :128] = high_first
-    delta_ref[:n, 128:] = low_first
-    conjugate_gradients(upper.at[1], lower.at[1], *work, ridge)
-    second = x_ref[...]
-    coef_ref[1] = old_ref[1] + second
-    high, low = split_two(second)
-    delta_ref[n:, :128] = high
-    delta_ref[n:, 128:] = low
-    delta = delta_ref[...]
+    cross = got_ref[:, grams * 8 : grams * 8 + 16, :].reshape(n, 128) - ridge * old_ref[s]
+    if s:
+        cross = cross - times(upper[1], lower[1], before_ref[...])
+    res_ref[...] = cross
+    conjugate_gradients(upper.at[0], lower.at[0], x_ref, res_ref, p_ref, ap_ref, parts_ref, ridge)
+    change = x_ref[...]
+    if s:
+        delta_out[0] = old_ref[0] + before_ref[...]
+        delta_out[1] = old_ref[1] + change
+    else:
+        delta_out[...] = change
+    high, low = split_two(change)
+    delta = jnp.concatenate([high, low], axis=1)
     tile = 256
     for load in loads:
         load.wait()
@@ -319,22 +317,21 @@
         out_ref[row : row + tile, :] = r_ref[row : row + tile, :] - both[:, :128] - both[:, 128:]
 
 
-def solve(pieces, cross, old, feats, residuals, ridge):
+def solve(s, pieces, got, old, feats, residuals, ridge, before=()):
     def full(array):
         return pl.BlockSpec(array.shape, lambda: (0,) * array.ndim)
 
+    second = jax.ShapeDtypeStruct(old.shape if s else old.shape[1:], F32)
     return pl.pallas_call(
-        functools.partial(solve_kernel, ridge),
+        functools.partial(solve_kernel, s, ridge),
         in_specs=[full(piece) for piece in pieces]
-        + [full(cross), full(old), pl.BlockSpec(memory_space=pl.ANY), pl.BlockSpec(memory_space=pl.ANY)],
-        out_specs=[full(old), full(residuals)],
-        out_shape=[
-            jax.ShapeDtypeStruct(old.shape, F32),
-            jax.ShapeDtypeStruct(residuals.shape, F32),
-        ],
+        + [full(got), full(old), pl.BlockSpec(memory_space=pl.ANY), pl.BlockSpec(memory_space=pl.ANY)]
+        + [full(array) for array in before],
+        out_specs=[full(residuals), full(second)],
+        out_shape=[jax.ShapeDtypeStruct(residuals.shape, F32), second],
         scratch_shapes=[
-            pltpu.VMEM((3, 512, 512), BF),
-            pltpu.VMEM((3, 512, 512), BF),
+            pltpu.VMEM((s + 1, 512, 512), BF),
+            pltpu.VMEM((s + 1, 512, 512), BF),
             pltpu.VMEM(feats.shape, BF),
             pltpu.VMEM(residuals.shape, F32),
             pltpu.VMEM((512, 128), F32),
@@ -342,12 +339,12 @@
             pltpu.VMEM((512, 128), F32),
             pltpu.VMEM((512, 128), F32),
             pltpu.VMEM((512, 256), BF),
-            pltpu.VMEM((1024, 256), BF),
             pltpu.SemaphoreType.DMA((2,)),
         ],
-        compiler_params=pltpu.CompilerParams(vmem_limit_bytes=52 << 20),
+        compiler_params=pltpu.CompilerParams(vmem_limit_bytes=48 << 20),
+        cost_estimate=pl.CostEstimate(flops=8 << 30, bytes_accessed=8 << 20, transcendentals=0),
         name="solve",
-    )(*pieces, cross, old, feats, residuals)
+    )(*pieces, got, old, feats, residuals, *before)
 
 
 def exchange(values, axes):
@@ -377,14 +374,13 @@
     got = exchange(payload(block_order, projections, phases, nrows), ROWS)
     copies, shifts = pick(block_order, got, local_blocks)
     weights = spread(exchange(copies, ROWS))
-    feats, parts = features(weights, embeddings, shifts, residuals)
-
-    summed = jnp.sum(exchange(parts, ROWS), axis=0)
-    grams = gather(summed[:24], ROWS, nrows)
-    cross, grams = lax.optimization_barrier((summed[24:], grams))
-    pieces = spread(grams)
-    cross = gather(cross, ROWS, nrows)
-    coef, current = solve(pieces, cross, old_coef, feats, residuals, ridge)
+    feats_a, parts_a = features(0, weights, embeddings, shifts, residuals)
+    feats_b, parts_b = features(1, weights, embeddings, shifts, residuals, (feats_a,))
+
+    got_a = gather(jnp.sum(exchange(parts_a, ROWS), axis=0), ROWS, nrows)
+    got_b = gather(jnp.sum(exchange(parts_b, ROWS), axis=0), ROWS, nrows)
+    current, change = solve(0, spread(got_a[:, :8]), got_a, old_coef, feats_a, residuals, ridge)
+    current, coef = solve(1, spread(got_b[:, :16]), got_b, old_coef, feats_b, current, ridge, (change,))
     return current, coef
 
 

time: 187 us -> 201 us (1.075); the launches traced: 191 us -> 202 us
  blocking collectives: 69.3 us -> 40.1 us
  starting transfers between devices: 40.9 us -> 61.5 us
  waiting for transfers between devices: 25.5 us -> 42 us
  Pallas kernels: 50 us -> 52.5 us
    all_to_all x3 -> x2, blocking collectives: 69.3 us -> 40.1 us  [exchange(): return lax.all_to_all(values, axes, split_axis=0, concat_axis=0, tiled=True)]
    all_to_all x2 -> x4, waiting for transfers between devices: 12.9 us -> 39.6 us  [exchange(): return lax.all_to_all(values, axes, split_axis=0, concat_axis=0, tiled=True)]
    all_to_all x2 -> x4, starting transfers between devices: 11.5 us -> 23 us  [exchange(): return lax.all_to_all(values, axes, split_axis=0, concat_axis=0, tiled=True)]
    ppermute x6 -> x9, waiting for transfers between devices: 10.9 us -> 0.02 us  [spread(): lax.ppermute(values, 'x', [(i, (i + shift) % nx) for i in range(nx)])]
    ppermute x6 -> x9, starting transfers between devices: 5.15 us -> 12.6 us  [spread(): lax.ppermute(values, 'x', [(i, (i + shift) % nx) for i in range(nx)])]
    pallas_call x2 -> x4, Pallas kernels: 45.9 us -> 48.3 us  [the longest x2 31.1 us: solve(): pl.pallas_call(functools.partial(solve_kernel, s, ridge), in_specs=[full(...]
    ppermute x8 -> x12, starting transfers between devices: 24.2 us -> 26 us  [spread(): lax.ppermute(value, 'c', [(i, (i + 1) % nc) for i in range(nc)])]
  transfers between devices with their start and end apart: 16 -> 25, of which waited for: 7 -> 7; matrix products, arithmetic and copies ran while one was open for 0% -> 0% of each run, Pallas kernels for 0% -> 12%
where the time goes in v4:
time: 201 us; the launch traced here: 202 us
  starting transfers between devices  61.5 us (31%)
  Pallas kernels  52.5 us (26%)
  waiting for transfers between devices  42 us (21%)
  blocking collectives  40.1 us (20%)
  local copies, waits for them, and re-layouts  5.02 us (2%)
    all_to_all x2, blocking collectives, exchange(): return lax.all_to_all(values, axes, split_axis=0, concat_axis=0, tiled=True)  40.1 us
    all_to_all x4, waiting for transfers between devices, exchange(): return lax.all_to_all(values, axes, split_axis=0, concat_axis=0, tiled=True)  39.6 us
    pallas_call x2, Pallas kernels, solve(): pl.pallas_call(functools.partial(solve_kernel, s, ridge), in_specs=[full(...  31.1 us
    ppermute x12, starting transfers between devices, spread(): lax.ppermute(value, 'c', [(i, (i + 1) % nc) for i in range(nc)])  26 us
    all_to_all x4, starting transfers between devices, exchange(): return lax.all_to_all(values, axes, split_axis=0, concat_axis=0, tiled=True)  23 us
    pallas_call x2, Pallas kernels, features(): pl.pallas_call(functools.partial(feature_kernel, s), grid=(total // tile,...  17.1 us
    ppermute x9, starting transfers between devices, spread(): lax.ppermute(values, 'x', [(i, (i + shift) % nx) for i in range(nx)])  12.6 us
  transfers between devices with their start and end apart: 25, of which 7 were waited for; matrix products, arithmetic and copies ran while one was open for 0% of the time, Pallas kernels for 12%

profile of v4, /device:TPU:1, one launch (start us, length us, event | category | flops | bytes accessed | tf_op | source)
XLA Modules:
  0.0 202.2 jit_solution(6308104690528872739)
XLA Ops:
  0.6 2.5 %payload.1 = bf16[32,8,640]{2,1,0:T(8,128)(2,1)} custom-call(s32[2]{0:T(128)} %order.3, bf16[2,1024,512]{2,1,0:T(8,128)(2,1)} %proj_ref.1, bf16[2,512]{1,0:T(2,128)(2,1)} %phase_ref.1), custom_call_target="tpu_custom_call" | custom-call | tf_op jit(solution)/shard_map/payload/pallas_call | solution.py:67
  3.1 24.8 %all_to_all.30.got_ref = bf16[32,8,640]{2,1,0:T(8,128)(2,1)} all-to-all(bf16[32,8,640]{2,1,0:T(8,128)(2,1)} %payload.1), channel_id=1, replica_groups=mesh['z'=8,'y'=4,'x'=4,'c'=2] {'z','y'}, dimensions={0} | all-to-all | bytes 655360 | tf_op jit(solution)/shard_map/all_to_all | solution.py:351
  27.9 1.7 pick.1
  29.6 15.3 %all_to_all.31.refs_0_ = bf16[32,8,512]{2,1,0:T(8,128)(2,1)S(1)} all-to-all(bf16[32,8,512]{2,1,0:T(8,128)(2,1)} %get-tuple-element.10), channel_id=1, replica_groups=mesh['z'=8,'y'=4,'x'=4,'c'=2] {'z','y'}, dimensions={0} | all-to-all | bytes 524288 | tf_op jit(solution)/shard_map/all_to_all | solution.py:351
  44.9 1.2 collective-permute-start.1
  46.1 2.5 %collective-permute-start.3 = (bf16[32,8,512]{2,1,0:T(8,128)(2,1)S(1)}, bf16[32,8,512]{2,1,0:T(8,128)(2,1)S(1)}, u32[]{:S(2)}, u32[]{:S(2)}) collective-permute-start(bf16[32,8,512]{2,1,0:T(8,128)(2,1)S(1)} %all_to_all.31.refs_0_), channel_id=1, source_target_pairs={{0,4},{2,6},{4,0},{6,2},{1,5},{3,7},{5,1},{7,3},{8,12},{10,14},{12... | collective-permute-start | bytes 786440 | tf_op jit(solution)/shard_map/ppermute | solution.py:362
  48.6 1.2 collective-permute-start.5
  49.7 4.3 %collective-permute-start = (bf16[32,8,512]{2,1,0:T(8,128)(2,1)S(1)}, bf16[32,8,512]{2,1,0:T(8,128)(2,1)S(1)}, u32[]{:S(2)}, u32[]{:S(2)}) collective-permute-start(bf16[32,8,512]{2,1,0:T(8,128)(2,1)S(1)} %all_to_all.31.refs_0_), channel_id=1, source_target_pairs={{0,1},{1,0},{2,3},{3,2},{4,5},{5,4},{6,7},{7,6},{8,9},{9,8},{10,11... | collective-permute-start | bytes 786440 | tf_op jit(solution)/shard_map/ppermute | solution.py:365
  54.1 0.0 collective-permute-done.1.refs_2_
  54.1 4.6 %collective-permute-start.2 = (bf16[32,8,512]{2,1,0:T(8,128)(2,1)S(1)}, bf16[32,8,512]{2,1,0:T(8,128)(2,1)S(1)}, u32[]{:S(2)}, u32[]{:S(2)}) collective-permute-start(bf16[32,8,512]{2,1,0:T(8,128)(2,1)S(1)} %collective-permute-done.1.refs_2_), channel_id=1, source_target_pairs={{0,1},{1,0},{2,3},{3,2},{4,5},{5,4},{6,7},{7,6},{8,9},{9,8},{10,11... | collective-permute-start | bytes 786440 | tf_op jit(solution)/shard_map/ppermute | solution.py:365
  58.7 0.0 collective-permute-done.3.refs_4_
  58.7 2.8 %collective-permute-start.4 = (bf16[32,8,512]{2,1,0:T(8,128)(2,1)S(1)}, bf16[32,8,512]{2,1,0:T(8,128)(2,1)S(1)}, u32[]{:S(2)}, u32[]{:S(2)}) collective-permute-start(bf16[32,8,512]{2,1,0:T(8,128)(2,1)S(1)} %collective-permute-done.3.refs_4_), channel_id=1, source_target_pairs={{0,1},{1,0},{2,3},{3,2},{4,5},{5,4},{6,7},{7,6},{8,9},{9,8},{10,11... | collective-permute-start | bytes 786440 | tf_op jit(solution)/shard_map/ppermute | solution.py:365
  61.5 0.0 collective-permute-done.5.refs_6_
  61.5 0.0 collective-permute-start.6
  61.5 0.0 collective-permute-done.refs_1_
  61.5 0.0 collective-permute-done.2.refs_3_
  61.5 1.1 collective-permute-done.4.refs_5_
  62.6 0.4 collective-permute-done.6.refs_7_
  63.0 0.7 copy-done.2
  63.7 8.0 %features.2 = (bf16[2048,512]{1,0:T(8,128)(2,1)S(1)}, f32[32,24,128]{2,1,0:T(8,128)}) custom-call(bf16[32,8,512]{2,1,0:T(8,128)(2,1)S(1)} %all_to_all.31.refs_0_, bf16[32,8,512]{2,1,0:T(8,128)(2,1)S(1)} %collective-permute-done.refs_1_, bf16[32,8,512]{2,1,0:T(8,128)(2,1)S(1)} %collective-permute-done.1.refs_2_, ...), custom_call_target="tpu_custom_call" | custom-call | flops 4294967296 | bytes 8388608 | tf_op jit(solution)/shard_map/features/pallas_call | solution.py:174
  71.7 1.4 copy-done.5
  73.1 5.2 %all-to-all-start.4 = ((f32[32,24,128]{2,1,0:T(8,128)}), f32[32,24,128]{2,1,0:T(8,128)S(1)}, u32[]{:S(2)}, u32[]{:S(2)}) async-start(f32[32,24,128]{2,1,0:T(8,128)} %get-tuple-element.15), calls=%async_computation.4 | async-start | bytes 786432 | tf_op jit(solution)/shard_map/all_to_all | solution.py:351
  78.3 9.1 %features.3 = (bf16[2048,512]{1,0:T(8,128)(2,1)S(1)}, f32[32,32,128]{2,1,0:T(8,128)}) custom-call(bf16[32,8,512]{2,1,0:T(8,128)(2,1)S(1)} %all_to_all.31.refs_0_, bf16[32,8,512]{2,1,0:T(8,128)(2,1)S(1)} %collective-permute-done.refs_1_, bf16[32,8,512]{2,1,0:T(8,128)(2,1)S(1)} %collective-permute-done.1.refs_2_, ...), custom_call_target="tpu_custom_call" | custom-call | flops 4294967296 | bytes 8388608 | tf_op jit(solution)/shard_map/features/pallas_call | solution.py:174
  87.4 1.3 copy-done.4
  88.7 3.4 %all-to-all-done.4 = f32[32,24,128]{2,1,0:T(8,128)S(1)} async-done(((f32[32,24,128]{2,1,0:T(8,128)}), f32[32,24,128]{2,1,0:T(8,128)S(1)}, u32[]{:S(2)}, u32[]{:S(2)}) %all-to-all-start.4) | async-done | bytes 393248 | tf_op jit(solution)/shard_map/all_to_all | solution.py:351
  92.2 5.8 %all-to-all-start.2 = ((f32[32,32,128]{2,1,0:T(8,128)}), f32[32,32,128]{2,1,0:T(8,128)S(1)}, u32[]{:S(2)}, u32[]{:S(2)}) async-start(f32[32,32,128]{2,1,0:T(8,128)} %get-tuple-element.13), calls=%async_computation.2 | async-start | bytes 1048576 | tf_op jit(solution)/shard_map/all_to_all | solution.py:351
  98.0 0.0 copy-start.1
  98.0 15.4 %all-to-all-done.2 = f32[32,32,128]{2,1,0:T(8,128)S(1)} async-done(((f32[32,32,128]{2,1,0:T(8,128)}), f32[32,32,128]{2,1,0:T(8,128)S(1)}, u32[]{:S(2)}, u32[]{:S(2)}) %all-to-all-start.2) | async-done | bytes 524320 | tf_op jit(solution)/shard_map/all_to_all | solution.py:351
  113.4 0.8 broadcast_in_dim.5
  114.2 6.1 %all-to-all-start.5 = ((f32[32,24,128]{2,1,0:T(8,128)}), f32[32,24,128]{2,1,0:T(8,128)S(1)}, u32[]{:S(2)}, u32[]{:S(2)}) async-start(f32[32,24,128]{2,1,0:T(8,128)} %broadcast_in_dim.5), calls=%async_computation.5 | async-start | bytes 786432 | tf_op jit(solution)/shard_map/all_to_all | solution.py:351
  120.3 12.8 %all-to-all-done.5.refs_8_ = f32[32,24,128]{2,1,0:T(8,128)S(1)} async-done(((f32[32,24,128]{2,1,0:T(8,128)}), f32[32,24,128]{2,1,0:T(8,128)S(1)}, u32[]{:S(2)}, u32[]{:S(2)}) %all-to-all-start.5) | async-done | bytes 393248 | tf_op jit(solution)/shard_map/all_to_all | solution.py:351
  133.1 0.9 broadcast_in_dim.4
  134.0 5.8 %all-to-all-start.3 = ((f32[32,32,128]{2,1,0:T(8,128)}), f32[32,32,128]{2,1,0:T(8,128)S(1)}, u32[]{:S(2)}, u32[]{:S(2)}) async-start(f32[32,32,128]{2,1,0:T(8,128)} %broadcast_in_dim.4), calls=%async_computation.3 | async-start | bytes 1048576 | tf_op jit(solution)/shard_map/all_to_all | solution.py:351
  139.9 0.8 collective-permute-start.15
  140.6 2.1 %collective-permute-start.17 = (f32[32,8,128]{2,1,0:T(8,128)S(1)}, f32[32,8,128]{2,1,0:T(8,128)S(1)}, u32[]{:S(2)}, u32[]{:S(2)}) collective-permute-start(f32[32,8,128]{2,1,0:T(8,128)S(1)} %slice.9.refs_0_), channel_id=1, source_target_pairs={{0,4},{2,6},{4,0},{6,2},{1,5},{3,7},{5,1},{7,3},{8,12},{10,14},{12... | collective-permute-start | bytes 393224 | tf_op jit(solution)/shard_map/ppermute | solution.py:362
  142.8 1.3 collective-permute-start.19
  144.0 2.9 %collective-permute-start.14 = (f32[32,8,128]{2,1,0:T(8,128)S(1)}, f32[32,8,128]{2,1,0:T(8,128)S(1)}, u32[]{:S(2)}, u32[]{:S(2)}) collective-permute-start(f32[32,8,128]{2,1,0:T(8,128)S(1)} %slice.9.refs_0_), channel_id=1, source_target_pairs={{0,1},{1,0},{2,3},{3,2},{4,5},{5,4},{6,7},{7,6},{8,9},{9,8},{10,11... | collective-permute-start | bytes 393224 | tf_op jit(solution)/shard_map/ppermute | solution.py:365
  146.9 8.0 %all-to-all-done.3.refs_8_ = f32[32,32,128]{2,1,0:T(8,128)S(1)} async-done(((f32[32,32,128]{2,1,0:T(8,128)}), f32[32,32,128]{2,1,0:T(8,128)S(1)}, u32[]{:S(2)}, u32[]{:S(2)}) %all-to-all-start.3) | async-done | bytes 524320 | tf_op jit(solution)/shard_map/all_to_all | solution.py:351
  154.9 2.1 %collective-permute-start.10 = (f32[32,16,128]{2,1,0:T(8,128)S(1)}, f32[32,16,128]{2,1,0:T(8,128)S(1)}, u32[]{:S(2)}, u32[]{:S(2)}) collective-permute-start(f32[32,16,128]{2,1,0:T(8,128)S(1)} %slice.8.refs_0_), channel_id=1, source_target_pairs={{0,4},{2,6},{4,0},{6,2},{1,5},{3,7},{5,1},{7,3},{8,12},{10,14},{12... | collective-permute-start | bytes 786440 | tf_op jit(solution)/shard_map/ppermute | solution.py:362
  157.0 0.0 collective-permute-done.15.refs_2_
  157.0 1.0 collective-permute-start.12
  158.1 0.0 collective-permute-done.17.refs_4_
  158.1 0.4 collective-permute-start.8
  158.5 0.0 collective-permute-done.19.refs_6_
  158.5 4.6 %collective-permute-start.16 = (f32[32,8,128]{2,1,0:T(8,128)S(1)}, f32[32,8,128]{2,1,0:T(8,128)S(1)}, u32[]{:S(2)}, u32[]{:S(2)}) collective-permute-start(f32[32,8,128]{2,1,0:T(8,128)S(1)} %collective-permute-done.15.refs_2_), channel_id=1, source_target_pairs={{0,1},{1,0},{2,3},{3,2},{4,5},{5,4},{6,7},{7,6},{8,9},{9,8},{10,11... | collective-permute-start | bytes 393224 | tf_op jit(solution)/shard_map/ppermute | solution.py:365
  163.1 0.0 collective-permute-done.14.refs_1_
  163.1 0.1 collective-permute-start.18
  163.2 0.9 collective-permute-done.16.refs_3_
  164.1 0.4 collective-permute-start.20
  164.5 0.0 collective-permute-done.18.refs_5_
  164.5 0.2 collective-permute-start.7
  164.6 0.0 collective-permute-done.10.refs_4_
  164.7 3.5 %collective-permute-start.11 = (f32[32,16,128]{2,1,0:T(8,128)S(1)}, f32[32,16,128]{2,1,0:T(8,128)S(1)}, u32[]{:S(2)}, u32[]{:S(2)}) collective-permute-start(f32[32,16,128]{2,1,0:T(8,128)S(1)} %collective-permute-done.10.refs_4_), channel_id=1, source_target_pairs={{0,1},{1,0},{2,3},{3,2},{4,5},{5,4},{6,7},{7,6},{8,9},{9,8},{10,11... | collective-permute-start | bytes 786440 | tf_op jit(solution)/shard_map/ppermute | solution.py:365
  168.1 0.0 collective-permute-done.12.refs_6_
  168.1 2.0 collective-permute-start.13
  170.1 0.0 collective-permute-done.8.refs_2_
  170.1 0.7 collective-permute-start.9
  170.8 0.0 collective-permute-done.20.refs_7_
  170.8 14.8 %solve.2 = (f32[2048,128]{1,0:T(8,128)S(1)}, f32[512,128]{1,0:T(8,128)S(1)}) custom-call(f32[32,8,128]{2,1,0:T(8,128)S(1)} %slice.9.refs_0_, f32[32,8,128]{2,1,0:T(8,128)S(1)} %collective-permute-done.14.refs_1_, f32[32,8,128]{2,1,0:T(8,128)S(1)} %collective-permute-done.15.refs_2_, f32[32,8,128]{2,1,0:T(8,128)S(1)} %collective-permute-done.16.refs_3_, ...), custom_call_target="tpu_custom_call" | custom-call | flops 8589934592 | bytes 8388608 | tf_op jit(solution)/shard_map/solve/pallas_call | solution.py:325
  185.7 0.0 collective-permute-done.7.refs_1_
  185.7 0.0 collective-permute-done.11.refs_5_
  185.7 0.0 collective-permute-done.13.refs_7_
  185.7 0.0 collective-permute-done.9.refs_3_
  185.7 16.3 %solve.3 = (f32[2048,128]{1,0:T(8,128)}, f32[2,512,128]{2,1,0:T(8,128)}) custom-call(f32[32,16,128]{2,1,0:T(8,128)S(1)} %slice.8.refs_0_, f32[32,16,128]{2,1,0:T(8,128)S(1)} %collective-permute-done.7.refs_1_, f32[32,16,128]{2,1,0:T(8,128)S(1)} %collective-permute-done.8.refs_2_, f32[32,16,128]{2,1,0:T(8,128)S(1)} %collective-permute-done.9.refs_3_, ...), custom_call_target="tpu_custom_call" | custom-call | flops 8589934592 | bytes 8388608 | tf_op jit(solution)/shard_map/solve/pallas_call | solution.py:325
  (12 shorter events, 0.1 us)
Async XLA Ops:
  0.6 62.4 %copy-start = (f32[2048,128]{1,0:T(8,128)S(1)}, f32[2048,128]{1,0:T(8,128)}, u32[]{:S(2)}) copy-start(f32[2048,128]{1,0:T(8,128)} %refs_11_.1) | copy-start | bytes 3145732
  44.9 9.2 %collective-permute-start.1 = (bf16[32,8,512]{2,1,0:T(8,128)(2,1)S(1)}, bf16[32,8,512]{2,1,0:T(8,128)(2,1)S(1)}, u32[]{:S(2)}, u32[]{:S(2)}) collective-permute-start(bf16[32,8,512]{2,1,0:T(8,128)(2,1)S(1)} %all_to_all.31.refs_0_), channel_id=1, source_target_pairs={{0,2},{2,4},{4,6},{6,0},{1,3},{3,5},{5,7},{7,1},{8,10},{10,12},{12... | collective-permute-start | bytes 786440 | tf_op jit(solution)/shard_map/ppermute | solution.py:362
  46.1 12.5 %collective-permute-start.3 = (bf16[32,8,512]{2,1,0:T(8,128)(2,1)S(1)}, bf16[32,8,512]{2,1,0:T(8,128)(2,1)S(1)}, u32[]{:S(2)}, u32[]{:S(2)}) collective-permute-start(bf16[32,8,512]{2,1,0:T(8,128)(2,1)S(1)} %all_to_all.31.refs_0_), channel_id=1, source_target_pairs={{0,4},{2,6},{4,0},{6,2},{1,5},{3,7},{5,1},{7,3},{8,12},{10,14},{12... | collective-permute-start | bytes 786440 | tf_op jit(solution)/shard_map/ppermute | solution.py:362
  48.6 12.9 %collective-permute-start.5 = (bf16[32,8,512]{2,1,0:T(8,128)(2,1)S(1)}, bf16[32,8,512]{2,1,0:T(8,128)(2,1)S(1)}, u32[]{:S(2)}, u32[]{:S(2)}) collective-permute-start(bf16[32,8,512]{2,1,0:T(8,128)(2,1)S(1)} %all_to_all.31.refs_0_), channel_id=1, source_target_pairs={{0,6},{2,0},{4,2},{6,4},{1,7},{3,1},{5,3},{7,5},{8,14},{10,8},{12,... | collective-permute-start | bytes 786440 | tf_op jit(solution)/shard_map/ppermute | solution.py:362
  49.7 11.7 %collective-permute-start = (bf16[32,8,512]{2,1,0:T(8,128)(2,1)S(1)}, bf16[32,8,512]{2,1,0:T(8,128)(2,1)S(1)}, u32[]{:S(2)}, u32[]{:S(2)}) collective-permute-start(bf16[32,8,512]{2,1,0:T(8,128)(2,1)S(1)} %all_to_all.31.refs_0_), channel_id=1, source_target_pairs={{0,1},{1,0},{2,3},{3,2},{4,5},{5,4},{6,7},{7,6},{8,9},{9,8},{10,11... | collective-permute-start | bytes 786440 | tf_op jit(solution)/shard_map/ppermute | solution.py:365
  54.1 7.4 %collective-permute-start.2 = (bf16[32,8,512]{2,1,0:T(8,128)(2,1)S(1)}, bf16[32,8,512]{2,1,0:T(8,128)(2,1)S(1)}, u32[]{:S(2)}, u32[]{:S(2)}) collective-permute-start(bf16[32,8,512]{2,1,0:T(8,128)(2,1)S(1)} %collective-permute-done.1.refs_2_), channel_id=1, source_target_pairs={{0,1},{1,0},{2,3},{3,2},{4,5},{5,4},{6,7},{7,6},{8,9},{9,8},{10,11... | collective-permute-start | bytes 786440 | tf_op jit(solution)/shard_map/ppermute | solution.py:365
  58.7 4.0 %collective-permute-start.4 = (bf16[32,8,512]{2,1,0:T(8,128)(2,1)S(1)}, bf16[32,8,512]{2,1,0:T(8,128)(2,1)S(1)}, u32[]{:S(2)}, u32[]{:S(2)}) collective-permute-start(bf16[32,8,512]{2,1,0:T(8,128)(2,1)S(1)} %collective-permute-done.3.refs_4_), channel_id=1, source_target_pairs={{0,1},{1,0},{2,3},{3,2},{4,5},{5,4},{6,7},{7,6},{8,9},{9,8},{10,11... | collective-permute-start | bytes 786440 | tf_op jit(solution)/shard_map/ppermute | solution.py:365
  61.5 1.5 collective-permute-start.6
  63.0 0.7 copy-start.2
  63.7 14.6 %copy-start.3 = (f32[2,512]{1,0:T(2,128)S(1)}, f32[2,512]{1,0:T(2,128)}, u32[]{:S(2)}) copy-start(f32[2,512]{1,0:T(2,128)} %get-tuple-element.11.refs_9_) | copy-start | bytes 12292
  71.7 1.4 copy-start.5
  73.1 19.1 %all-to-all-start.4 = ((f32[32,24,128]{2,1,0:T(8,128)}), f32[32,24,128]{2,1,0:T(8,128)S(1)}, u32[]{:S(2)}, u32[]{:S(2)}) async-start(f32[32,24,128]{2,1,0:T(8,128)} %get-tuple-element.15), calls=%async_computation.4 | async-start | bytes 786432 | tf_op jit(solution)/shard_map/all_to_all | solution.py:351
  87.4 1.3 copy-start.4
  92.2 21.2 %all-to-all-start.2 = ((f32[32,32,128]{2,1,0:T(8,128)}), f32[32,32,128]{2,1,0:T(8,128)S(1)}, u32[]{:S(2)}, u32[]{:S(2)}) async-start(f32[32,32,128]{2,1,0:T(8,128)} %get-tuple-element.13), calls=%async_computation.2 | async-start | bytes 1048576 | tf_op jit(solution)/shard_map/all_to_all | solution.py:351
  98.0 72.8 %copy-start.1 = (f32[2,512,128]{2,1,0:T(8,128)S(1)}, f32[2,512,128]{2,1,0:T(8,128)}, u32[]{:S(2)}) copy-start(f32[2,512,128]{2,1,0:T(8,128)} %refs_9_.3) | copy-start | bytes 1572868
  114.2 19.0 %all-to-all-start.5 = ((f32[32,24,128]{2,1,0:T(8,128)}), f32[32,24,128]{2,1,0:T(8,128)S(1)}, u32[]{:S(2)}, u32[]{:S(2)}) async-start(f32[32,24,128]{2,1,0:T(8,128)} %broadcast_in_dim.5), calls=%async_computation.5 | async-start | bytes 786432 | tf_op jit(solution)/shard_map/all_to_all | solution.py:351
  134.0 20.9 %all-to-all-start.3 = ((f32[32,32,128]{2,1,0:T(8,128)}), f32[32,32,128]{2,1,0:T(8,128)S(1)}, u32[]{:S(2)}, u32[]{:S(2)}) async-start(f32[32,32,128]{2,1,0:T(8,128)} %broadcast_in_dim.4), calls=%async_computation.3 | async-start | bytes 1048576 | tf_op jit(solution)/shard_map/all_to_all | solution.py:351
  139.9 17.2 %collective-permute-start.15 = (f32[32,8,128]{2,1,0:T(8,128)S(1)}, f32[32,8,128]{2,1,0:T(8,128)S(1)}, u32[]{:S(2)}, u32[]{:S(2)}) collective-permute-start(f32[32,8,128]{2,1,0:T(8,128)S(1)} %slice.9.refs_0_), channel_id=1, source_target_pairs={{0,2},{2,4},{4,6},{6,0},{1,3},{3,5},{5,7},{7,1},{8,10},{10,12},{12... | collective-permute-start | bytes 393224 | tf_op jit(solution)/shard_map/ppermute | solution.py:362
  140.6 17.5 %collective-permute-start.17 = (f32[32,8,128]{2,1,0:T(8,128)S(1)}, f32[32,8,128]{2,1,0:T(8,128)S(1)}, u32[]{:S(2)}, u32[]{:S(2)}) collective-permute-start(f32[32,8,128]{2,1,0:T(8,128)S(1)} %slice.9.refs_0_), channel_id=1, source_target_pairs={{0,4},{2,6},{4,0},{6,2},{1,5},{3,7},{5,1},{7,3},{8,12},{10,14},{12... | collective-permute-start | bytes 393224 | tf_op jit(solution)/shard_map/ppermute | solution.py:362
  142.8 15.7 %collective-permute-start.19 = (f32[32,8,128]{2,1,0:T(8,128)S(1)}, f32[32,8,128]{2,1,0:T(8,128)S(1)}, u32[]{:S(2)}, u32[]{:S(2)}) collective-permute-start(f32[32,8,128]{2,1,0:T(8,128)S(1)} %slice.9.refs_0_), channel_id=1, source_target_pairs={{0,6},{2,0},{4,2},{6,4},{1,7},{3,1},{5,3},{7,5},{8,14},{10,8},{12,... | collective-permute-start | bytes 393224 | tf_op jit(solution)/shard_map/ppermute | solution.py:362
  144.0 19.1 %collective-permute-start.14 = (f32[32,8,128]{2,1,0:T(8,128)S(1)}, f32[32,8,128]{2,1,0:T(8,128)S(1)}, u32[]{:S(2)}, u32[]{:S(2)}) collective-permute-start(f32[32,8,128]{2,1,0:T(8,128)S(1)} %slice.9.refs_0_), channel_id=1, source_target_pairs={{0,1},{1,0},{2,3},{3,2},{4,5},{5,4},{6,7},{7,6},{8,9},{9,8},{10,11... | collective-permute-start | bytes 393224 | tf_op jit(solution)/shard_map/ppermute | solution.py:365
  154.9 9.7 %collective-permute-start.10 = (f32[32,16,128]{2,1,0:T(8,128)S(1)}, f32[32,16,128]{2,1,0:T(8,128)S(1)}, u32[]{:S(2)}, u32[]{:S(2)}) collective-permute-start(f32[32,16,128]{2,1,0:T(8,128)S(1)} %slice.8.refs_0_), channel_id=1, source_target_pairs={{0,4},{2,6},{4,0},{6,2},{1,5},{3,7},{5,1},{7,3},{8,12},{10,14},{12... | collective-permute-start | bytes 786440 | tf_op jit(solution)/shard_map/ppermute | solution.py:362
  157.0 11.1 %collective-permute-start.12 = (f32[32,16,128]{2,1,0:T(8,128)S(1)}, f32[32,16,128]{2,1,0:T(8,128)S(1)}, u32[]{:S(2)}, u32[]{:S(2)}) collective-permute-start(f32[32,16,128]{2,1,0:T(8,128)S(1)} %slice.8.refs_0_), channel_id=1, source_target_pairs={{0,6},{2,0},{4,2},{6,4},{1,7},{3,1},{5,3},{7,5},{8,14},{10,8},{12,... | collective-permute-start | bytes 786440 | tf_op jit(solution)/shard_map/ppermute | solution.py:362
  158.1 12.1 %collective-permute-start.8 = (f32[32,16,128]{2,1,0:T(8,128)S(1)}, f32[32,16,128]{2,1,0:T(8,128)S(1)}, u32[]{:S(2)}, u32[]{:S(2)}) collective-permute-start(f32[32,16,128]{2,1,0:T(8,128)S(1)} %slice.8.refs_0_), channel_id=1, source_target_pairs={{0,2},{2,4},{4,6},{6,0},{1,3},{3,5},{5,7},{7,1},{8,10},{10,12},{12... | collective-permute-start | bytes 786440 | tf_op jit(solution)/shard_map/ppermute | solution.py:362
  158.5 5.6 %collective-permute-start.16 = (f32[32,8,128]{2,1,0:T(8,128)S(1)}, f32[32,8,128]{2,1,0:T(8,128)S(1)}, u32[]{:S(2)}, u32[]{:S(2)}) collective-permute-start(f32[32,8,128]{2,1,0:T(8,128)S(1)} %collective-permute-done.15.refs_2_), channel_id=1, source_target_pairs={{0,1},{1,0},{2,3},{3,2},{4,5},{5,4},{6,7},{7,6},{8,9},{9,8},{10,11... | collective-permute-start | bytes 393224 | tf_op jit(solution)/shard_map/ppermute | solution.py:365
  163.1 1.3 collective-permute-start.18
  164.1 6.7 %collective-permute-start.20 = (f32[32,8,128]{2,1,0:T(8,128)S(1)}, f32[32,8,128]{2,1,0:T(8,128)S(1)}, u32[]{:S(2)}, u32[]{:S(2)}) collective-permute-start(f32[32,8,128]{2,1,0:T(8,128)S(1)} %collective-permute-done.19.refs_6_), channel_id=1, source_target_pairs={{0,1},{1,0},{2,3},{3,2},{4,5},{5,4},{6,7},{7,6},{8,9},{9,8},{10,11... | collective-permute-start | bytes 393224 | tf_op jit(solution)/shard_map/ppermute | solution.py:365
  164.5 21.2 %collective-permute-start.7 = (f32[32,16,128]{2,1,0:T(8,128)S(1)}, f32[32,16,128]{2,1,0:T(8,128)S(1)}, u32[]{:S(2)}, u32[]{:S(2)}) collective-permute-start(f32[32,16,128]{2,1,0:T(8,128)S(1)} %slice.8.refs_0_), channel_id=1, source_target_pairs={{0,1},{1,0},{2,3},{3,2},{4,5},{5,4},{6,7},{7,6},{8,9},{9,8},{10,11... | collective-permute-start | bytes 786440 | tf_op jit(solution)/shard_map/ppermute | solution.py:365
  164.7 21.0 %collective-permute-start.11 = (f32[32,16,128]{2,1,0:T(8,128)S(1)}, f32[32,16,128]{2,1,0:T(8,128)S(1)}, u32[]{:S(2)}, u32[]{:S(2)}) collective-permute-start(f32[32,16,128]{2,1,0:T(8,128)S(1)} %collective-permute-done.10.refs_4_), channel_id=1, source_target_pairs={{0,1},{1,0},{2,3},{3,2},{4,5},{5,4},{6,7},{7,6},{8,9},{9,8},{10,11... | collective-permute-start | bytes 786440 | tf_op jit(solution)/shard_map/ppermute | solution.py:365
  168.1 17.6 %collective-permute-start.13 = (f32[32,16,128]{2,1,0:T(8,128)S(1)}, f32[32,16,128]{2,1,0:T(8,128)S(1)}, u32[]{:S(2)}, u32[]{:S(2)}) collective-permute-start(f32[32,16,128]{2,1,0:T(8,128)S(1)} %collective-permute-done.12.refs_6_), channel_id=1, source_target_pairs={{0,1},{1,0},{2,3},{3,2},{4,5},{5,4},{6,7},{7,6},{8,9},{9,8},{10,11... | collective-permute-start | bytes 786440 | tf_op jit(solution)/shard_map/ppermute | solution.py:365
  170.1 15.6 %collective-permute-start.9 = (f32[32,16,128]{2,1,0:T(8,128)S(1)}, f32[32,16,128]{2,1,0:T(8,128)S(1)}, u32[]{:S(2)}, u32[]{:S(2)}) collective-permute-start(f32[32,16,128]{2,1,0:T(8,128)S(1)} %collective-permute-done.8.refs_2_), channel_id=1, source_target_pairs={{0,1},{1,0},{2,3},{3,2},{4,5},{5,4},{6,7},{7,6},{8,9},{9,8},{10,11... | collective-permute-start | bytes 786440 | tf_op jit(solution)/shard_map/ppermute | solution.py:365

commit v5 on v3

--- a/solution.py
+++ b/solution.py
@@ -219,7 +219,7 @@
     return jnp.sum(parts[0], axis=0, keepdims=True)
 
 
-def conjugate_gradients(upper_ref, lower_ref, x_ref, r_ref, p_ref, ap_ref, parts_ref, ridge):
+def conjugate_gradients(upper_ref, lower_ref, x_ref, r_ref, p_ref, ap_ref, v_ref, parts_ref, ridge):
     n = r_ref.shape[0]
     bound = (TOLERANCE * ridge) ** 2
     bands = [slice(row, row + 128) for row in range(0, n, 128)]
@@ -230,51 +230,66 @@
         parts_ref[band, :128] = high
         parts_ref[band, 128:] = low
 
-    def one(rr):
-        sums = []
-        for row in range(0, n, 512):
-            band = slice(row, row + 512)
-            both = jnp.dot(upper_ref[band, :], parts_ref[...], preferred_element_type=F32)
-            rest = jnp.dot(lower_ref[band, :], parts_ref[:, :128], preferred_element_type=F32)
-            p = p_ref[band]
-            ap = both[:, :128] + both[:, 128:] + rest + ridge * p
-            ap_ref[band] = ap
-            sums.append(folded(p * ap))
-        curve = total(sums)
-        alpha = jnp.where(curve > 0.0, rr / curve, 0.0)
-        sums = []
+    first = upper_ref[:, :128].astype(F32)
+    signs = jnp.where(first[:, :1] >= 0.0, 1.0, -1.0)
+    once = jnp.dot(upper_ref[...], jnp.broadcast_to(signs, (n, 128)).astype(BF), preferred_element_type=F32)
+    twice = jnp.dot(upper_ref[...], once.astype(BF), preferred_element_type=F32)
+    norm = total([folded(twice * twice)])
+    along = total([folded(once * once)])
+    top = ridge + jnp.where(along > 0.0, total([folded(once * twice)]) / along, 0.0)
+    v_ref[...] = twice * jnp.where(norm > 0.0, lax.rsqrt(norm), 0.0)
+    keep = jnp.minimum((ridge + first[:1, :1]) / top, 1.0)
+    drop = 1.0 - keep
+
+    def weighed(rr, vr):
+        return jnp.maximum(rr - drop * vr * vr, keep * rr)
+
+    def one(rz):
+        both = jnp.dot(upper_ref[...], parts_ref[...], preferred_element_type=F32)
+        rest = jnp.dot(lower_ref[...], parts_ref[:, :128], preferred_element_type=F32)
+        p = p_ref[...]
+        ap = both[:, :128] + both[:, 128:] + rest + ridge * p
+        ap_ref[...] = ap
+        curve = total([folded(p * ap)])
+        alpha = jnp.where(curve > 0.0, rz / curve, 0.0)
+        squares, shadows = [], []
         for band in bands:
             r = r_ref[band] - alpha * ap_ref[band]
             r_ref[band] = r
-            sums.append(folded(r * r))
-        new = total(sums)
-        beta = jnp.where(rr > 0.0, new / rr, 0.0)
+            squares.append(folded(r * r))
+            shadows.append(folded(v_ref[band] * r))
+        rr, vr = total(squares), total(shadows)
+        new = weighed(rr, vr)
+        beta = jnp.where(rz > 0.0, new / rz, 0.0)
+        shadow = drop * vr
         for band in bands:
             p = p_ref[band]
             x_ref[band] += alpha * p
-            direct(band, r_ref[band] + beta * p)
-        return new
+            direct(band, r_ref[band] - shadow * v_ref[band] + beta * p)
+        return rr, new
 
     def open_still(state):
         return jnp.logical_and(state[0] < MAX_LOOPS, state[1] > 0.0)
 
     def body(state):
-        rr = state[2]
+        rz = state[2]
         for _ in range(UNROLL):
-            rr = one(rr)
+            rr, rz = one(rz)
         size = total([folded(x_ref[band] * x_ref[band]) for band in bands])
-        return state[0] + 1, jnp.max(rr - bound * size), rr
-
+        return state[0] + 1, jnp.max(rr - bound * size), rz
+
+    rr = total([folded(r_ref[band] * r_ref[band]) for band in bands])
+    vr = total([folded(v_ref[band] * r_ref[band]) for band in bands])
+    shadow = drop * vr
     for band in bands:
         x_ref[band] = jnp.zeros_like(r_ref[band])
-        direct(band, r_ref[band])
-    size = total([folded(r_ref[band] * r_ref[band]) for band in bands])
-    lax.while_loop(open_still, body, (jnp.int32(0), jnp.float32(1.0), size))
+        direct(band, r_ref[band] - shadow * v_ref[band])
+    lax.while_loop(open_still, body, (jnp.int32(0), jnp.float32(1.0), weighed(rr, vr)))
 
 
 def solve_kernel(ridge, *refs):
     pieces = refs[:8]
-    cross_ref, old_ref, f_hbm, r_hbm, coef_ref, out_ref, upper, lower, f_ref, r_ref, x_ref, res_ref, p_ref, ap_ref, parts_ref, delta_ref, sems = refs[8:]
+    cross_ref, old_ref, f_hbm, r_hbm, coef_ref, out_ref, upper, lower, f_ref, r_ref, x_ref, res_ref, p_ref, ap_ref, v_ref, parts_ref, delta_ref, sems = refs[8:]
     loads = [
         pltpu.make_async_copy(f_hbm, f_ref, sems.at[0]),
         pltpu.make_async_copy(r_hbm, r_ref, sems.at[1]),
@@ -295,7 +310,7 @@
                     lower[group, pl.ds(row, 128), lanes] = low
     n = upper.shape[1]
     per = 32 // STEPS
-    work = (x_ref, res_ref, p_ref, ap_ref, parts_ref)
+    work = (x_ref, res_ref, p_ref, ap_ref, v_ref, parts_ref)
     res_ref[...] = cross_ref[:per].reshape(n, 128) - ridge * old_ref[0]
     conjugate_gradients(upper.at[0], lower.at[0], *work, ridge)
     first = x_ref[...]
@@ -341,6 +356,7 @@
             pltpu.VMEM((512, 128), F32),
             pltpu.VMEM((512, 128), F32),
             pltpu.VMEM((512, 128), F32),
+            pltpu.VMEM((512, 128), F32),
             pltpu.VMEM((512, 256), BF),
             pltpu.VMEM((1024, 256), BF),
             pltpu.SemaphoreType.DMA((2,)),

time: 187 us -> 184 us (0.984); the launches traced: 191 us -> 184 us
  Pallas kernels: 50 us -> 43.2 us
    pallas_call x1, Pallas kernels: 32 us -> 25.1 us  [solve(): pl.pallas_call(functools.partial(solve_kernel, ridge), in_specs=[full(pie...]
where the time goes in v5:
time: 184 us
  blocking collectives  69.3 us (38%)
  Pallas kernels  43.2 us (23%)
  starting transfers between devices  40.9 us (22%)
  waiting for transfers between devices  25.5 us (14%)
  local copies, waits for them, and re-layouts  3.92 us (2%)
    all_to_all x3, blocking collectives, exchange(): return lax.all_to_all(values, axes, split_axis=0, concat_axis=0, tiled=True)  69.3 us
    pallas_call x1, Pallas kernels, solve(): pl.pallas_call(functools.partial(solve_kernel, ridge), in_specs=[full(pie...  25.1 us
    ppermute x8, starting transfers between devices, spread(): lax.ppermute(value, 'c', [(i, (i + 1) % nc) for i in range(nc)])  24.2 us
    pallas_call x1, Pallas kernels, features(): pl.pallas_call(feature_kernel, grid=(total // tile,), in_specs=[whole] *...  14 us
    all_to_all x2, waiting for transfers between devices, exchange(): return lax.all_to_all(values, axes, split_axis=0, concat_axis=0, tiled=True)  12.9 us
    all_to_all x2, starting transfers between devices, exchange(): return lax.all_to_all(values, axes, split_axis=0, concat_axis=0, tiled=True)  11.5 us
    ppermute x6, waiting for transfers between devices, spread(): lax.ppermute(values, 'x', [(i, (i + shift) % nx) for i in range(nx)])  10.9 us
    ppermute x6, starting transfers between devices, spread(): lax.ppermute(values, 'x', [(i, (i + shift) % nx) for i in range(nx)])  5.15 us
  transfers between devices with their start and end apart: 16, of which 7 were waited for; matrix products, arithmetic and copies ran while one was open for 0% of the time, Pallas kernels for 0%

profile of v5, /device:TPU:1, one launch (start us, length us, event | category | flops | bytes accessed | tf_op | source)
XLA Modules:
  0.0 183.7 jit_solution(1586031882781639412)
XLA Ops:
  0.6 2.4 %payload.1 = bf16[32,8,640]{2,1,0:T(8,128)(2,1)} custom-call(s32[2]{0:T(128)} %order.3, bf16[2,1024,512]{2,1,0:T(8,128)(2,1)} %proj_ref.1, bf16[2,512]{1,0:T(2,128)(2,1)} %phase_ref.1), custom_call_target="tpu_custom_call" | custom-call | tf_op jit(solution)/shard_map/payload/pallas_call | solution.py:67
  3.0 24.8 %all_to_all.25.got_ref = bf16[32,8,640]{2,1,0:T(8,128)(2,1)} all-to-all(bf16[32,8,640]{2,1,0:T(8,128)(2,1)} %payload.1), channel_id=1, replica_groups=mesh['z'=8,'y'=4,'x'=4,'c'=2] {'z','y'}, dimensions={0} | all-to-all | bytes 655360 | tf_op jit(solution)/shard_map/all_to_all | solution.py:370
  27.8 1.7 pick.1
  29.6 15.3 %all_to_all.26.refs_0_ = bf16[32,8,512]{2,1,0:T(8,128)(2,1)S(1)} all-to-all(bf16[32,8,512]{2,1,0:T(8,128)(2,1)} %get-tuple-element.10), channel_id=1, replica_groups=mesh['z'=8,'y'=4,'x'=4,'c'=2] {'z','y'}, dimensions={0} | all-to-all | bytes 524288 | tf_op jit(solution)/shard_map/all_to_all | solution.py:370
  44.8 2.5 %collective-permute-start.5 = (bf16[32,8,512]{2,1,0:T(8,128)(2,1)S(1)}, bf16[32,8,512]{2,1,0:T(8,128)(2,1)S(1)}, u32[]{:S(2)}, u32[]{:S(2)}) collective-permute-start(bf16[32,8,512]{2,1,0:T(8,128)(2,1)S(1)} %all_to_all.26.refs_0_), channel_id=1, source_target_pairs={{0,6},{2,0},{4,2},{6,4},{1,7},{3,1},{5,3},{7,5},{8,14},{10,8},{12,... | collective-permute-start | bytes 786440 | tf_op jit(solution)/shard_map/ppermute | solution.py:381
  47.3 0.5 collective-permute-start.3
  47.8 0.6 collective-permute-start.1
  48.4 4.3 %collective-permute-start = (bf16[32,8,512]{2,1,0:T(8,128)(2,1)S(1)}, bf16[32,8,512]{2,1,0:T(8,128)(2,1)S(1)}, u32[]{:S(2)}, u32[]{:S(2)}) collective-permute-start(bf16[32,8,512]{2,1,0:T(8,128)(2,1)S(1)} %all_to_all.26.refs_0_), channel_id=1, source_target_pairs={{0,1},{1,0},{2,3},{3,2},{4,5},{5,4},{6,7},{7,6},{8,9},{9,8},{10,11... | collective-permute-start | bytes 786440 | tf_op jit(solution)/shard_map/ppermute | solution.py:384
  52.8 0.9 collective-permute-done.5.refs_6_
  53.7 5.8 %collective-permute-start.6 = (bf16[32,8,512]{2,1,0:T(8,128)(2,1)S(1)}, bf16[32,8,512]{2,1,0:T(8,128)(2,1)S(1)}, u32[]{:S(2)}, u32[]{:S(2)}) collective-permute-start(bf16[32,8,512]{2,1,0:T(8,128)(2,1)S(1)} %collective-permute-done.5.refs_6_), channel_id=1, source_target_pairs={{0,1},{1,0},{2,3},{3,2},{4,5},{5,4},{6,7},{7,6},{8,9},{9,8},{10,11... | collective-permute-start | bytes 786440 | tf_op jit(solution)/shard_map/ppermute | solution.py:384
  59.5 0.0 collective-permute-done.3.refs_4_
  59.5 1.0 collective-permute-start.4
  60.5 0.6 collective-permute-done.1.refs_2_
  61.1 2.1 %collective-permute-start.2 = (bf16[32,8,512]{2,1,0:T(8,128)(2,1)S(1)}, bf16[32,8,512]{2,1,0:T(8,128)(2,1)S(1)}, u32[]{:S(2)}, u32[]{:S(2)}) collective-permute-start(bf16[32,8,512]{2,1,0:T(8,128)(2,1)S(1)} %collective-permute-done.1.refs_2_), channel_id=1, source_target_pairs={{0,1},{1,0},{2,3},{3,2},{4,5},{5,4},{6,7},{7,6},{8,9},{9,8},{10,11... | collective-permute-start | bytes 786440 | tf_op jit(solution)/shard_map/ppermute | solution.py:384
  63.2 0.0 collective-permute-done.refs_1_
  63.2 0.0 collective-permute-done.6.refs_7_
  63.2 0.0 copy-start.5
  63.2 0.0 collective-permute-done.4.refs_5_
  63.2 1.1 collective-permute-done.2.refs_3_
  64.3 0.0 copy-done.5
  64.3 0.0 copy-start
  64.3 0.7 copy-done
  65.0 14.0 %features.1 = (bf16[2048,1024]{1,0:T(8,128)(2,1)}, f32[32,56,128]{2,1,0:T(8,128)}) custom-call(bf16[32,8,512]{2,1,0:T(8,128)(2,1)S(1)} %all_to_all.26.refs_0_, bf16[32,8,512]{2,1,0:T(8,128)(2,1)S(1)} %collective-permute-done.refs_1_, bf16[32,8,512]{2,1,0:T(8,128)(2,1)S(1)} %collective-permute-done.1.refs_2_, ...), custom_call_target="tpu_custom_call" | custom-call | tf_op jit(solution)/shard_map/features/pallas_call | solution.py:179
  79.0 29.2 %all_to_all.27 = f32[32,56,128]{2,1,0:T(8,128)S(1)} all-to-all(f32[32,56,128]{2,1,0:T(8,128)} %get-tuple-element.12), channel_id=1, replica_groups=mesh['z'=8,'y'=4,'x'=4,'c'=2] {'z','y'}, dimensions={0} | all-to-all | bytes 1835008 | tf_op jit(solution)/shard_map/all_to_all | solution.py:370
  108.2 0.1 reduce_sum.9
  108.2 0.8 broadcast_in_dim.4
  109.0 5.9 %all-to-all-start.3 = ((f32[32,24,128]{2,1,0:T(8,128)}), f32[32,24,128]{2,1,0:T(8,128)S(1)}, u32[]{:S(2)}, u32[]{:S(2)}) async-start(f32[32,24,128]{2,1,0:T(8,128)} %broadcast_in_dim.4), calls=%async_computation.3 | async-start | bytes 786432 | tf_op jit(solution)/shard_map/all_to_all | solution.py:370
  115.0 12.9 %all-to-all-done.3.refs_0_ = f32[32,24,128]{2,1,0:T(8,128)S(1)} async-done(((f32[32,24,128]{2,1,0:T(8,128)}), f32[32,24,128]{2,1,0:T(8,128)S(1)}, u32[]{:S(2)}, u32[]{:S(2)}) %all-to-all-start.3) | async-done | bytes 393248 | tf_op jit(solution)/shard_map/all_to_all | solution.py:370
  127.9 0.9 broadcast_in_dim.5
  128.7 5.5 %all-to-all-start.4 = ((f32[32,32,128]{2,1,0:T(8,128)}), f32[32,32,128]{2,1,0:T(8,128)S(1)}, u32[]{:S(2)}, u32[]{:S(2)}) async-start(f32[32,32,128]{2,1,0:T(8,128)} %broadcast_in_dim.5), calls=%async_computation.4 | async-start | bytes 1048576 | tf_op jit(solution)/shard_map/all_to_all | solution.py:370
  134.3 0.5 collective-permute-start.12
  134.8 0.4 collective-permute-start.10
  135.2 0.6 collective-permute-start.8
  135.8 2.8 %collective-permute-start.7 = (f32[32,24,128]{2,1,0:T(8,128)S(1)}, f32[32,24,128]{2,1,0:T(8,128)S(1)}, u32[]{:S(2)}, u32[]{:S(2)}) collective-permute-start(f32[32,24,128]{2,1,0:T(8,128)S(1)} %all-to-all-done.3.refs_0_), channel_id=1, source_target_pairs={{0,1},{1,0},{2,3},{3,2},{4,5},{5,4},{6,7},{7,6},{8,9},{9,8},{10,11... | collective-permute-start | bytes 1179656 | tf_op jit(solution)/shard_map/ppermute | solution.py:384
  138.7 4.3 %collective-permute-done.12.refs_6_ = f32[32,24,128]{2,1,0:T(8,128)S(1)} collective-permute-done((f32[32,24,128]{2,1,0:T(8,128)S(1)}, f32[32,24,128]{2,1,0:T(8,128)S(1)}, u32[]{:S(2)}, u32[]{:S(2)}) %collective-permute-start.12) | collective-permute-done | bytes 393248 | tf_op jit(solution)/shard_map/ppermute | solution.py:381
  142.9 0.0 copy-start.2
  143.0 5.5 %collective-permute-start.13 = (f32[32,24,128]{2,1,0:T(8,128)S(1)}, f32[32,24,128]{2,1,0:T(8,128)S(1)}, u32[]{:S(2)}, u32[]{:S(2)}) collective-permute-start(f32[32,24,128]{2,1,0:T(8,128)S(1)} %collective-permute-done.12.refs_6_), channel_id=1, source_target_pairs={{0,1},{1,0},{2,3},{3,2},{4,5},{5,4},{6,7},{7,6},{8,9},{9,8},{10,11... | collective-permute-start | bytes 1179656 | tf_op jit(solution)/shard_map/ppermute | solution.py:384
  148.4 0.0 collective-permute-done.10.refs_4_
  148.4 2.2 %collective-permute-start.11 = (f32[32,24,128]{2,1,0:T(8,128)S(1)}, f32[32,24,128]{2,1,0:T(8,128)S(1)}, u32[]{:S(2)}, u32[]{:S(2)}) collective-permute-start(f32[32,24,128]{2,1,0:T(8,128)S(1)} %collective-permute-done.10.refs_4_), channel_id=1, source_target_pairs={{0,1},{1,0},{2,3},{3,2},{4,5},{5,4},{6,7},{7,6},{8,9},{9,8},{10,11... | collective-permute-start | bytes 1179656 | tf_op jit(solution)/shard_map/ppermute | solution.py:384
  150.7 5.1 %collective-permute-done.8.refs_2_ = f32[32,24,128]{2,1,0:T(8,128)S(1)} collective-permute-done((f32[32,24,128]{2,1,0:T(8,128)S(1)}, f32[32,24,128]{2,1,0:T(8,128)S(1)}, u32[]{:S(2)}, u32[]{:S(2)}) %collective-permute-start.8) | collective-permute-done | bytes 393248 | tf_op jit(solution)/shard_map/ppermute | solution.py:381
  155.8 0.5 collective-permute-start.9
  156.3 0.0 collective-permute-done.7.refs_1_
  156.3 0.0 collective-permute-done.13.refs_7_
  156.3 0.0 copy-start.3
  156.3 0.0 collective-permute-done.11.refs_5_
  156.3 0.0 copy-start.4
  156.3 0.8 copy-done.4
  157.1 0.5 collective-permute-done.9.refs_3_
  157.6 0.0 all-to-all-done.4.refs_8_
  157.6 0.0 copy-start.1
  157.6 0.0 copy-done.2
  157.6 0.0 copy-done.3
  157.6 0.8 copy-done.1
  158.4 25.1 %solve.1 = (f32[2,512,128]{2,1,0:T(8,128)}, f32[2048,128]{1,0:T(8,128)}) custom-call(f32[32,24,128]{2,1,0:T(8,128)S(1)} %all-to-all-done.3.refs_0_, f32[32,24,128]{2,1,0:T(8,128)S(1)} %collective-permute-done.7.refs_1_, f32[32,24,128]{2,1,0:T(8,128)S(1)} %collective-permute-done.8.refs_2_, f32[32,24,128]{2,1,0:T(8,128)S(1)} %collective-permute-done.9.refs_3_, ...), custom_call_target="tpu_custom_call" | custom-call | tf_op jit(solution)/shard_map/solve/pallas_call | solution.py:341
  (2 shorter events, 0.0 us)
Async XLA Ops:
  44.8 8.9 %collective-permute-start.5 = (bf16[32,8,512]{2,1,0:T(8,128)(2,1)S(1)}, bf16[32,8,512]{2,1,0:T(8,128)(2,1)S(1)}, u32[]{:S(2)}, u32[]{:S(2)}) collective-permute-start(bf16[32,8,512]{2,1,0:T(8,128)(2,1)S(1)} %all_to_all.26.refs_0_), channel_id=1, source_target_pairs={{0,6},{2,0},{4,2},{6,4},{1,7},{3,1},{5,3},{7,5},{8,14},{10,8},{12,... | collective-permute-start | bytes 786440 | tf_op jit(solution)/shard_map/ppermute | solution.py:381
  47.3 12.2 %collective-permute-start.3 = (bf16[32,8,512]{2,1,0:T(8,128)(2,1)S(1)}, bf16[32,8,512]{2,1,0:T(8,128)(2,1)S(1)}, u32[]{:S(2)}, u32[]{:S(2)}) collective-permute-start(bf16[32,8,512]{2,1,0:T(8,128)(2,1)S(1)} %all_to_all.26.refs_0_), channel_id=1, source_target_pairs={{0,4},{2,6},{4,0},{6,2},{1,5},{3,7},{5,1},{7,3},{8,12},{10,14},{12... | collective-permute-start | bytes 786440 | tf_op jit(solution)/shard_map/ppermute | solution.py:381
  47.8 13.2 %collective-permute-start.1 = (bf16[32,8,512]{2,1,0:T(8,128)(2,1)S(1)}, bf16[32,8,512]{2,1,0:T(8,128)(2,1)S(1)}, u32[]{:S(2)}, u32[]{:S(2)}) collective-permute-start(bf16[32,8,512]{2,1,0:T(8,128)(2,1)S(1)} %all_to_all.26.refs_0_), channel_id=1, source_target_pairs={{0,2},{2,4},{4,6},{6,0},{1,3},{3,5},{5,7},{7,1},{8,10},{10,12},{12... | collective-permute-start | bytes 786440 | tf_op jit(solution)/shard_map/ppermute | solution.py:381
  48.4 14.7 %collective-permute-start = (bf16[32,8,512]{2,1,0:T(8,128)(2,1)S(1)}, bf16[32,8,512]{2,1,0:T(8,128)(2,1)S(1)}, u32[]{:S(2)}, u32[]{:S(2)}) collective-permute-start(bf16[32,8,512]{2,1,0:T(8,128)(2,1)S(1)} %all_to_all.26.refs_0_), channel_id=1, source_target_pairs={{0,1},{1,0},{2,3},{3,2},{4,5},{5,4},{6,7},{7,6},{8,9},{9,8},{10,11... | collective-permute-start | bytes 786440 | tf_op jit(solution)/shard_map/ppermute | solution.py:384
  53.7 9.5 %collective-permute-start.6 = (bf16[32,8,512]{2,1,0:T(8,128)(2,1)S(1)}, bf16[32,8,512]{2,1,0:T(8,128)(2,1)S(1)}, u32[]{:S(2)}, u32[]{:S(2)}) collective-permute-start(bf16[32,8,512]{2,1,0:T(8,128)(2,1)S(1)} %collective-permute-done.5.refs_6_), channel_id=1, source_target_pairs={{0,1},{1,0},{2,3},{3,2},{4,5},{5,4},{6,7},{7,6},{8,9},{9,8},{10,11... | collective-permute-start | bytes 786440 | tf_op jit(solution)/shard_map/ppermute | solution.py:384
  59.5 3.7 %collective-permute-start.4 = (bf16[32,8,512]{2,1,0:T(8,128)(2,1)S(1)}, bf16[32,8,512]{2,1,0:T(8,128)(2,1)S(1)}, u32[]{:S(2)}, u32[]{:S(2)}) collective-permute-start(bf16[32,8,512]{2,1,0:T(8,128)(2,1)S(1)} %collective-permute-done.3.refs_4_), channel_id=1, source_target_pairs={{0,1},{1,0},{2,3},{3,2},{4,5},{5,4},{6,7},{7,6},{8,9},{9,8},{10,11... | collective-permute-start | bytes 786440 | tf_op jit(solution)/shard_map/ppermute | solution.py:384
  61.1 3.2 %collective-permute-start.2 = (bf16[32,8,512]{2,1,0:T(8,128)(2,1)S(1)}, bf16[32,8,512]{2,1,0:T(8,128)(2,1)S(1)}, u32[]{:S(2)}, u32[]{:S(2)}) collective-permute-start(bf16[32,8,512]{2,1,0:T(8,128)(2,1)S(1)} %collective-permute-done.1.refs_2_), channel_id=1, source_target_pairs={{0,1},{1,0},{2,3},{3,2},{4,5},{5,4},{6,7},{7,6},{8,9},{9,8},{10,11... | collective-permute-start | bytes 786440 | tf_op jit(solution)/shard_map/ppermute | solution.py:384
  63.2 1.2 copy-start.5
  64.3 0.7 copy-start
  109.0 18.9 %all-to-all-start.3 = ((f32[32,24,128]{2,1,0:T(8,128)}), f32[32,24,128]{2,1,0:T(8,128)S(1)}, u32[]{:S(2)}, u32[]{:S(2)}) async-start(f32[32,24,128]{2,1,0:T(8,128)} %broadcast_in_dim.4), calls=%async_computation.3 | async-start | bytes 786432 | tf_op jit(solution)/shard_map/all_to_all | solution.py:370
  128.7 28.9 %all-to-all-start.4 = ((f32[32,32,128]{2,1,0:T(8,128)}), f32[32,32,128]{2,1,0:T(8,128)S(1)}, u32[]{:S(2)}, u32[]{:S(2)}) async-start(f32[32,32,128]{2,1,0:T(8,128)} %broadcast_in_dim.5), calls=%async_computation.4 | async-start | bytes 1048576 | tf_op jit(solution)/shard_map/all_to_all | solution.py:370
  134.3 8.7 %collective-permute-start.12 = (f32[32,24,128]{2,1,0:T(8,128)S(1)}, f32[32,24,128]{2,1,0:T(8,128)S(1)}, u32[]{:S(2)}, u32[]{:S(2)}) collective-permute-start(f32[32,24,128]{2,1,0:T(8,128)S(1)} %all-to-all-done.3.refs_0_), channel_id=1, source_target_pairs={{0,6},{2,0},{4,2},{6,4},{1,7},{3,1},{5,3},{7,5},{8,14},{10,8},{12,... | collective-permute-start | bytes 1179656 | tf_op jit(solution)/shard_map/ppermute | solution.py:381
  134.8 13.6 %collective-permute-start.10 = (f32[32,24,128]{2,1,0:T(8,128)S(1)}, f32[32,24,128]{2,1,0:T(8,128)S(1)}, u32[]{:S(2)}, u32[]{:S(2)}) collective-permute-start(f32[32,24,128]{2,1,0:T(8,128)S(1)} %all-to-all-done.3.refs_0_), channel_id=1, source_target_pairs={{0,4},{2,6},{4,0},{6,2},{1,5},{3,7},{5,1},{7,3},{8,12},{10,14},{12... | collective-permute-start | bytes 1179656 | tf_op jit(solution)/shard_map/ppermute | solution.py:381
  135.2 20.6 %collective-permute-start.8 = (f32[32,24,128]{2,1,0:T(8,128)S(1)}, f32[32,24,128]{2,1,0:T(8,128)S(1)}, u32[]{:S(2)}, u32[]{:S(2)}) collective-permute-start(f32[32,24,128]{2,1,0:T(8,128)S(1)} %all-to-all-done.3.refs_0_), channel_id=1, source_target_pairs={{0,2},{2,4},{4,6},{6,0},{1,3},{3,5},{5,7},{7,1},{8,10},{10,12},{12... | collective-permute-start | bytes 1179656 | tf_op jit(solution)/shard_map/ppermute | solution.py:381
  135.8 20.4 %collective-permute-start.7 = (f32[32,24,128]{2,1,0:T(8,128)S(1)}, f32[32,24,128]{2,1,0:T(8,128)S(1)}, u32[]{:S(2)}, u32[]{:S(2)}) collective-permute-start(f32[32,24,128]{2,1,0:T(8,128)S(1)} %all-to-all-done.3.refs_0_), channel_id=1, source_target_pairs={{0,1},{1,0},{2,3},{3,2},{4,5},{5,4},{6,7},{7,6},{8,9},{9,8},{10,11... | collective-permute-start | bytes 1179656 | tf_op jit(solution)/shard_map/ppermute | solution.py:384
  142.9 14.7 %copy-start.2 = (f32[32,24,128]{2,1,0:T(8,128)}, f32[32,24,128]{2,1,0:T(8,128)S(1)}, u32[]{:S(2)}) copy-start(f32[32,24,128]{2,1,0:T(8,128)S(1)} %collective-permute-done.12.refs_6_) | copy-start | bytes 1179652
  143.0 13.3 %collective-permute-start.13 = (f32[32,24,128]{2,1,0:T(8,128)S(1)}, f32[32,24,128]{2,1,0:T(8,128)S(1)}, u32[]{:S(2)}, u32[]{:S(2)}) collective-permute-start(f32[32,24,128]{2,1,0:T(8,128)S(1)} %collective-permute-done.12.refs_6_), channel_id=1, source_target_pairs={{0,1},{1,0},{2,3},{3,2},{4,5},{5,4},{6,7},{7,6},{8,9},{9,8},{10,11... | collective-permute-start | bytes 1179656 | tf_op jit(solution)/shard_map/ppermute | solution.py:384
  148.4 7.9 %collective-permute-start.11 = (f32[32,24,128]{2,1,0:T(8,128)S(1)}, f32[32,24,128]{2,1,0:T(8,128)S(1)}, u32[]{:S(2)}, u32[]{:S(2)}) collective-permute-start(f32[32,24,128]{2,1,0:T(8,128)S(1)} %collective-permute-done.10.refs_4_), channel_id=1, source_target_pairs={{0,1},{1,0},{2,3},{3,2},{4,5},{5,4},{6,7},{7,6},{8,9},{9,8},{10,11... | collective-permute-start | bytes 1179656 | tf_op jit(solution)/shard_map/ppermute | solution.py:384
  155.8 1.8 %collective-permute-start.9 = (f32[32,24,128]{2,1,0:T(8,128)S(1)}, f32[32,24,128]{2,1,0:T(8,128)S(1)}, u32[]{:S(2)}, u32[]{:S(2)}) collective-permute-start(f32[32,24,128]{2,1,0:T(8,128)S(1)} %collective-permute-done.8.refs_2_), channel_id=1, source_target_pairs={{0,1},{1,0},{2,3},{3,2},{4,5},{5,4},{6,7},{7,6},{8,9},{9,8},{10,11... | collective-permute-start | bytes 1179656 | tf_op jit(solution)/shard_map/ppermute | solution.py:384
  156.3 1.4 copy-start.3
  156.3 0.8 copy-start.4
  157.6 0.8 copy-start.1

commit v6 on v5

--- a/solution.py
+++ b/solution.py
@@ -8,6 +8,7 @@
 from jax.experimental.pallas import tpu as pltpu
 from jax.sharding import Mesh
 from jax.sharding import PartitionSpec as P
+
 
 STEPS = 2
 BF = jnp.bfloat16
@@ -62,7 +63,7 @@
 
 
 def payload(order, projections, phases, nrows):
-    local_blocks, depth, width = projections.shape
+    local_blocks, _, width = projections.shape
     whole = pl.BlockSpec(memory_space=pltpu.VMEM)
     return pl.pallas_call(
         functools.partial(payload_kernel, local_blocks),
@@ -366,12 +367,31 @@
     )(*pieces, cross, old, feats, residuals)
 
 
+def copies_kernel(got_ref, gram_ref, cross_ref):
+    summed = [got_ref[i] for i in range(got_ref.shape[0])]
+    while len(summed) > 1:
+        summed = [summed[i] + summed[i + 1] for i in range(0, len(summed), 2)]
+    first = gram_ref.shape[1]
+    gram_ref[...] = jnp.broadcast_to(summed[0][None, :first], gram_ref.shape)
+    cross_ref[...] = jnp.broadcast_to(summed[0][None, first:], cross_ref.shape)
+
+
+def copies_of_sum(got):
+    whole = pl.BlockSpec(memory_space=pltpu.VMEM)
+    return pl.pallas_call(
+        copies_kernel,
+        in_specs=[whole],
+        out_specs=[whole, whole],
+        out_shape=[
+            jax.ShapeDtypeStruct((got.shape[0], 24, 128), F32),
+            jax.ShapeDtypeStruct((got.shape[0], 32, 128), F32),
+        ],
+        name="copies",
+    )(got)
+
+
 def exchange(values, axes):
     return lax.all_to_all(values, axes, split_axis=0, concat_axis=0, tiled=True)
-
-
-def gather(values, axes, count):
-    return exchange(jnp.broadcast_to(values[None], (count,) + values.shape), axes)
 
 
 def spread(values):
@@ -386,7 +406,7 @@
 
 
 def body(embeddings, residuals, projections, phases, old_coef, block_order):
-    local_blocks, depth, width = projections.shape
+    local_blocks, _, width = projections.shape
     nrows = lax.axis_size("z") * lax.axis_size("y")
     ridge = 0.25 * (embeddings.shape[0] * nrows) / width
 
@@ -395,11 +415,11 @@
     weights = spread(exchange(copies, ROWS))
     feats, parts = features(weights, embeddings, shifts, residuals)
 
-    summed = jnp.sum(exchange(parts, ROWS), axis=0)
-    grams = gather(summed[:24], ROWS, nrows)
-    cross, grams = lax.optimization_barrier((summed[24:], grams))
+    gram_copies, cross_copies = copies_of_sum(exchange(parts, ROWS))
+    grams = exchange(gram_copies, ROWS)
+    cross_copies, grams = lax.optimization_barrier((cross_copies, grams))
     pieces = spread(grams)
-    cross = gather(cross, ROWS, nrows)
+    cross = exchange(cross_copies, ROWS)
     coef, current = solve(pieces, cross, old_coef, feats, residuals, ridge)
     return current, coef
 

time: 184 us -> 184 us (level)
  blocking collectives: 69.3 us -> 88.3 us
  waiting for transfers between devices: 25.5 us -> 12.6 us
  starting transfers between devices: 40.9 us -> 34.9 us
    all_to_all x3 -> x4, blocking collectives: 69.3 us -> 88.3 us  [exchange(): return lax.all_to_all(values, axes, split_axis=0, concat_axis=0, tiled=True)]
    all_to_all x2 -> x1, waiting for transfers between devices: 12.9 us -> 0.01 us  [exchange(): return lax.all_to_all(values, axes, split_axis=0, concat_axis=0, tiled=True)]
    all_to_all x2 -> x1, starting transfers between devices: 11.5 us -> 5.55 us  [exchange(): return lax.all_to_all(values, axes, split_axis=0, concat_axis=0, tiled=True)]
    pallas_call x0 -> x1, Pallas kernels: none -> 2.14 us  [copies_of_sum(): pl.pallas_call(copies_kernel, in_specs=[whole], out_specs=[whole, whole],...]
  transfers between devices with their start and end apart: 16 -> 15, of which waited for: 7 -> 6; matrix products, arithmetic and copies ran while one was open for 0% -> 0% of each run, Pallas kernels for 0% -> 0%
where the time goes in v6:
time: 184 us; the launch traced here: 183 us
  blocking collectives  88.3 us (48%)
  Pallas kernels  43.9 us (24%)
  starting transfers between devices  34.9 us (19%)
  waiting for transfers between devices  12.6 us (7%)
  local copies, waits for them, and re-layouts  2.3 us (1%)
    all_to_all x4, blocking collectives, exchange(): return lax.all_to_all(values, axes, split_axis=0, concat_axis=0, tiled=True)  88.3 us
    ppermute x8, starting transfers between devices, spread(): lax.ppermute(value, 'c', [(i, (i + 1) % nc) for i in range(nc)])  24.2 us
    pallas_call x1, Pallas kernels, solve(): pl.pallas_call(functools.partial(solve_kernel, ridge), in_specs=[full(pie...  23.7 us
    pallas_call x1, Pallas kernels, features(): pl.pallas_call(feature_kernel, grid=(total // tile,), in_specs=[whole] *...  14 us
    ppermute x6, waiting for transfers between devices, spread(): lax.ppermute(values, 'x', [(i, (i + shift) % nx) for i in range(nx)])  10.9 us
    all_to_all x1, starting transfers between devices, exchange(): return lax.all_to_all(values, axes, split_axis=0, concat_axis=0, tiled=True)  5.55 us
    ppermute x6, starting transfers between devices, spread(): lax.ppermute(values, 'x', [(i, (i + shift) % nx) for i in range(nx)])  5.15 us
  transfers between devices with their start and end apart: 15, of which 6 were waited for; matrix products, arithmetic and copies ran while one was open for 0% of the time, Pallas kernels for 0%

profile of v6, /device:TPU:1, one launch (start us, length us, event | category | flops | bytes accessed | tf_op | source)
XLA Modules:
  0.0 182.8 jit_solution(15898218311058522625)
XLA Ops:
  0.6 2.4 %payload.1 = bf16[32,8,640]{2,1,0:T(8,128)(2,1)} custom-call(s32[2]{0:T(128)} %order.3, bf16[2,1024,512]{2,1,0:T(8,128)(2,1)} %proj_ref.1, bf16[2,512]{1,0:T(2,128)(2,1)} %phase_ref.1), custom_call_target="tpu_custom_call" | custom-call | tf_op jit(solution)/shard_map/payload/pallas_call | solution.py:68
  3.0 24.8 %all_to_all.25.got_ref = bf16[32,8,640]{2,1,0:T(8,128)(2,1)} all-to-all(bf16[32,8,640]{2,1,0:T(8,128)(2,1)} %payload.1), channel_id=1, replica_groups=mesh['z'=8,'y'=4,'x'=4,'c'=2] {'z','y'}, dimensions={0} | all-to-all | bytes 655360 | tf_op jit(solution)/shard_map/all_to_all | solution.py:394
  27.8 1.7 pick.1
  29.6 15.3 %all_to_all.26.refs_0_ = bf16[32,8,512]{2,1,0:T(8,128)(2,1)S(1)} all-to-all(bf16[32,8,512]{2,1,0:T(8,128)(2,1)} %get-tuple-element.12), channel_id=1, replica_groups=mesh['z'=8,'y'=4,'x'=4,'c'=2] {'z','y'}, dimensions={0} | all-to-all | bytes 524288 | tf_op jit(solution)/shard_map/all_to_all | solution.py:394
  44.8 2.5 %collective-permute-start.5 = (bf16[32,8,512]{2,1,0:T(8,128)(2,1)S(1)}, bf16[32,8,512]{2,1,0:T(8,128)(2,1)S(1)}, u32[]{:S(2)}, u32[]{:S(2)}) collective-permute-start(bf16[32,8,512]{2,1,0:T(8,128)(2,1)S(1)} %all_to_all.26.refs_0_), channel_id=1, source_target_pairs={{0,6},{2,0},{4,2},{6,4},{1,7},{3,1},{5,3},{7,5},{8,14},{10,8},{12,... | collective-permute-start | bytes 786440 | tf_op jit(solution)/shard_map/ppermute | solution.py:401
  47.3 0.5 collective-permute-start.3
  47.8 0.6 collective-permute-start.1
  48.4 4.3 %collective-permute-start = (bf16[32,8,512]{2,1,0:T(8,128)(2,1)S(1)}, bf16[32,8,512]{2,1,0:T(8,128)(2,1)S(1)}, u32[]{:S(2)}, u32[]{:S(2)}) collective-permute-start(bf16[32,8,512]{2,1,0:T(8,128)(2,1)S(1)} %all_to_all.26.refs_0_), channel_id=1, source_target_pairs={{0,1},{1,0},{2,3},{3,2},{4,5},{5,4},{6,7},{7,6},{8,9},{9,8},{10,11... | collective-permute-start | bytes 786440 | tf_op jit(solution)/shard_map/ppermute | solution.py:404
  52.8 0.9 collective-permute-done.5.refs_6_
  53.7 5.8 %collective-permute-start.6 = (bf16[32,8,512]{2,1,0:T(8,128)(2,1)S(1)}, bf16[32,8,512]{2,1,0:T(8,128)(2,1)S(1)}, u32[]{:S(2)}, u32[]{:S(2)}) collective-permute-start(bf16[32,8,512]{2,1,0:T(8,128)(2,1)S(1)} %collective-permute-done.5.refs_6_), channel_id=1, source_target_pairs={{0,1},{1,0},{2,3},{3,2},{4,5},{5,4},{6,7},{7,6},{8,9},{9,8},{10,11... | collective-permute-start | bytes 786440 | tf_op jit(solution)/shard_map/ppermute | solution.py:404
  59.5 0.0 collective-permute-done.3.refs_4_
  59.5 1.0 collective-permute-start.4
  60.5 0.6 collective-permute-done.1.refs_2_
  61.1 2.1 %collective-permute-start.2 = (bf16[32,8,512]{2,1,0:T(8,128)(2,1)S(1)}, bf16[32,8,512]{2,1,0:T(8,128)(2,1)S(1)}, u32[]{:S(2)}, u32[]{:S(2)}) collective-permute-start(bf16[32,8,512]{2,1,0:T(8,128)(2,1)S(1)} %collective-permute-done.1.refs_2_), channel_id=1, source_target_pairs={{0,1},{1,0},{2,3},{3,2},{4,5},{5,4},{6,7},{7,6},{8,9},{9,8},{10,11... | collective-permute-start | bytes 786440 | tf_op jit(solution)/shard_map/ppermute | solution.py:404
  63.2 0.0 collective-permute-done.refs_1_
  63.2 0.0 collective-permute-done.6.refs_7_
  63.2 0.0 copy-start.5
  63.2 0.0 collective-permute-done.4.refs_5_
  63.2 1.1 collective-permute-done.2.refs_3_
  64.3 0.0 copy-done.5
  64.3 0.0 copy-start
  64.3 0.7 copy-done
  65.0 14.0 %features.1 = (bf16[2048,1024]{1,0:T(8,128)(2,1)}, f32[32,56,128]{2,1,0:T(8,128)}) custom-call(bf16[32,8,512]{2,1,0:T(8,128)(2,1)S(1)} %all_to_all.26.refs_0_, bf16[32,8,512]{2,1,0:T(8,128)(2,1)S(1)} %collective-permute-done.refs_1_, bf16[32,8,512]{2,1,0:T(8,128)(2,1)S(1)} %collective-permute-done.1.refs_2_, ...), custom_call_target="tpu_custom_call" | custom-call | tf_op jit(solution)/shard_map/features/pallas_call | solution.py:180
  79.0 29.3 %all_to_all.27.got_ref = f32[32,56,128]{2,1,0:T(8,128)} all-to-all(f32[32,56,128]{2,1,0:T(8,128)} %get-tuple-element.14), channel_id=1, replica_groups=mesh['z'=8,'y'=4,'x'=4,'c'=2] {'z','y'}, dimensions={0} | all-to-all | bytes 1835008 | tf_op jit(solution)/shard_map/all_to_all | solution.py:394
  108.3 2.1 %copies.1 = (f32[32,24,128]{2,1,0:T(8,128)}, f32[32,32,128]{2,1,0:T(8,128)}) custom-call(f32[32,56,128]{2,1,0:T(8,128)} %all_to_all.27.got_ref), custom_call_target="tpu_custom_call" | custom-call | tf_op jit(solution)/shard_map/copies/pallas_call | solution.py:381
  110.4 18.9 %all_to_all.28.refs_0_ = f32[32,24,128]{2,1,0:T(8,128)S(1)} all-to-all(f32[32,24,128]{2,1,0:T(8,128)} %get-tuple-element.16), channel_id=1, replica_groups=mesh['z'=8,'y'=4,'x'=4,'c'=2] {'z','y'}, dimensions={0} | all-to-all | bytes 786432 | tf_op jit(solution)/shard_map/all_to_all | solution.py:394
  129.3 5.5 %all-to-all-start.4 = ((f32[32,32,128]{2,1,0:T(8,128)}), f32[32,32,128]{2,1,0:T(8,128)S(1)}, u32[]{:S(2)}, u32[]{:S(2)}) async-start(f32[32,32,128]{2,1,0:T(8,128)} %get-tuple-element.18), calls=%async_computation.4 | async-start | bytes 1048576 | tf_op jit(solution)/shard_map/all_to_all | solution.py:394
  134.8 0.5 collective-permute-start.12
  135.3 0.4 collective-permute-start.10
  135.7 0.6 collective-permute-start.8
  136.4 2.8 %collective-permute-start.7 = (f32[32,24,128]{2,1,0:T(8,128)S(1)}, f32[32,24,128]{2,1,0:T(8,128)S(1)}, u32[]{:S(2)}, u32[]{:S(2)}) collective-permute-start(f32[32,24,128]{2,1,0:T(8,128)S(1)} %all_to_all.28.refs_0_), channel_id=1, source_target_pairs={{0,1},{1,0},{2,3},{3,2},{4,5},{5,4},{6,7},{7,6},{8,9},{9,8},{10,11... | collective-permute-start | bytes 1179656 | tf_op jit(solution)/shard_map/ppermute | solution.py:404
  139.2 4.3 %collective-permute-done.12.refs_6_ = f32[32,24,128]{2,1,0:T(8,128)S(1)} collective-permute-done((f32[32,24,128]{2,1,0:T(8,128)S(1)}, f32[32,24,128]{2,1,0:T(8,128)S(1)}, u32[]{:S(2)}, u32[]{:S(2)}) %collective-permute-start.12) | collective-permute-done | bytes 393248 | tf_op jit(solution)/shard_map/ppermute | solution.py:401
  143.5 0.0 copy-start.2
  143.5 5.5 %collective-permute-start.13 = (f32[32,24,128]{2,1,0:T(8,128)S(1)}, f32[32,24,128]{2,1,0:T(8,128)S(1)}, u32[]{:S(2)}, u32[]{:S(2)}) collective-permute-start(f32[32,24,128]{2,1,0:T(8,128)S(1)} %collective-permute-done.12.refs_6_), channel_id=1, source_target_pairs={{0,1},{1,0},{2,3},{3,2},{4,5},{5,4},{6,7},{7,6},{8,9},{9,8},{10,11... | collective-permute-start | bytes 1179656 | tf_op jit(solution)/shard_map/ppermute | solution.py:404
  149.0 0.0 collective-permute-done.10.refs_4_
  149.0 2.2 %collective-permute-start.11 = (f32[32,24,128]{2,1,0:T(8,128)S(1)}, f32[32,24,128]{2,1,0:T(8,128)S(1)}, u32[]{:S(2)}, u32[]{:S(2)}) collective-permute-start(f32[32,24,128]{2,1,0:T(8,128)S(1)} %collective-permute-done.10.refs_4_), channel_id=1, source_target_pairs={{0,1},{1,0},{2,3},{3,2},{4,5},{5,4},{6,7},{7,6},{8,9},{9,8},{10,11... | collective-permute-start | bytes 1179656 | tf_op jit(solution)/shard_map/ppermute | solution.py:404
  151.2 5.1 %collective-permute-done.8.refs_2_ = f32[32,24,128]{2,1,0:T(8,128)S(1)} collective-permute-done((f32[32,24,128]{2,1,0:T(8,128)S(1)}, f32[32,24,128]{2,1,0:T(8,128)S(1)}, u32[]{:S(2)}, u32[]{:S(2)}) %collective-permute-start.8) | collective-permute-done | bytes 393248 | tf_op jit(solution)/shard_map/ppermute | solution.py:401
  156.3 0.5 collective-permute-start.9
  156.8 0.0 collective-permute-done.7.refs_1_
  156.8 0.0 collective-permute-done.13.refs_7_
  156.8 0.0 copy-start.3
  156.8 0.0 collective-permute-done.11.refs_5_
  156.8 0.0 copy-start.4
  156.8 0.8 copy-done.4
  157.6 0.5 collective-permute-done.9.refs_3_
  158.2 0.0 all-to-all-done.4.refs_8_
  158.2 0.0 copy-start.1
  158.2 0.0 copy-done.2
  158.2 0.0 copy-done.3
  158.2 0.8 copy-done.1
  159.0 23.7 %solve.1 = (f32[2,512,128]{2,1,0:T(8,128)}, f32[2048,128]{1,0:T(8,128)}) custom-call(f32[32,24,128]{2,1,0:T(8,128)S(1)} %all_to_all.28.refs_0_, f32[32,24,128]{2,1,0:T(8,128)S(1)} %collective-permute-done.7.refs_1_, f32[32,24,128]{2,1,0:T(8,128)S(1)} %collective-permute-done.8.refs_2_, f32[32,24,128]{2,1,0:T(8,128)S(1)} %collective-permute-done.9.refs_3_, ...), custom_call_target="tpu_custom_call" | custom-call | tf_op jit(solution)/shard_map/solve/pallas_call | solution.py:342
Async XLA Ops:
  44.8 8.9 %collective-permute-start.5 = (bf16[32,8,512]{2,1,0:T(8,128)(2,1)S(1)}, bf16[32,8,512]{2,1,0:T(8,128)(2,1)S(1)}, u32[]{:S(2)}, u32[]{:S(2)}) collective-permute-start(bf16[32,8,512]{2,1,0:T(8,128)(2,1)S(1)} %all_to_all.26.refs_0_), channel_id=1, source_target_pairs={{0,6},{2,0},{4,2},{6,4},{1,7},{3,1},{5,3},{7,5},{8,14},{10,8},{12,... | collective-permute-start | bytes 786440 | tf_op jit(solution)/shard_map/ppermute | solution.py:401
  47.3 12.2 %collective-permute-start.3 = (bf16[32,8,512]{2,1,0:T(8,128)(2,1)S(1)}, bf16[32,8,512]{2,1,0:T(8,128)(2,1)S(1)}, u32[]{:S(2)}, u32[]{:S(2)}) collective-permute-start(bf16[32,8,512]{2,1,0:T(8,128)(2,1)S(1)} %all_to_all.26.refs_0_), channel_id=1, source_target_pairs={{0,4},{2,6},{4,0},{6,2},{1,5},{3,7},{5,1},{7,3},{8,12},{10,14},{12... | collective-permute-start | bytes 786440 | tf_op jit(solution)/shard_map/ppermute | solution.py:401
  47.8 13.2 %collective-permute-start.1 = (bf16[32,8,512]{2,1,0:T(8,128)(2,1)S(1)}, bf16[32,8,512]{2,1,0:T(8,128)(2,1)S(1)}, u32[]{:S(2)}, u32[]{:S(2)}) collective-permute-start(bf16[32,8,512]{2,1,0:T(8,128)(2,1)S(1)} %all_to_all.26.refs_0_), channel_id=1, source_target_pairs={{0,2},{2,4},{4,6},{6,0},{1,3},{3,5},{5,7},{7,1},{8,10},{10,12},{12... | collective-permute-start | bytes 786440 | tf_op jit(solution)/shard_map/ppermute | solution.py:401
  48.4 14.7 %collective-permute-start = (bf16[32,8,512]{2,1,0:T(8,128)(2,1)S(1)}, bf16[32,8,512]{2,1,0:T(8,128)(2,1)S(1)}, u32[]{:S(2)}, u32[]{:S(2)}) collective-permute-start(bf16[32,8,512]{2,1,0:T(8,128)(2,1)S(1)} %all_to_all.26.refs_0_), channel_id=1, source_target_pairs={{0,1},{1,0},{2,3},{3,2},{4,5},{5,4},{6,7},{7,6},{8,9},{9,8},{10,11... | collective-permute-start | bytes 786440 | tf_op jit(solution)/shard_map/ppermute | solution.py:404
  53.7 9.5 %collective-permute-start.6 = (bf16[32,8,512]{2,1,0:T(8,128)(2,1)S(1)}, bf16[32,8,512]{2,1,0:T(8,128)(2,1)S(1)}, u32[]{:S(2)}, u32[]{:S(2)}) collective-permute-start(bf16[32,8,512]{2,1,0:T(8,128)(2,1)S(1)} %collective-permute-done.5.refs_6_), channel_id=1, source_target_pairs={{0,1},{1,0},{2,3},{3,2},{4,5},{5,4},{6,7},{7,6},{8,9},{9,8},{10,11... | collective-permute-start | bytes 786440 | tf_op jit(solution)/shard_map/ppermute | solution.py:404
  59.5 3.7 %collective-permute-start.4 = (bf16[32,8,512]{2,1,0:T(8,128)(2,1)S(1)}, bf16[32,8,512]{2,1,0:T(8,128)(2,1)S(1)}, u32[]{:S(2)}, u32[]{:S(2)}) collective-permute-start(bf16[32,8,512]{2,1,0:T(8,128)(2,1)S(1)} %collective-permute-done.3.refs_4_), channel_id=1, source_target_pairs={{0,1},{1,0},{2,3},{3,2},{4,5},{5,4},{6,7},{7,6},{8,9},{9,8},{10,11... | collective-permute-start | bytes 786440 | tf_op jit(solution)/shard_map/ppermute | solution.py:404
  61.1 3.2 %collective-permute-start.2 = (bf16[32,8,512]{2,1,0:T(8,128)(2,1)S(1)}, bf16[32,8,512]{2,1,0:T(8,128)(2,1)S(1)}, u32[]{:S(2)}, u32[]{:S(2)}) collective-permute-start(bf16[32,8,512]{2,1,0:T(8,128)(2,1)S(1)} %collective-permute-done.1.refs_2_), channel_id=1, source_target_pairs={{0,1},{1,0},{2,3},{3,2},{4,5},{5,4},{6,7},{7,6},{8,9},{9,8},{10,11... | collective-permute-start | bytes 786440 | tf_op jit(solution)/shard_map/ppermute | solution.py:404
  63.2 1.2 copy-start.5
  64.3 0.7 copy-start
  129.3 28.9 %all-to-all-start.4 = ((f32[32,32,128]{2,1,0:T(8,128)}), f32[32,32,128]{2,1,0:T(8,128)S(1)}, u32[]{:S(2)}, u32[]{:S(2)}) async-start(f32[32,32,128]{2,1,0:T(8,128)} %get-tuple-element.18), calls=%async_computation.4 | async-start | bytes 1048576 | tf_op jit(solution)/shard_map/all_to_all | solution.py:394
  134.8 8.7 %collective-permute-start.12 = (f32[32,24,128]{2,1,0:T(8,128)S(1)}, f32[32,24,128]{2,1,0:T(8,128)S(1)}, u32[]{:S(2)}, u32[]{:S(2)}) collective-permute-start(f32[32,24,128]{2,1,0:T(8,128)S(1)} %all_to_all.28.refs_0_), channel_id=1, source_target_pairs={{0,6},{2,0},{4,2},{6,4},{1,7},{3,1},{5,3},{7,5},{8,14},{10,8},{12,... | collective-permute-start | bytes 1179656 | tf_op jit(solution)/shard_map/ppermute | solution.py:401
  135.3 13.6 %collective-permute-start.10 = (f32[32,24,128]{2,1,0:T(8,128)S(1)}, f32[32,24,128]{2,1,0:T(8,128)S(1)}, u32[]{:S(2)}, u32[]{:S(2)}) collective-permute-start(f32[32,24,128]{2,1,0:T(8,128)S(1)} %all_to_all.28.refs_0_), channel_id=1, source_target_pairs={{0,4},{2,6},{4,0},{6,2},{1,5},{3,7},{5,1},{7,3},{8,12},{10,14},{12... | collective-permute-start | bytes 1179656 | tf_op jit(solution)/shard_map/ppermute | solution.py:401
  135.7 20.6 %collective-permute-start.8 = (f32[32,24,128]{2,1,0:T(8,128)S(1)}, f32[32,24,128]{2,1,0:T(8,128)S(1)}, u32[]{:S(2)}, u32[]{:S(2)}) collective-permute-start(f32[32,24,128]{2,1,0:T(8,128)S(1)} %all_to_all.28.refs_0_), channel_id=1, source_target_pairs={{0,2},{2,4},{4,6},{6,0},{1,3},{3,5},{5,7},{7,1},{8,10},{10,12},{12... | collective-permute-start | bytes 1179656 | tf_op jit(solution)/shard_map/ppermute | solution.py:401
  136.4 20.4 %collective-permute-start.7 = (f32[32,24,128]{2,1,0:T(8,128)S(1)}, f32[32,24,128]{2,1,0:T(8,128)S(1)}, u32[]{:S(2)}, u32[]{:S(2)}) collective-permute-start(f32[32,24,128]{2,1,0:T(8,128)S(1)} %all_to_all.28.refs_0_), channel_id=1, source_target_pairs={{0,1},{1,0},{2,3},{3,2},{4,5},{5,4},{6,7},{7,6},{8,9},{9,8},{10,11... | collective-permute-start | bytes 1179656 | tf_op jit(solution)/shard_map/ppermute | solution.py:404
  143.5 14.7 %copy-start.2 = (f32[32,24,128]{2,1,0:T(8,128)}, f32[32,24,128]{2,1,0:T(8,128)S(1)}, u32[]{:S(2)}) copy-start(f32[32,24,128]{2,1,0:T(8,128)S(1)} %collective-permute-done.12.refs_6_) | copy-start | bytes 1179652
  143.5 13.3 %collective-permute-start.13 = (f32[32,24,128]{2,1,0:T(8,128)S(1)}, f32[32,24,128]{2,1,0:T(8,128)S(1)}, u32[]{:S(2)}, u32[]{:S(2)}) collective-permute-start(f32[32,24,128]{2,1,0:T(8,128)S(1)} %collective-permute-done.12.refs_6_), channel_id=1, source_target_pairs={{0,1},{1,0},{2,3},{3,2},{4,5},{5,4},{6,7},{7,6},{8,9},{9,8},{10,11... | collective-permute-start | bytes 1179656 | tf_op jit(solution)/shard_map/ppermute | solution.py:404
  149.0 7.9 %collective-permute-start.11 = (f32[32,24,128]{2,1,0:T(8,128)S(1)}, f32[32,24,128]{2,1,0:T(8,128)S(1)}, u32[]{:S(2)}, u32[]{:S(2)}) collective-permute-start(f32[32,24,128]{2,1,0:T(8,128)S(1)} %collective-permute-done.10.refs_4_), channel_id=1, source_target_pairs={{0,1},{1,0},{2,3},{3,2},{4,5},{5,4},{6,7},{7,6},{8,9},{9,8},{10,11... | collective-permute-start | bytes 1179656 | tf_op jit(solution)/shard_map/ppermute | solution.py:404
  156.3 1.8 %collective-permute-start.9 = (f32[32,24,128]{2,1,0:T(8,128)S(1)}, f32[32,24,128]{2,1,0:T(8,128)S(1)}, u32[]{:S(2)}, u32[]{:S(2)}) collective-permute-start(f32[32,24,128]{2,1,0:T(8,128)S(1)} %collective-permute-done.8.refs_2_), channel_id=1, source_target_pairs={{0,1},{1,0},{2,3},{3,2},{4,5},{5,4},{6,7},{7,6},{8,9},{9,8},{10,11... | collective-permute-start | bytes 1179656 | tf_op jit(solution)/shard_map/ppermute | solution.py:404
  156.8 1.4 copy-start.3
  156.8 0.8 copy-start.4
  158.2 0.8 copy-start.1

commit v7 on v6

--- a/solution.py
+++ b/solution.py
@@ -42,24 +42,29 @@
     return lax.rem(lax.axis_index("x") + 4 - shift, 4), lax.rem(lax.axis_index("c") + other, 2)
 
 
-def payload_kernel(local_blocks, order, proj_ref, phase_ref, out_ref):
-    part = 128
-    width = proj_ref.shape[2]
+def payload_kernel(local_blocks, order, proj_hbm, phase_ref, out_ref, slice_ref, sems):
+    part = slice_ref.shape[1]
+    width = slice_ref.shape[2]
     share = out_ref.shape[0] // STEPS
     at = pl.multiple_of((lax.axis_index("x") * 2 + lax.axis_index("c")) * part, part)
-    for s in range(STEPS):
-        slot = lax.rem(order[s], local_blocks)
-        mine = proj_ref[pl.ds(slot, 1), pl.ds(at, part), :]
-        out_ref[s * share : (s + 1) * share, :, :width] = mine.reshape(share, part // share, width)
+    slots = [lax.rem(order[s], local_blocks) for s in range(STEPS)]
+    loads = [
+        pltpu.make_async_copy(proj_hbm.at[slots[s], pl.ds(at, part), :], slice_ref.at[s], sems.at[s])
+        for s in range(STEPS)
+    ]
+    for load in loads:
+        load.start()
     bands = []
     for s in range(STEPS):
-        slot = lax.rem(order[s], local_blocks)
         shift = phase_ref[0:1, :].astype(F32)
         for k in range(1, phase_ref.shape[0]):
-            shift = jnp.where(slot == k, phase_ref[k : k + 1, :].astype(F32), shift)
+            shift = jnp.where(slots[s] == k, phase_ref[k : k + 1, :].astype(F32), shift)
         bands += [shift[:, q * 128 : (q + 1) * 128] for q in range(width // 128)]
     band = jnp.concatenate(bands, axis=0).astype(BF)
     out_ref[:, :, width:] = jnp.broadcast_to(band[None], (out_ref.shape[0],) + band.shape)
+    for s in range(STEPS):
+        loads[s].wait()
+        out_ref[s * share : (s + 1) * share, :, :width] = slice_ref[s].reshape(share, part // share, width)
 
 
 def payload(order, projections, phases, nrows):
@@ -67,9 +72,10 @@
     whole = pl.BlockSpec(memory_space=pltpu.VMEM)
     return pl.pallas_call(
         functools.partial(payload_kernel, local_blocks),
-        in_specs=[pl.BlockSpec(memory_space=pltpu.SMEM), whole, whole],
+        in_specs=[pl.BlockSpec(memory_space=pltpu.SMEM), pl.BlockSpec(memory_space=pl.ANY), whole],
         out_specs=whole,
         out_shape=jax.ShapeDtypeStruct((nrows, 8, width + 128), BF),
+        scratch_shapes=[pltpu.VMEM((STEPS, 128, width), BF), pltpu.SemaphoreType.DMA((STEPS,))],
         name="payload",
     )(order, projections, phases)
 
@@ -290,16 +296,16 @@
 
 def solve_kernel(ridge, *refs):
     pieces = refs[:8]
-    cross_ref, old_ref, f_hbm, r_hbm, coef_ref, out_ref, upper, lower, f_ref, r_ref, x_ref, res_ref, p_ref, ap_ref, v_ref, parts_ref, delta_ref, sems = refs[8:]
-    loads = [
-        pltpu.make_async_copy(f_hbm, f_ref, sems.at[0]),
-        pltpu.make_async_copy(r_hbm, r_ref, sems.at[1]),
-    ]
+    cross_hbm, old_hbm, f_hbm, r_hbm, coef_ref, out_ref, pieces_ref, cross_ref, old_ref, upper, lower, f_ref, r_ref, x_ref, res_ref, p_ref, ap_ref, v_ref, parts_ref, delta_ref, sems = refs[8:]
+    loads = [pltpu.make_async_copy(pieces[i], pieces_ref.at[i], sems.at[i]) for i in range(8)]
+    rest = ((cross_hbm, cross_ref), (old_hbm, old_ref), (f_hbm, f_ref), (r_hbm, r_ref))
+    loads += [pltpu.make_async_copy(there, here, sems.at[8 + i]) for i, (there, here) in enumerate(rest)]
     for load in loads:
         load.start()
     for shift in range(4):
         for other in range(2):
-            ref = pieces[shift * 2 + other]
+            loads[shift * 2 + other].wait()
+            ref = pieces_ref.at[shift * 2 + other]
             px, pc = offsets(shift, other)
             row = pl.multiple_of(px * 128, 128)
             for group in range(3):
@@ -312,6 +318,8 @@
     n = upper.shape[1]
     per = 32 // STEPS
     work = (x_ref, res_ref, p_ref, ap_ref, v_ref, parts_ref)
+    for load in loads[8:10]:
+        load.wait()
     res_ref[...] = cross_ref[:per].reshape(n, 128) - ridge * old_ref[0]
     conjugate_gradients(upper.at[0], lower.at[0], *work, ridge)
     first = x_ref[...]
@@ -328,7 +336,7 @@
     delta_ref[n:, 128:] = low
     delta = delta_ref[...]
     tile = 256
-    for load in loads:
+    for load in loads[10:]:
         load.wait()
     for row in range(0, f_ref.shape[0], tile):
         both = jnp.dot(f_ref[row : row + tile, :], delta, preferred_element_type=F32)
@@ -341,14 +349,16 @@
 
     return pl.pallas_call(
         functools.partial(solve_kernel, ridge),
-        in_specs=[full(piece) for piece in pieces]
-        + [full(cross), full(old), pl.BlockSpec(memory_space=pl.ANY), pl.BlockSpec(memory_space=pl.ANY)],
+        in_specs=[pl.BlockSpec(memory_space=pl.ANY)] * 12,
         out_specs=[full(old), full(residuals)],
         out_shape=[
             jax.ShapeDtypeStruct(old.shape, F32),
             jax.ShapeDtypeStruct(residuals.shape, F32),
         ],
         scratch_shapes=[
+            pltpu.VMEM((8, 32, 24, 128), F32),
+            pltpu.VMEM(cross.shape, F32),
+            pltpu.VMEM(old.shape, F32),
             pltpu.VMEM((3, 512, 512), BF),
             pltpu.VMEM((3, 512, 512), BF),
             pltpu.VMEM(feats.shape, BF),
@@ -360,7 +370,7 @@
             pltpu.VMEM((512, 128), F32),
             pltpu.VMEM((512, 256), BF),
             pltpu.VMEM((1024, 256), BF),
-            pltpu.SemaphoreType.DMA((2,)),
+            pltpu.SemaphoreType.DMA((12,)),
         ],
         compiler_params=pltpu.CompilerParams(vmem_limit_bytes=52 << 20),
         name="solve",

time: 184 us -> 184 us (level)
  no operation moved by 1% of the time
where the time goes in v7:
time: 184 us; the launch traced here: 183 us
  blocking collectives  88.3 us (48%)
  Pallas kernels  44.4 us (24%)
  starting transfers between devices  34.9 us (19%)
  waiting for transfers between devices  12.6 us (7%)
  local copies, waits for them, and re-layouts  2.3 us (1%)
    all_to_all x4, blocking collectives, exchange(): return lax.all_to_all(values, axes, split_axis=0, concat_axis=0, tiled=True)  88.3 us
    ppermute x8, starting transfers between devices, spread(): lax.ppermute(value, 'c', [(i, (i + 1) % nc) for i in range(nc)])  24.2 us
    pallas_call x1, Pallas kernels, solve(): pl.pallas_call(functools.partial(solve_kernel, ridge), in_specs=[pl.Block...  24.1 us
    pallas_call x1, Pallas kernels, features(): pl.pallas_call(feature_kernel, grid=(total // tile,), in_specs=[whole] *...  14 us
    ppermute x6, waiting for transfers between devices, spread(): lax.ppermute(values, 'x', [(i, (i + shift) % nx) for i in range(nx)])  10.9 us
    all_to_all x1, starting transfers between devices, exchange(): return lax.all_to_all(values, axes, split_axis=0, concat_axis=0, tiled=True)  5.55 us
    ppermute x6, starting transfers between devices, spread(): lax.ppermute(values, 'x', [(i, (i + shift) % nx) for i in range(nx)])  5.15 us
  transfers between devices with their start and end apart: 15, of which 6 were waited for; matrix products, arithmetic and copies ran while one was open for 0% of the time, Pallas kernels for 0%

profile of v7, /device:TPU:1, one launch (start us, length us, event | category | flops | bytes accessed | tf_op | source)
XLA Modules:
  0.0 183.3 jit_solution(6238449028977649655)
XLA Ops:
  0.6 2.4 %payload.1 = bf16[32,8,640]{2,1,0:T(8,128)(2,1)} custom-call(s32[2]{0:T(128)} %order.3, bf16[2,1024,512]{2,1,0:T(8,128)(2,1)} %proj_hbm.1, bf16[2,512]{1,0:T(2,128)(2,1)} %phase_ref.1), custom_call_target="tpu_custom_call" | custom-call | tf_op jit(solution)/shard_map/payload/pallas_call | solution.py:73
  3.1 24.8 %all_to_all.25.got_ref = bf16[32,8,640]{2,1,0:T(8,128)(2,1)} all-to-all(bf16[32,8,640]{2,1,0:T(8,128)(2,1)} %payload.1), channel_id=1, replica_groups=mesh['z'=8,'y'=4,'x'=4,'c'=2] {'z','y'}, dimensions={0} | all-to-all | bytes 655360 | tf_op jit(solution)/shard_map/all_to_all | solution.py:404
  27.9 1.7 pick.1
  29.6 15.3 %all_to_all.26.refs_0_ = bf16[32,8,512]{2,1,0:T(8,128)(2,1)S(1)} all-to-all(bf16[32,8,512]{2,1,0:T(8,128)(2,1)} %get-tuple-element.12), channel_id=1, replica_groups=mesh['z'=8,'y'=4,'x'=4,'c'=2] {'z','y'}, dimensions={0} | all-to-all | bytes 524288 | tf_op jit(solution)/shard_map/all_to_all | solution.py:404
  44.9 2.5 %collective-permute-start.5 = (bf16[32,8,512]{2,1,0:T(8,128)(2,1)S(1)}, bf16[32,8,512]{2,1,0:T(8,128)(2,1)S(1)}, u32[]{:S(2)}, u32[]{:S(2)}) collective-permute-start(bf16[32,8,512]{2,1,0:T(8,128)(2,1)S(1)} %all_to_all.26.refs_0_), channel_id=1, source_target_pairs={{0,6},{2,0},{4,2},{6,4},{1,7},{3,1},{5,3},{7,5},{8,14},{10,8},{12,... | collective-permute-start | bytes 786440 | tf_op jit(solution)/shard_map/ppermute | solution.py:411
  47.4 0.5 collective-permute-start.3
  47.9 0.6 collective-permute-start.1
  48.5 4.3 %collective-permute-start = (bf16[32,8,512]{2,1,0:T(8,128)(2,1)S(1)}, bf16[32,8,512]{2,1,0:T(8,128)(2,1)S(1)}, u32[]{:S(2)}, u32[]{:S(2)}) collective-permute-start(bf16[32,8,512]{2,1,0:T(8,128)(2,1)S(1)} %all_to_all.26.refs_0_), channel_id=1, source_target_pairs={{0,1},{1,0},{2,3},{3,2},{4,5},{5,4},{6,7},{7,6},{8,9},{9,8},{10,11... | collective-permute-start | bytes 786440 | tf_op jit(solution)/shard_map/ppermute | solution.py:414
  52.8 0.9 collective-permute-done.5.refs_6_
  53.8 5.8 %collective-permute-start.6 = (bf16[32,8,512]{2,1,0:T(8,128)(2,1)S(1)}, bf16[32,8,512]{2,1,0:T(8,128)(2,1)S(1)}, u32[]{:S(2)}, u32[]{:S(2)}) collective-permute-start(bf16[32,8,512]{2,1,0:T(8,128)(2,1)S(1)} %collective-permute-done.5.refs_6_), channel_id=1, source_target_pairs={{0,1},{1,0},{2,3},{3,2},{4,5},{5,4},{6,7},{7,6},{8,9},{9,8},{10,11... | collective-permute-start | bytes 786440 | tf_op jit(solution)/shard_map/ppermute | solution.py:414
  59.6 0.0 collective-permute-done.3.refs_4_
  59.6 1.0 collective-permute-start.4
  60.6 0.6 collective-permute-done.1.refs_2_
  61.1 2.1 %collective-permute-start.2 = (bf16[32,8,512]{2,1,0:T(8,128)(2,1)S(1)}, bf16[32,8,512]{2,1,0:T(8,128)(2,1)S(1)}, u32[]{:S(2)}, u32[]{:S(2)}) collective-permute-start(bf16[32,8,512]{2,1,0:T(8,128)(2,1)S(1)} %collective-permute-done.1.refs_2_), channel_id=1, source_target_pairs={{0,1},{1,0},{2,3},{3,2},{4,5},{5,4},{6,7},{7,6},{8,9},{9,8},{10,11... | collective-permute-start | bytes 786440 | tf_op jit(solution)/shard_map/ppermute | solution.py:414
  63.2 0.0 collective-permute-done.refs_1_
  63.2 0.0 collective-permute-done.6.refs_7_
  63.2 0.0 copy-start.5
  63.2 0.0 collective-permute-done.4.refs_5_
  63.2 1.1 collective-permute-done.2.refs_3_
  64.4 0.0 copy-done.5
  64.4 0.0 copy-start
  64.4 0.7 copy-done
  65.1 14.0 %features.1 = (bf16[2048,1024]{1,0:T(8,128)(2,1)}, f32[32,56,128]{2,1,0:T(8,128)}) custom-call(bf16[32,8,512]{2,1,0:T(8,128)(2,1)S(1)} %all_to_all.26.refs_0_, bf16[32,8,512]{2,1,0:T(8,128)(2,1)S(1)} %collective-permute-done.refs_1_, bf16[32,8,512]{2,1,0:T(8,128)(2,1)S(1)} %collective-permute-done.1.refs_2_, ...), custom_call_target="tpu_custom_call" | custom-call | tf_op jit(solution)/shard_map/features/pallas_call | solution.py:186
  79.0 29.3 %all_to_all.27.got_ref = f32[32,56,128]{2,1,0:T(8,128)} all-to-all(f32[32,56,128]{2,1,0:T(8,128)} %get-tuple-element.14), channel_id=1, replica_groups=mesh['z'=8,'y'=4,'x'=4,'c'=2] {'z','y'}, dimensions={0} | all-to-all | bytes 1835008 | tf_op jit(solution)/shard_map/all_to_all | solution.py:404
  108.3 2.1 %copies.1 = (f32[32,24,128]{2,1,0:T(8,128)}, f32[32,32,128]{2,1,0:T(8,128)}) custom-call(f32[32,56,128]{2,1,0:T(8,128)} %all_to_all.27.got_ref), custom_call_target="tpu_custom_call" | custom-call | tf_op jit(solution)/shard_map/copies/pallas_call | solution.py:391
  110.5 18.8 %all_to_all.28.refs_0_ = f32[32,24,128]{2,1,0:T(8,128)S(1)} all-to-all(f32[32,24,128]{2,1,0:T(8,128)} %get-tuple-element.16), channel_id=1, replica_groups=mesh['z'=8,'y'=4,'x'=4,'c'=2] {'z','y'}, dimensions={0} | all-to-all | bytes 786432 | tf_op jit(solution)/shard_map/all_to_all | solution.py:404
  129.3 5.5 %all-to-all-start.4 = ((f32[32,32,128]{2,1,0:T(8,128)}), f32[32,32,128]{2,1,0:T(8,128)S(1)}, u32[]{:S(2)}, u32[]{:S(2)}) async-start(f32[32,32,128]{2,1,0:T(8,128)} %get-tuple-element.18), calls=%async_computation.4 | async-start | bytes 1048576 | tf_op jit(solution)/shard_map/all_to_all | solution.py:404
  134.9 0.5 collective-permute-start.12
  135.4 0.4 collective-permute-start.10
  135.8 0.6 collective-permute-start.8
  136.4 2.8 %collective-permute-start.7 = (f32[32,24,128]{2,1,0:T(8,128)S(1)}, f32[32,24,128]{2,1,0:T(8,128)S(1)}, u32[]{:S(2)}, u32[]{:S(2)}) collective-permute-start(f32[32,24,128]{2,1,0:T(8,128)S(1)} %all_to_all.28.refs_0_), channel_id=1, source_target_pairs={{0,1},{1,0},{2,3},{3,2},{4,5},{5,4},{6,7},{7,6},{8,9},{9,8},{10,11... | collective-permute-start | bytes 1179656 | tf_op jit(solution)/shard_map/ppermute | solution.py:414
  139.3 4.3 %collective-permute-done.12.refs_6_ = f32[32,24,128]{2,1,0:T(8,128)S(1)} collective-permute-done((f32[32,24,128]{2,1,0:T(8,128)S(1)}, f32[32,24,128]{2,1,0:T(8,128)S(1)}, u32[]{:S(2)}, u32[]{:S(2)}) %collective-permute-start.12) | collective-permute-done | bytes 393248 | tf_op jit(solution)/shard_map/ppermute | solution.py:411
  143.6 0.0 copy-start.2
  143.6 5.5 %collective-permute-start.13 = (f32[32,24,128]{2,1,0:T(8,128)S(1)}, f32[32,24,128]{2,1,0:T(8,128)S(1)}, u32[]{:S(2)}, u32[]{:S(2)}) collective-permute-start(f32[32,24,128]{2,1,0:T(8,128)S(1)} %collective-permute-done.12.refs_6_), channel_id=1, source_target_pairs={{0,1},{1,0},{2,3},{3,2},{4,5},{5,4},{6,7},{7,6},{8,9},{9,8},{10,11... | collective-permute-start | bytes 1179656 | tf_op jit(solution)/shard_map/ppermute | solution.py:414
  149.0 0.0 collective-permute-done.10.refs_4_
  149.0 2.2 %collective-permute-start.11 = (f32[32,24,128]{2,1,0:T(8,128)S(1)}, f32[32,24,128]{2,1,0:T(8,128)S(1)}, u32[]{:S(2)}, u32[]{:S(2)}) collective-permute-start(f32[32,24,128]{2,1,0:T(8,128)S(1)} %collective-permute-done.10.refs_4_), channel_id=1, source_target_pairs={{0,1},{1,0},{2,3},{3,2},{4,5},{5,4},{6,7},{7,6},{8,9},{9,8},{10,11... | collective-permute-start | bytes 1179656 | tf_op jit(solution)/shard_map/ppermute | solution.py:414
  151.3 5.1 %collective-permute-done.8.refs_2_ = f32[32,24,128]{2,1,0:T(8,128)S(1)} collective-permute-done((f32[32,24,128]{2,1,0:T(8,128)S(1)}, f32[32,24,128]{2,1,0:T(8,128)S(1)}, u32[]{:S(2)}, u32[]{:S(2)}) %collective-permute-start.8) | collective-permute-done | bytes 393248 | tf_op jit(solution)/shard_map/ppermute | solution.py:411
  156.4 0.5 collective-permute-start.9
  156.9 0.0 collective-permute-done.7.refs_1_
  156.9 0.0 collective-permute-done.13.refs_7_
  156.9 0.0 copy-start.3
  156.9 0.0 collective-permute-done.11.refs_5_
  156.9 0.0 copy-start.4
  156.9 0.8 copy-done.4
  157.7 0.5 collective-permute-done.9.refs_3_
  158.2 0.0 all-to-all-done.4.refs_8_
  158.2 0.0 copy-start.1
  158.2 0.0 copy-done.2
  158.2 0.0 copy-done.3
  158.2 0.8 copy-done.1
  159.0 24.1 %solve.1 = (f32[2,512,128]{2,1,0:T(8,128)}, f32[2048,128]{1,0:T(8,128)}) custom-call(f32[32,24,128]{2,1,0:T(8,128)S(1)} %all_to_all.28.refs_0_, f32[32,24,128]{2,1,0:T(8,128)S(1)} %collective-permute-done.7.refs_1_, f32[32,24,128]{2,1,0:T(8,128)S(1)} %collective-permute-done.8.refs_2_, f32[32,24,128]{2,1,0:T(8,128)S(1)} %collective-permute-done.9.refs_3_, ...), custom_call_target="tpu_custom_call" | custom-call | tf_op jit(solution)/shard_map/solve/pallas_call | solution.py:350
Async XLA Ops:
  44.9 8.9 %collective-permute-start.5 = (bf16[32,8,512]{2,1,0:T(8,128)(2,1)S(1)}, bf16[32,8,512]{2,1,0:T(8,128)(2,1)S(1)}, u32[]{:S(2)}, u32[]{:S(2)}) collective-permute-start(bf16[32,8,512]{2,1,0:T(8,128)(2,1)S(1)} %all_to_all.26.refs_0_), channel_id=1, source_target_pairs={{0,6},{2,0},{4,2},{6,4},{1,7},{3,1},{5,3},{7,5},{8,14},{10,8},{12,... | collective-permute-start | bytes 786440 | tf_op jit(solution)/shard_map/ppermute | solution.py:411
  47.4 12.2 %collective-permute-start.3 = (bf16[32,8,512]{2,1,0:T(8,128)(2,1)S(1)}, bf16[32,8,512]{2,1,0:T(8,128)(2,1)S(1)}, u32[]{:S(2)}, u32[]{:S(2)}) collective-permute-start(bf16[32,8,512]{2,1,0:T(8,128)(2,1)S(1)} %all_to_all.26.refs_0_), channel_id=1, source_target_pairs={{0,4},{2,6},{4,0},{6,2},{1,5},{3,7},{5,1},{7,3},{8,12},{10,14},{12... | collective-permute-start | bytes 786440 | tf_op jit(solution)/shard_map/ppermute | solution.py:411
  47.9 13.2 %collective-permute-start.1 = (bf16[32,8,512]{2,1,0:T(8,128)(2,1)S(1)}, bf16[32,8,512]{2,1,0:T(8,128)(2,1)S(1)}, u32[]{:S(2)}, u32[]{:S(2)}) collective-permute-start(bf16[32,8,512]{2,1,0:T(8,128)(2,1)S(1)} %all_to_all.26.refs_0_), channel_id=1, source_target_pairs={{0,2},{2,4},{4,6},{6,0},{1,3},{3,5},{5,7},{7,1},{8,10},{10,12},{12... | collective-permute-start | bytes 786440 | tf_op jit(solution)/shard_map/ppermute | solution.py:411
  48.5 14.7 %collective-permute-start = (bf16[32,8,512]{2,1,0:T(8,128)(2,1)S(1)}, bf16[32,8,512]{2,1,0:T(8,128)(2,1)S(1)}, u32[]{:S(2)}, u32[]{:S(2)}) collective-permute-start(bf16[32,8,512]{2,1,0:T(8,128)(2,1)S(1)} %all_to_all.26.refs_0_), channel_id=1, source_target_pairs={{0,1},{1,0},{2,3},{3,2},{4,5},{5,4},{6,7},{7,6},{8,9},{9,8},{10,11... | collective-permute-start | bytes 786440 | tf_op jit(solution)/shard_map/ppermute | solution.py:414
  53.8 9.5 %collective-permute-start.6 = (bf16[32,8,512]{2,1,0:T(8,128)(2,1)S(1)}, bf16[32,8,512]{2,1,0:T(8,128)(2,1)S(1)}, u32[]{:S(2)}, u32[]{:S(2)}) collective-permute-start(bf16[32,8,512]{2,1,0:T(8,128)(2,1)S(1)} %collective-permute-done.5.refs_6_), channel_id=1, source_target_pairs={{0,1},{1,0},{2,3},{3,2},{4,5},{5,4},{6,7},{7,6},{8,9},{9,8},{10,11... | collective-permute-start | bytes 786440 | tf_op jit(solution)/shard_map/ppermute | solution.py:414
  59.6 3.7 %collective-permute-start.4 = (bf16[32,8,512]{2,1,0:T(8,128)(2,1)S(1)}, bf16[32,8,512]{2,1,0:T(8,128)(2,1)S(1)}, u32[]{:S(2)}, u32[]{:S(2)}) collective-permute-start(bf16[32,8,512]{2,1,0:T(8,128)(2,1)S(1)} %collective-permute-done.3.refs_4_), channel_id=1, source_target_pairs={{0,1},{1,0},{2,3},{3,2},{4,5},{5,4},{6,7},{7,6},{8,9},{9,8},{10,11... | collective-permute-start | bytes 786440 | tf_op jit(solution)/shard_map/ppermute | solution.py:414
  61.1 3.2 %collective-permute-start.2 = (bf16[32,8,512]{2,1,0:T(8,128)(2,1)S(1)}, bf16[32,8,512]{2,1,0:T(8,128)(2,1)S(1)}, u32[]{:S(2)}, u32[]{:S(2)}) collective-permute-start(bf16[32,8,512]{2,1,0:T(8,128)(2,1)S(1)} %collective-permute-done.1.refs_2_), channel_id=1, source_target_pairs={{0,1},{1,0},{2,3},{3,2},{4,5},{5,4},{6,7},{7,6},{8,9},{9,8},{10,11... | collective-permute-start | bytes 786440 | tf_op jit(solution)/shard_map/ppermute | solution.py:414
  63.2 1.2 copy-start.5
  64.4 0.7 copy-start
  129.3 28.9 %all-to-all-start.4 = ((f32[32,32,128]{2,1,0:T(8,128)}), f32[32,32,128]{2,1,0:T(8,128)S(1)}, u32[]{:S(2)}, u32[]{:S(2)}) async-start(f32[32,32,128]{2,1,0:T(8,128)} %get-tuple-element.18), calls=%async_computation.4 | async-start | bytes 1048576 | tf_op jit(solution)/shard_map/all_to_all | solution.py:404
  134.9 8.7 %collective-permute-start.12 = (f32[32,24,128]{2,1,0:T(8,128)S(1)}, f32[32,24,128]{2,1,0:T(8,128)S(1)}, u32[]{:S(2)}, u32[]{:S(2)}) collective-permute-start(f32[32,24,128]{2,1,0:T(8,128)S(1)} %all_to_all.28.refs_0_), channel_id=1, source_target_pairs={{0,6},{2,0},{4,2},{6,4},{1,7},{3,1},{5,3},{7,5},{8,14},{10,8},{12,... | collective-permute-start | bytes 1179656 | tf_op jit(solution)/shard_map/ppermute | solution.py:411
  135.4 13.6 %collective-permute-start.10 = (f32[32,24,128]{2,1,0:T(8,128)S(1)}, f32[32,24,128]{2,1,0:T(8,128)S(1)}, u32[]{:S(2)}, u32[]{:S(2)}) collective-permute-start(f32[32,24,128]{2,1,0:T(8,128)S(1)} %all_to_all.28.refs_0_), channel_id=1, source_target_pairs={{0,4},{2,6},{4,0},{6,2},{1,5},{3,7},{5,1},{7,3},{8,12},{10,14},{12... | collective-permute-start | bytes 1179656 | tf_op jit(solution)/shard_map/ppermute | solution.py:411
  135.8 20.6 %collective-permute-start.8 = (f32[32,24,128]{2,1,0:T(8,128)S(1)}, f32[32,24,128]{2,1,0:T(8,128)S(1)}, u32[]{:S(2)}, u32[]{:S(2)}) collective-permute-start(f32[32,24,128]{2,1,0:T(8,128)S(1)} %all_to_all.28.refs_0_), channel_id=1, source_target_pairs={{0,2},{2,4},{4,6},{6,0},{1,3},{3,5},{5,7},{7,1},{8,10},{10,12},{12... | collective-permute-start | bytes 1179656 | tf_op jit(solution)/shard_map/ppermute | solution.py:411
  136.4 20.4 %collective-permute-start.7 = (f32[32,24,128]{2,1,0:T(8,128)S(1)}, f32[32,24,128]{2,1,0:T(8,128)S(1)}, u32[]{:S(2)}, u32[]{:S(2)}) collective-permute-start(f32[32,24,128]{2,1,0:T(8,128)S(1)} %all_to_all.28.refs_0_), channel_id=1, source_target_pairs={{0,1},{1,0},{2,3},{3,2},{4,5},{5,4},{6,7},{7,6},{8,9},{9,8},{10,11... | collective-permute-start | bytes 1179656 | tf_op jit(solution)/shard_map/ppermute | solution.py:414
  143.6 14.7 %copy-start.2 = (f32[32,24,128]{2,1,0:T(8,128)}, f32[32,24,128]{2,1,0:T(8,128)S(1)}, u32[]{:S(2)}) copy-start(f32[32,24,128]{2,1,0:T(8,128)S(1)} %collective-permute-done.12.refs_6_) | copy-start | bytes 1179652
  143.6 13.3 %collective-permute-start.13 = (f32[32,24,128]{2,1,0:T(8,128)S(1)}, f32[32,24,128]{2,1,0:T(8,128)S(1)}, u32[]{:S(2)}, u32[]{:S(2)}) collective-permute-start(f32[32,24,128]{2,1,0:T(8,128)S(1)} %collective-permute-done.12.refs_6_), channel_id=1, source_target_pairs={{0,1},{1,0},{2,3},{3,2},{4,5},{5,4},{6,7},{7,6},{8,9},{9,8},{10,11... | collective-permute-start | bytes 1179656 | tf_op jit(solution)/shard_map/ppermute | solution.py:414
  149.0 7.9 %collective-permute-start.11 = (f32[32,24,128]{2,1,0:T(8,128)S(1)}, f32[32,24,128]{2,1,0:T(8,128)S(1)}, u32[]{:S(2)}, u32[]{:S(2)}) collective-permute-start(f32[32,24,128]{2,1,0:T(8,128)S(1)} %collective-permute-done.10.refs_4_), channel_id=1, source_target_pairs={{0,1},{1,0},{2,3},{3,2},{4,5},{5,4},{6,7},{7,6},{8,9},{9,8},{10,11... | collective-permute-start | bytes 1179656 | tf_op jit(solution)/shard_map/ppermute | solution.py:414
  156.4 1.8 %collective-permute-start.9 = (f32[32,24,128]{2,1,0:T(8,128)S(1)}, f32[32,24,128]{2,1,0:T(8,128)S(1)}, u32[]{:S(2)}, u32[]{:S(2)}) collective-permute-start(f32[32,24,128]{2,1,0:T(8,128)S(1)} %collective-permute-done.8.refs_2_), channel_id=1, source_target_pairs={{0,1},{1,0},{2,3},{3,2},{4,5},{5,4},{6,7},{7,6},{8,9},{9,8},{10,11... | collective-permute-start | bytes 1179656 | tf_op jit(solution)/shard_map/ppermute | solution.py:414
  156.9 1.4 copy-start.3
  156.9 0.8 copy-start.4
  158.2 0.8 copy-start.1

commit v8 on v7

--- a/solution.py
+++ b/solution.py
@@ -189,7 +189,7 @@
         in_specs=[whole] * 8
         + [
             pl.BlockSpec((tile, depth), lambda i: (i, 0)),
-            whole,
+            pl.BlockSpec((STEPS, width), lambda i: (0, 0)),
             pl.BlockSpec((tile, 128), lambda i: (i, 0)),
         ],
         out_specs=[pl.BlockSpec((tile, STEPS * width), lambda i: (i, 0)), whole],
@@ -202,7 +202,7 @@
             pltpu.VMEM((512, total), BF),
             pltpu.VMEM((total, STEPS * width), BF),
         ],
-        compiler_params=pltpu.CompilerParams(vmem_limit_bytes=52 << 20),
+        compiler_params=pltpu.CompilerParams(vmem_limit_bytes=48 << 20),
         name="features",
     )(*pieces, embeddings, shifts, residuals)
 
@@ -296,9 +296,9 @@
 
 def solve_kernel(ridge, *refs):
     pieces = refs[:8]
-    cross_hbm, old_hbm, f_hbm, r_hbm, coef_ref, out_ref, pieces_ref, cross_ref, old_ref, upper, lower, f_ref, r_ref, x_ref, res_ref, p_ref, ap_ref, v_ref, parts_ref, delta_ref, sems = refs[8:]
+    cross_ref, old_hbm, f_hbm, r_hbm, coef_ref, out_ref, pieces_ref, old_ref, upper, lower, f_ref, r_ref, x_ref, res_ref, p_ref, ap_ref, v_ref, parts_ref, delta_ref, sems = refs[8:]
     loads = [pltpu.make_async_copy(pieces[i], pieces_ref.at[i], sems.at[i]) for i in range(8)]
-    rest = ((cross_hbm, cross_ref), (old_hbm, old_ref), (f_hbm, f_ref), (r_hbm, r_ref))
+    rest = ((old_hbm, old_ref), (f_hbm, f_ref), (r_hbm, r_ref))
     loads += [pltpu.make_async_copy(there, here, sems.at[8 + i]) for i, (there, here) in enumerate(rest)]
     for load in loads:
         load.start()
@@ -318,8 +318,7 @@
     n = upper.shape[1]
     per = 32 // STEPS
     work = (x_ref, res_ref, p_ref, ap_ref, v_ref, parts_ref)
-    for load in loads[8:10]:
-        load.wait()
+    loads[8].wait()
     res_ref[...] = cross_ref[:per].reshape(n, 128) - ridge * old_ref[0]
     conjugate_gradients(upper.at[0], lower.at[0], *work, ridge)
     first = x_ref[...]
@@ -336,7 +335,7 @@
     delta_ref[n:, 128:] = low
     delta = delta_ref[...]
     tile = 256
-    for load in loads[10:]:
+    for load in loads[9:]:
         load.wait()
     for row in range(0, f_ref.shape[0], tile):
         both = jnp.dot(f_ref[row : row + tile, :], delta, preferred_element_type=F32)
@@ -349,7 +348,9 @@
 
     return pl.pallas_call(
         functools.partial(solve_kernel, ridge),
-        in_specs=[pl.BlockSpec(memory_space=pl.ANY)] * 12,
+        in_specs=[pl.BlockSpec(memory_space=pl.ANY)] * 8
+        + [pl.BlockSpec(memory_space=pltpu.VMEM)]
+        + [pl.BlockSpec(memory_space=pl.ANY)] * 3,
         out_specs=[full(old), full(residuals)],
         out_shape=[
             jax.ShapeDtypeStruct(old.shape, F32),
@@ -357,7 +358,6 @@
         ],
         scratch_shapes=[
             pltpu.VMEM((8, 32, 24, 128), F32),
-            pltpu.VMEM(cross.shape, F32),
             pltpu.VMEM(old.shape, F32),
             pltpu.VMEM((3, 512, 512), BF),
             pltpu.VMEM((3, 512, 512), BF),
@@ -370,9 +370,9 @@
             pltpu.VMEM((512, 128), F32),
             pltpu.VMEM((512, 256), BF),
             pltpu.VMEM((1024, 256), BF),
-            pltpu.SemaphoreType.DMA((12,)),
-        ],
-        compiler_params=pltpu.CompilerParams(vmem_limit_bytes=52 << 20),
+            pltpu.SemaphoreType.DMA((11,)),
+        ],
+        compiler_params=pltpu.CompilerParams(vmem_limit_bytes=51 << 20),
         name="solve",
     )(*pieces, cross, old, feats, residuals)
 

time: 184 us -> 184 us (level)
  no operation moved by 1% of the time
where the time goes in v8:
time: 184 us
  blocking collectives  88.1 us (48%)
  Pallas kernels  45.1 us (25%)
  starting transfers between devices  35 us (19%)
  waiting for transfers between devices  12.7 us (7%)
  local copies, waits for them, and re-layouts  2.24 us (1%)
    all_to_all x4, blocking collectives, exchange(): return lax.all_to_all(values, axes, split_axis=0, concat_axis=0, tiled=True)  88.1 us
    pallas_call x1, Pallas kernels, solve(): pl.pallas_call(functools.partial(solve_kernel, ridge), in_specs=[pl.Block...  25.2 us
    ppermute x8, starting transfers between devices, spread(): lax.ppermute(value, 'c', [(i, (i + 1) % nc) for i in range(nc)])  24.3 us
    pallas_call x1, Pallas kernels, features(): pl.pallas_call(feature_kernel, grid=(total // tile,), in_specs=[whole] *...  13.5 us
    ppermute x6, waiting for transfers between devices, spread(): lax.ppermute(values, 'x', [(i, (i + shift) % nx) for i in range(nx)])  10.9 us
    all_to_all x1, starting transfers between devices, exchange(): return lax.all_to_all(values, axes, split_axis=0, concat_axis=0, tiled=True)  5.55 us
    ppermute x6, starting transfers between devices, spread(): lax.ppermute(values, 'x', [(i, (i + shift) % nx) for i in range(nx)])  5.15 us
  transfers between devices with their start and end apart: 15, of which 6 were waited for; matrix products, arithmetic and copies ran while one was open for 0% of the time, Pallas kernels for 0%

profile of v8, /device:TPU:1, one launch (start us, length us, event | category | flops | bytes accessed | tf_op | source)
XLA Modules:
  0.0 183.8 jit_solution(3351277812275955687)
XLA Ops:
  0.6 0.0 copy-start
  0.6 2.5 %payload.1 = bf16[32,8,640]{2,1,0:T(8,128)(2,1)} custom-call(s32[2]{0:T(128)} %order.3, bf16[2,1024,512]{2,1,0:T(8,128)(2,1)} %proj_hbm.1, bf16[2,512]{1,0:T(2,128)(2,1)} %phase_ref.1), custom_call_target="tpu_custom_call" | custom-call | tf_op jit(solution)/shard_map/payload/pallas_call | solution.py:73
  3.2 24.8 %all_to_all.25.got_ref = bf16[32,8,640]{2,1,0:T(8,128)(2,1)} all-to-all(bf16[32,8,640]{2,1,0:T(8,128)(2,1)} %payload.1), channel_id=1, replica_groups=mesh['z'=8,'y'=4,'x'=4,'c'=2] {'z','y'}, dimensions={0} | all-to-all | bytes 655360 | tf_op jit(solution)/shard_map/all_to_all | solution.py:404
  28.0 1.7 pick.1
  29.7 15.3 %all_to_all.26.refs_0_ = bf16[32,8,512]{2,1,0:T(8,128)(2,1)S(1)} all-to-all(bf16[32,8,512]{2,1,0:T(8,128)(2,1)} %get-tuple-element.12), channel_id=1, replica_groups=mesh['z'=8,'y'=4,'x'=4,'c'=2] {'z','y'}, dimensions={0} | all-to-all | bytes 524288 | tf_op jit(solution)/shard_map/all_to_all | solution.py:404
  45.0 2.5 %collective-permute-start.5 = (bf16[32,8,512]{2,1,0:T(8,128)(2,1)S(1)}, bf16[32,8,512]{2,1,0:T(8,128)(2,1)S(1)}, u32[]{:S(2)}, u32[]{:S(2)}) collective-permute-start(bf16[32,8,512]{2,1,0:T(8,128)(2,1)S(1)} %all_to_all.26.refs_0_), channel_id=1, source_target_pairs={{0,6},{2,0},{4,2},{6,4},{1,7},{3,1},{5,3},{7,5},{8,14},{10,8},{12,... | collective-permute-start | bytes 786440 | tf_op jit(solution)/shard_map/ppermute | solution.py:411
  47.5 0.5 collective-permute-start.3
  48.0 0.6 collective-permute-start.1
  48.6 4.3 %collective-permute-start = (bf16[32,8,512]{2,1,0:T(8,128)(2,1)S(1)}, bf16[32,8,512]{2,1,0:T(8,128)(2,1)S(1)}, u32[]{:S(2)}, u32[]{:S(2)}) collective-permute-start(bf16[32,8,512]{2,1,0:T(8,128)(2,1)S(1)} %all_to_all.26.refs_0_), channel_id=1, source_target_pairs={{0,1},{1,0},{2,3},{3,2},{4,5},{5,4},{6,7},{7,6},{8,9},{9,8},{10,11... | collective-permute-start | bytes 786440 | tf_op jit(solution)/shard_map/ppermute | solution.py:414
  53.0 0.9 collective-permute-done.5.refs_6_
  53.9 5.8 %collective-permute-start.6 = (bf16[32,8,512]{2,1,0:T(8,128)(2,1)S(1)}, bf16[32,8,512]{2,1,0:T(8,128)(2,1)S(1)}, u32[]{:S(2)}, u32[]{:S(2)}) collective-permute-start(bf16[32,8,512]{2,1,0:T(8,128)(2,1)S(1)} %collective-permute-done.5.refs_6_), channel_id=1, source_target_pairs={{0,1},{1,0},{2,3},{3,2},{4,5},{5,4},{6,7},{7,6},{8,9},{9,8},{10,11... | collective-permute-start | bytes 786440 | tf_op jit(solution)/shard_map/ppermute | solution.py:414
  59.7 0.0 collective-permute-done.3.refs_4_
  59.7 1.0 collective-permute-start.4
  60.7 0.6 collective-permute-done.1.refs_2_
  61.3 2.1 %collective-permute-start.2 = (bf16[32,8,512]{2,1,0:T(8,128)(2,1)S(1)}, bf16[32,8,512]{2,1,0:T(8,128)(2,1)S(1)}, u32[]{:S(2)}, u32[]{:S(2)}) collective-permute-start(bf16[32,8,512]{2,1,0:T(8,128)(2,1)S(1)} %collective-permute-done.1.refs_2_), channel_id=1, source_target_pairs={{0,1},{1,0},{2,3},{3,2},{4,5},{5,4},{6,7},{7,6},{8,9},{9,8},{10,11... | collective-permute-start | bytes 786440 | tf_op jit(solution)/shard_map/ppermute | solution.py:414
  63.3 0.0 collective-permute-done.refs_1_
  63.3 0.0 collective-permute-done.6.refs_7_
  63.4 0.0 collective-permute-done.4.refs_5_
  63.4 1.1 collective-permute-done.2.refs_3_
  64.5 0.0 copy-done
  64.5 0.0 copy-start.1
  64.5 0.7 copy-done.1
  65.2 13.5 %features.1 = (bf16[2048,1024]{1,0:T(8,128)(2,1)}, f32[32,56,128]{2,1,0:T(8,128)S(1)}) custom-call(bf16[32,8,512]{2,1,0:T(8,128)(2,1)S(1)} %all_to_all.26.refs_0_, bf16[32,8,512]{2,1,0:T(8,128)(2,1)S(1)} %collective-permute-done.refs_1_, bf16[32,8,512]{2,1,0:T(8,128)(2,1)S(1)} %collective-permute-done.1.refs_2_, ...), custom_call_target="tpu_custom_call" | custom-call | tf_op jit(solution)/shard_map/features/pallas_call | solution.py:186
  78.7 29.1 %all_to_all.27.got_ref = f32[32,56,128]{2,1,0:T(8,128)} all-to-all(f32[32,56,128]{2,1,0:T(8,128)S(1)} %get-tuple-element.14), channel_id=1, replica_groups=mesh['z'=8,'y'=4,'x'=4,'c'=2] {'z','y'}, dimensions={0} | all-to-all | bytes 1835008 | tf_op jit(solution)/shard_map/all_to_all | solution.py:404
  107.8 2.1 %copies.1 = (f32[32,24,128]{2,1,0:T(8,128)}, f32[32,32,128]{2,1,0:T(8,128)}) custom-call(f32[32,56,128]{2,1,0:T(8,128)} %all_to_all.27.got_ref), custom_call_target="tpu_custom_call" | custom-call | tf_op jit(solution)/shard_map/copies/pallas_call | solution.py:391
  109.9 18.9 %all_to_all.28.refs_0_ = f32[32,24,128]{2,1,0:T(8,128)S(1)} all-to-all(f32[32,24,128]{2,1,0:T(8,128)} %get-tuple-element.16), channel_id=1, replica_groups=mesh['z'=8,'y'=4,'x'=4,'c'=2] {'z','y'}, dimensions={0} | all-to-all | bytes 786432 | tf_op jit(solution)/shard_map/all_to_all | solution.py:404
  128.8 5.6 %all-to-all-start.4 = ((f32[32,32,128]{2,1,0:T(8,128)}), f32[32,32,128]{2,1,0:T(8,128)S(1)}, u32[]{:S(2)}, u32[]{:S(2)}) async-start(f32[32,32,128]{2,1,0:T(8,128)} %get-tuple-element.18), calls=%async_computation.4 | async-start | bytes 1048576 | tf_op jit(solution)/shard_map/all_to_all | solution.py:404
  134.3 0.5 collective-permute-start.12
  134.9 0.4 collective-permute-start.10
  135.3 0.6 collective-permute-start.8
  135.9 2.8 %collective-permute-start.7 = (f32[32,24,128]{2,1,0:T(8,128)S(1)}, f32[32,24,128]{2,1,0:T(8,128)S(1)}, u32[]{:S(2)}, u32[]{:S(2)}) collective-permute-start(f32[32,24,128]{2,1,0:T(8,128)S(1)} %all_to_all.28.refs_0_), channel_id=1, source_target_pairs={{0,1},{1,0},{2,3},{3,2},{4,5},{5,4},{6,7},{7,6},{8,9},{9,8},{10,11... | collective-permute-start | bytes 1179656 | tf_op jit(solution)/shard_map/ppermute | solution.py:414
  138.7 4.3 %collective-permute-done.12.refs_6_ = f32[32,24,128]{2,1,0:T(8,128)S(1)} collective-permute-done((f32[32,24,128]{2,1,0:T(8,128)S(1)}, f32[32,24,128]{2,1,0:T(8,128)S(1)}, u32[]{:S(2)}, u32[]{:S(2)}) %collective-permute-start.12) | collective-permute-done | bytes 393248 | tf_op jit(solution)/shard_map/ppermute | solution.py:411
  143.0 5.5 %collective-permute-start.13 = (f32[32,24,128]{2,1,0:T(8,128)S(1)}, f32[32,24,128]{2,1,0:T(8,128)S(1)}, u32[]{:S(2)}, u32[]{:S(2)}) collective-permute-start(f32[32,24,128]{2,1,0:T(8,128)S(1)} %collective-permute-done.12.refs_6_), channel_id=1, source_target_pairs={{0,1},{1,0},{2,3},{3,2},{4,5},{5,4},{6,7},{7,6},{8,9},{9,8},{10,11... | collective-permute-start | bytes 1179656 | tf_op jit(solution)/shard_map/ppermute | solution.py:414
  148.5 0.0 collective-permute-done.10.refs_4_
  148.5 2.2 %collective-permute-start.11 = (f32[32,24,128]{2,1,0:T(8,128)S(1)}, f32[32,24,128]{2,1,0:T(8,128)S(1)}, u32[]{:S(2)}, u32[]{:S(2)}) collective-permute-start(f32[32,24,128]{2,1,0:T(8,128)S(1)} %collective-permute-done.10.refs_4_), channel_id=1, source_target_pairs={{0,1},{1,0},{2,3},{3,2},{4,5},{5,4},{6,7},{7,6},{8,9},{9,8},{10,11... | collective-permute-start | bytes 1179656 | tf_op jit(solution)/shard_map/ppermute | solution.py:414
  150.7 5.1 %collective-permute-done.8.refs_2_ = f32[32,24,128]{2,1,0:T(8,128)S(1)} collective-permute-done((f32[32,24,128]{2,1,0:T(8,128)S(1)}, f32[32,24,128]{2,1,0:T(8,128)S(1)}, u32[]{:S(2)}, u32[]{:S(2)}) %collective-permute-start.8) | collective-permute-done | bytes 393248 | tf_op jit(solution)/shard_map/ppermute | solution.py:411
  155.9 0.5 collective-permute-start.9
  156.4 0.0 collective-permute-done.7.refs_1_
  156.4 0.0 collective-permute-done.13.refs_7_
  156.4 0.0 copy-start.3
  156.4 0.0 collective-permute-done.11.refs_5_
  156.4 0.7 copy-done.3
  157.1 0.6 collective-permute-done.9.refs_3_
  157.7 0.0 all-to-all-done.4.refs_8_
  157.7 0.0 copy-start.2
  157.7 0.8 copy-done.2
  158.5 25.2 %solve.1 = (f32[2,512,128]{2,1,0:T(8,128)}, f32[2048,128]{1,0:T(8,128)}) custom-call(f32[32,24,128]{2,1,0:T(8,128)S(1)} %all_to_all.28.refs_0_, f32[32,24,128]{2,1,0:T(8,128)S(1)} %collective-permute-done.7.refs_1_, f32[32,24,128]{2,1,0:T(8,128)S(1)} %collective-permute-done.8.refs_2_, f32[32,24,128]{2,1,0:T(8,128)S(1)} %collective-permute-done.9.refs_3_, ...), custom_call_target="tpu_custom_call" | custom-call | tf_op jit(solution)/shard_map/solve/pallas_call | solution.py:349
Async XLA Ops:
  0.6 63.9 %copy-start = (f32[2048,128]{1,0:T(8,128)S(1)}, f32[2048,128]{1,0:T(8,128)}, u32[]{:S(2)}) copy-start(f32[2048,128]{1,0:T(8,128)} %refs_11_.1) | copy-start | bytes 3145732
  45.0 8.9 %collective-permute-start.5 = (bf16[32,8,512]{2,1,0:T(8,128)(2,1)S(1)}, bf16[32,8,512]{2,1,0:T(8,128)(2,1)S(1)}, u32[]{:S(2)}, u32[]{:S(2)}) collective-permute-start(bf16[32,8,512]{2,1,0:T(8,128)(2,1)S(1)} %all_to_all.26.refs_0_), channel_id=1, source_target_pairs={{0,6},{2,0},{4,2},{6,4},{1,7},{3,1},{5,3},{7,5},{8,14},{10,8},{12,... | collective-permute-start | bytes 786440 | tf_op jit(solution)/shard_map/ppermute | solution.py:411
  47.5 12.2 %collective-permute-start.3 = (bf16[32,8,512]{2,1,0:T(8,128)(2,1)S(1)}, bf16[32,8,512]{2,1,0:T(8,128)(2,1)S(1)}, u32[]{:S(2)}, u32[]{:S(2)}) collective-permute-start(bf16[32,8,512]{2,1,0:T(8,128)(2,1)S(1)} %all_to_all.26.refs_0_), channel_id=1, source_target_pairs={{0,4},{2,6},{4,0},{6,2},{1,5},{3,7},{5,1},{7,3},{8,12},{10,14},{12... | collective-permute-start | bytes 786440 | tf_op jit(solution)/shard_map/ppermute | solution.py:411
  48.0 13.2 %collective-permute-start.1 = (bf16[32,8,512]{2,1,0:T(8,128)(2,1)S(1)}, bf16[32,8,512]{2,1,0:T(8,128)(2,1)S(1)}, u32[]{:S(2)}, u32[]{:S(2)}) collective-permute-start(bf16[32,8,512]{2,1,0:T(8,128)(2,1)S(1)} %all_to_all.26.refs_0_), channel_id=1, source_target_pairs={{0,2},{2,4},{4,6},{6,0},{1,3},{3,5},{5,7},{7,1},{8,10},{10,12},{12... | collective-permute-start | bytes 786440 | tf_op jit(solution)/shard_map/ppermute | solution.py:411
  48.6 14.7 %collective-permute-start = (bf16[32,8,512]{2,1,0:T(8,128)(2,1)S(1)}, bf16[32,8,512]{2,1,0:T(8,128)(2,1)S(1)}, u32[]{:S(2)}, u32[]{:S(2)}) collective-permute-start(bf16[32,8,512]{2,1,0:T(8,128)(2,1)S(1)} %all_to_all.26.refs_0_), channel_id=1, source_target_pairs={{0,1},{1,0},{2,3},{3,2},{4,5},{5,4},{6,7},{7,6},{8,9},{9,8},{10,11... | collective-permute-start | bytes 786440 | tf_op jit(solution)/shard_map/ppermute | solution.py:414
  53.9 9.5 %collective-permute-start.6 = (bf16[32,8,512]{2,1,0:T(8,128)(2,1)S(1)}, bf16[32,8,512]{2,1,0:T(8,128)(2,1)S(1)}, u32[]{:S(2)}, u32[]{:S(2)}) collective-permute-start(bf16[32,8,512]{2,1,0:T(8,128)(2,1)S(1)} %collective-permute-done.5.refs_6_), channel_id=1, source_target_pairs={{0,1},{1,0},{2,3},{3,2},{4,5},{5,4},{6,7},{7,6},{8,9},{9,8},{10,11... | collective-permute-start | bytes 786440 | tf_op jit(solution)/shard_map/ppermute | solution.py:414
  59.7 3.7 %collective-permute-start.4 = (bf16[32,8,512]{2,1,0:T(8,128)(2,1)S(1)}, bf16[32,8,512]{2,1,0:T(8,128)(2,1)S(1)}, u32[]{:S(2)}, u32[]{:S(2)}) collective-permute-start(bf16[32,8,512]{2,1,0:T(8,128)(2,1)S(1)} %collective-permute-done.3.refs_4_), channel_id=1, source_target_pairs={{0,1},{1,0},{2,3},{3,2},{4,5},{5,4},{6,7},{7,6},{8,9},{9,8},{10,11... | collective-permute-start | bytes 786440 | tf_op jit(solution)/shard_map/ppermute | solution.py:414
  61.3 3.2 %collective-permute-start.2 = (bf16[32,8,512]{2,1,0:T(8,128)(2,1)S(1)}, bf16[32,8,512]{2,1,0:T(8,128)(2,1)S(1)}, u32[]{:S(2)}, u32[]{:S(2)}) collective-permute-start(bf16[32,8,512]{2,1,0:T(8,128)(2,1)S(1)} %collective-permute-done.1.refs_2_), channel_id=1, source_target_pairs={{0,1},{1,0},{2,3},{3,2},{4,5},{5,4},{6,7},{7,6},{8,9},{9,8},{10,11... | collective-permute-start | bytes 786440 | tf_op jit(solution)/shard_map/ppermute | solution.py:414
  64.5 0.7 copy-start.1
  128.8 28.9 %all-to-all-start.4 = ((f32[32,32,128]{2,1,0:T(8,128)}), f32[32,32,128]{2,1,0:T(8,128)S(1)}, u32[]{:S(2)}, u32[]{:S(2)}) async-start(f32[32,32,128]{2,1,0:T(8,128)} %get-tuple-element.18), calls=%async_computation.4 | async-start | bytes 1048576 | tf_op jit(solution)/shard_map/all_to_all | solution.py:404
  134.3 8.7 %collective-permute-start.12 = (f32[32,24,128]{2,1,0:T(8,128)S(1)}, f32[32,24,128]{2,1,0:T(8,128)S(1)}, u32[]{:S(2)}, u32[]{:S(2)}) collective-permute-start(f32[32,24,128]{2,1,0:T(8,128)S(1)} %all_to_all.28.refs_0_), channel_id=1, source_target_pairs={{0,6},{2,0},{4,2},{6,4},{1,7},{3,1},{5,3},{7,5},{8,14},{10,8},{12,... | collective-permute-start | bytes 1179656 | tf_op jit(solution)/shard_map/ppermute | solution.py:411
  134.9 13.6 %collective-permute-start.10 = (f32[32,24,128]{2,1,0:T(8,128)S(1)}, f32[32,24,128]{2,1,0:T(8,128)S(1)}, u32[]{:S(2)}, u32[]{:S(2)}) collective-permute-start(f32[32,24,128]{2,1,0:T(8,128)S(1)} %all_to_all.28.refs_0_), channel_id=1, source_target_pairs={{0,4},{2,6},{4,0},{6,2},{1,5},{3,7},{5,1},{7,3},{8,12},{10,14},{12... | collective-permute-start | bytes 1179656 | tf_op jit(solution)/shard_map/ppermute | solution.py:411
  135.3 20.6 %collective-permute-start.8 = (f32[32,24,128]{2,1,0:T(8,128)S(1)}, f32[32,24,128]{2,1,0:T(8,128)S(1)}, u32[]{:S(2)}, u32[]{:S(2)}) collective-permute-start(f32[32,24,128]{2,1,0:T(8,128)S(1)} %all_to_all.28.refs_0_), channel_id=1, source_target_pairs={{0,2},{2,4},{4,6},{6,0},{1,3},{3,5},{5,7},{7,1},{8,10},{10,12},{12... | collective-permute-start | bytes 1179656 | tf_op jit(solution)/shard_map/ppermute | solution.py:411
  135.9 20.5 %collective-permute-start.7 = (f32[32,24,128]{2,1,0:T(8,128)S(1)}, f32[32,24,128]{2,1,0:T(8,128)S(1)}, u32[]{:S(2)}, u32[]{:S(2)}) collective-permute-start(f32[32,24,128]{2,1,0:T(8,128)S(1)} %all_to_all.28.refs_0_), channel_id=1, source_target_pairs={{0,1},{1,0},{2,3},{3,2},{4,5},{5,4},{6,7},{7,6},{8,9},{9,8},{10,11... | collective-permute-start | bytes 1179656 | tf_op jit(solution)/shard_map/ppermute | solution.py:414
  143.0 13.3 %collective-permute-start.13 = (f32[32,24,128]{2,1,0:T(8,128)S(1)}, f32[32,24,128]{2,1,0:T(8,128)S(1)}, u32[]{:S(2)}, u32[]{:S(2)}) collective-permute-start(f32[32,24,128]{2,1,0:T(8,128)S(1)} %collective-permute-done.12.refs_6_), channel_id=1, source_target_pairs={{0,1},{1,0},{2,3},{3,2},{4,5},{5,4},{6,7},{7,6},{8,9},{9,8},{10,11... | collective-permute-start | bytes 1179656 | tf_op jit(solution)/shard_map/ppermute | solution.py:414
  148.5 7.9 %collective-permute-start.11 = (f32[32,24,128]{2,1,0:T(8,128)S(1)}, f32[32,24,128]{2,1,0:T(8,128)S(1)}, u32[]{:S(2)}, u32[]{:S(2)}) collective-permute-start(f32[32,24,128]{2,1,0:T(8,128)S(1)} %collective-permute-done.10.refs_4_), channel_id=1, source_target_pairs={{0,1},{1,0},{2,3},{3,2},{4,5},{5,4},{6,7},{7,6},{8,9},{9,8},{10,11... | collective-permute-start | bytes 1179656 | tf_op jit(solution)/shard_map/ppermute | solution.py:414
  155.9 1.8 %collective-permute-start.9 = (f32[32,24,128]{2,1,0:T(8,128)S(1)}, f32[32,24,128]{2,1,0:T(8,128)S(1)}, u32[]{:S(2)}, u32[]{:S(2)}) collective-permute-start(f32[32,24,128]{2,1,0:T(8,128)S(1)} %collective-permute-done.8.refs_2_), channel_id=1, source_target_pairs={{0,1},{1,0},{2,3},{3,2},{4,5},{5,4},{6,7},{7,6},{8,9},{9,8},{10,11... | collective-permute-start | bytes 1179656 | tf_op jit(solution)/shard_map/ppermute | solution.py:414
  156.4 0.8 copy-start.3
  157.7 0.8 copy-start.2
